TPU v7x, 32 devices: a whole 2x2x4 slice. The times are simulated.
32 devices in a mesh: det: 4 (over y, x), tm: 8 (over z, core).
Axes of the slice: x: 2, y: 2, z: 4, core: 2. Of those that a mesh axis runs over, the one named last changes fastest.
Arguments:
- timestream: float32 [2048, 4096], P('det', 'tm'), may hold values from -18 to 18
- sample_flags: int32 [2048, 4096], P('det', 'tm'), may hold values 0 or 1
- pointing: bfloat16 [32, 4, 128, 128], P('tm'), may hold values from -0.5 to 0.5
- tile_ids: int32 [32, 4], P('tm'), may hold values from 0 to 31
- block_offsets: int32 [32, 4], P('tm'), may hold values from 0 to 127
- tile_owner: int32 [32], replicated, may hold values from 0 to 31, each once
- det_gains: float32 [2048], P('det'), may hold values from 0.5 to 2
- mode_vectors: float32 [2048, 32], P('det'), may hold values from -0.125 to 0.125
- filter_gain: float32 [257], replicated, may hold values from 0.05 to 1
Outputs:
- tile_snr: float32 [32, 128, 128], P(('det', 'tm'))
- cleaned: bfloat16 [2048, 4096], P('det', 'tm')
Inputs may be any that keep to these rules, and one draw needn't show every extreme that they name: Tile t is held in slot tile_owner[t]; slot q belongs to device q of det+tm in mesh order (one tile per device).
All inputs are finite; a program needn't handle non-finite values. No bound on the sum of `sample_flags` on one device may be relied on, other than what follows from the above.
Results may differ from a plain program's by a relative error of at most 0.0085.
Values may be sent and summed in bfloat16 or wider, within the bound.
No kernel may reach another device: no remote copies, remote signals or barrier semaphores. Data moves between devices by JAX's collectives and lax.ppermute only.
A program may use at most 64 MiB of HBM per device.

v0:
```python
import math

import jax
import jax.numpy as jnp
from jax import lax
from jax.sharding import PartitionSpec as P

FLEN = 512
SEGLEN = 128
TILE = 128
BLOCKS_TILE = 128
TILES_DEV = 1


def spectral_tables():
    position = lax.iota(jnp.int32, FLEN)
    phase_index = position[:, None] * position[None, :] % FLEN
    angles = phase_index.astype(jnp.float32) * (2.0 * math.pi / FLEN)
    return (jnp.cos(angles).astype(jnp.bfloat16), jnp.sin(angles).astype(jnp.bfloat16))


def filter_rows(residual, response, forward, inverse):
    sample_rows = residual.astype(jnp.bfloat16)
    spectrum = jnp.dot(sample_rows, forward, preferred_element_type=jnp.float32)
    shaped = (spectrum * response[None, :]).astype(jnp.bfloat16)
    filtered = jnp.dot(shaped, inverse, preferred_element_type=jnp.float32) / FLEN
    return filtered


def shards(
    timestream,
    sample_flags,
    pointing,
    tile_ids,
    block_offsets,
    tile_owner,
    det_gains,
    mode_vectors,
    filter_gain,
):
    hi = lax.Precision.HIGHEST
    cosine, sine = spectral_tables()
    forward = jnp.concatenate([cosine, sine], axis=1)
    inverse = jnp.concatenate([cosine, sine], axis=0)
    full_gain = jnp.concatenate([filter_gain, filter_gain[1 : FLEN // 2][::-1]])
    response = jnp.concatenate([full_gain, full_gain])
    keep = (1 - sample_flags).astype(jnp.float32)
    seg_count, per_seg = tile_ids.shape
    listed = seg_count * per_seg
    tile_count = tile_owner.shape[0]
    own_rows = TILES_DEV * BLOCKS_TILE
    tile_match = tile_ids[:, :, None] == lax.iota(jnp.int32, tile_count)[None, None, :]
    owner_slot = jnp.sum(jnp.where(tile_match, tile_owner[None, None, :], 0), axis=-1)
    target_rows = (owner_slot * BLOCKS_TILE + block_offsets).reshape(-1)
    my_first = lax.axis_index(("det", "tm")) * own_rows
    squares = jnp.einsum("sktp,sktp->skp", pointing, pointing, preferred_element_type=jnp.float32)
    weights = (jnp.sum(det_gains * det_gains) * squares).reshape(listed, TILE)

    def clean_data(signal_rows):
        residual = (timestream - det_gains[:, None] * signal_rows[None, :]) * keep
        filtered = filter_rows(residual, response, forward, inverse)
        amplitudes = lax.psum(
            jnp.dot(mode_vectors.T, filtered, precision=hi).astype(jnp.bfloat16), "det"
        ).astype(jnp.float32)
        return filtered - jnp.dot(mode_vectors, amplitudes, precision=hi)

    def project(clean):
        summed = (
            jnp.dot(det_gains, clean, precision=hi).astype(jnp.bfloat16).reshape(seg_count, SEGLEN)
        )
        projected = jnp.einsum("sktp,st->skp", pointing, summed, preferred_element_type=jnp.float32)
        return projected.reshape(listed, TILE)

    def accumulate(values):
        values_part = lax.all_gather(values, ("det", "tm"), axis=0, tiled=True)
        rows_part = lax.all_gather(target_rows, ("det", "tm"), axis=0, tiled=True)
        onehot = ((rows_part - my_first)[None, :] == lax.iota(jnp.int32, own_rows)[:, None]).astype(
            jnp.float32
        )
        return jnp.dot(onehot, values_part, precision=hi)

    first_clean = clean_data(jnp.zeros((timestream.shape[1],), jnp.float32))
    sums = accumulate(jnp.concatenate([project(first_clean), weights], axis=1))
    weight_sum = sums[:, TILE:] + 1.0
    map_rows = sums[:, :TILE] / weight_sum
    map_half = map_rows.astype(jnp.bfloat16)
    shard_part = lax.all_gather(map_half, ("det", "tm"), axis=0, tiled=True)
    onehot = (target_rows[:, None] == lax.iota(jnp.int32, shard_part.shape[0])[None, :]).astype(
        jnp.bfloat16
    )
    fetched = jnp.dot(onehot, shard_part, preferred_element_type=jnp.float32)
    fetched = fetched.astype(jnp.bfloat16).reshape(seg_count, per_seg, TILE)
    signal_rows = jnp.einsum(
        "sktp,skp->st", pointing, fetched, preferred_element_type=jnp.float32
    ).reshape(-1)
    second_clean = clean_data(signal_rows)
    second_sums = accumulate(project(second_clean))
    map_rows = map_rows + second_sums / weight_sum
    tile_snr = (map_rows * jnp.sqrt(weight_sum)).reshape(TILES_DEV, BLOCKS_TILE, TILE)
    return (tile_snr, second_clean.astype(jnp.bfloat16))


def solution(mesh):
    return jax.shard_map(
        shards,
        mesh=mesh,
        in_specs=(
            P("det", "tm"),
            P("det", "tm"),
            P("tm", None, None, None),
            P("tm", None),
            P("tm", None),
            P(),
            P("det"),
            P("det", None),
            P(),
        ),
        out_specs=(P(("det", "tm"), None, None), P("det", "tm")),
        check_vma=False,
    )
```

profile of v0, /device:TPU:0, one launch (start us, length us, event | category | flops | bytes accessed | tf_op | source)
XLA Modules:
  0.0 246.9 jit_solution(13828459270647979635)
XLA Ops:
  7.2 0.0 copy-start
  7.2 0.0 copy-start.3
  7.2 0.0 copy-start.6
  7.2 0.0 copy-start.5
  7.2 0.0 copy-start.4
  7.2 0.0 copy-start.2
  7.2 0.0 copy-start.1
  7.2 0.0 all-gather.2.cloned.1.call-start
  7.3 4.3 %sine_convert_fusion = (bf16[512,512]{1,0:T(8,128)(2,1)S(1)}, bf16[512,512]{1,0:T(8,128)(2,1)S(1)}) fusion(), kind=kLoop, calls=%fused_computation.30 | loop fusion | flops 4194304 | bytes 1048576 | tf_op jit(solution)/shard_map/convert_element_type | solution.py:19
  11.6 0.0 copy-done.3
  11.6 0.1 slice.9
  11.7 0.1 reverse
  11.8 0.1 slice.28
  11.9 0.0 copy-done.6
  11.9 0.0 copy-done.5
  11.9 0.2 select_reduce_fusion
  12.1 0.0 copy-done.4
  12.1 0.1 reshape.43
  12.2 0.2 dynamic-update-slice
  12.4 42.0 %all-reduce = s32[512]{0:T(512)S(1)} all-reduce(s32[512]{0:T(512)S(1)} %dynamic-update-slice), channel_id=1, replica_groups=mesh['det'=4,'tm'=8] {'det','tm'}, use_global_device_ids=true, to_apply=%add | all-reduce | flops 512 | bytes 4096
  54.4 0.0 copy-done.2
  54.4 0.6 broadcast_multiply_fusion.1
  55.0 0.1 pad_maximum_fusion.9
  55.0 0.0 copy-done.1
  55.0 0.1 fusion.10
  55.2 2.9 %convolution_multiply_fusion.1 = f32[512,512]{1,0:T(8,128)S(1)} fusion(f32[1024]{0:T(1024)S(1)} %pad_maximum_fusion.9, bf16[512,512]{1,0:T(8,128)(2,1)S(1)} %get-tuple-element.6, bf16[512,512]{1,0:T(8,128)(2,1)S(1)} %get-tuple-element.7, f32[512,512]{1,0:T(8,128)} %param.9, s32[512,512]{1,0:T(8,128)} %param.10, f32[512]{0:T(512)S(1)} %get-tuple-element.2), kind=kOutput, calls=%fused_computation.10 | convolution fusion | flops 1080557568 | bytes 4200448 | tf_op jit(solution)/shard_map/dot_general | solution.py:26
  58.1 0.0 copy-done
  58.1 1.8 fusion.2
  59.9 18.3 %psum.14 = bf16[32,512]{0,1:T(8,128)(2,1)S(1)} all-reduce(bf16[32,512]{0,1:T(8,128)(2,1)S(1)} %fusion.2), channel_id=1, replica_groups=mesh['det'=4,'tm'=8] {'det'}, use_global_device_ids=true, to_apply=%region_1.2 | all-reduce | flops 16384 | bytes 65536 | tf_op jit(solution)/shard_map/psum | solution.py:62
  78.2 0.7 fusion.1
  78.9 0.6 fusion.46
  79.5 0.2 fusion.34
  79.7 0.7 broadcast_multiply_fusion
  80.4 41.1 %all_gather.14 = f32[512,256]{1,0:T(8,128)S(1)} all-gather(f32[16,256]{1,0:T(8,128)S(1)} %pad_maximum_fusion.8), channel_id=1, replica_groups=mesh['det'=4,'tm'=8] {'det','tm'}, dimensions={0}, use_global_device_ids=true | all-gather | bytes 540672 | tf_op jit(solution)/shard_map/all_gather | solution.py:75
  121.5 0.3 fusion.26
  121.8 0.6 fusion.44
  122.5 0.0 all-gather.2.cloned.1.call-update
  122.5 50.7 %all-gather.2.cloned.1.call-done = bf16[4096,128]{1,0:T(8,128)(2,1)} async-done(((bf16[128,128]{1,0:T(8,128)(2,1)}), bf16[4096,128]{1,0:T(8,128)(2,1)}) %all-gather.2.cloned.1.call-update) | async-done | bytes 1048592 | tf_op jit(solution)/shard_map/all_gather | solution.py:87
  173.2 1.5 convolution_convert_fusion.2
  174.7 0.2 fusion.30
  174.9 2.9 %convolution_multiply_fusion = f32[512,512]{1,0:T(8,128)S(1)} fusion(f32[1024]{0:T(1024)S(1)} %pad_maximum_fusion.9, bf16[512,512]{1,0:T(8,128)(2,1)S(1)} %get-tuple-element.6, bf16[512,512]{1,0:T(8,128)(2,1)S(1)} %get-tuple-element.7, f32[512,512]{1,0:T(8,128)} %param.9, s32[512,512]{1,0:T(8,128)} %param.10, f32[512]{0:T(512)S(1)} %bitcast.77, ...), kind=kOutput, calls=%fused_computation.7 | convolution fusion | flops 1080819712 | bytes 4202496 | tf_op jit(solution)/shard_map/dot_general | solution.py:26
  177.8 1.8 fusion.3
  179.6 17.2 %psum.15 = bf16[32,512]{0,1:T(8,128)(2,1)S(1)} all-reduce(bf16[32,512]{0,1:T(8,128)(2,1)S(1)} %fusion.3), channel_id=1, replica_groups=mesh['det'=4,'tm'=8] {'det'}, use_global_device_ids=true, to_apply=%region_3.4 | all-reduce | flops 16384 | bytes 65536 | tf_op jit(solution)/shard_map/psum | solution.py:62
  196.9 1.5 fusion.45
  198.4 0.6 fusion.47
  199.0 0.2 fusion.32
  199.2 39.9 %all_gather.16 = f32[512,128]{1,0:T(8,128)S(1)} all-gather(f32[16,128]{1,0:T(8,128)S(1)} %bitcast.68), channel_id=1, replica_groups=mesh['det'=4,'tm'=8] {'det','tm'}, dimensions={0}, use_global_device_ids=true | all-gather | bytes 270336 | tf_op jit(solution)/shard_map/all_gather | solution.py:75
  239.1 0.9 fusion.6
  (6 shorter events, 0.0 us)
Async XLA Ops:
  7.2 50.9 %copy-start = (f32[512,32]{0,1:T(8,128)S(1)}, f32[512,32]{0,1:T(8,128)}, u32[]{:S(2)}) copy-start(f32[512,32]{0,1:T(8,128)} %param.16) | copy-start | bytes 196612
  7.2 4.4 %copy-start.3 = (f32[257]{0:T(512)S(1)}, f32[257]{0:T(512)}, u32[]{:S(2)}) copy-start(f32[257]{0:T(512)} %param.17) | copy-start | bytes 3088
  7.2 4.7 %copy-start.6 = (s32[32]{0:T(128)S(1)}, s32[32]{0:T(128)}, u32[]{:S(2)}) copy-start(s32[32]{0:T(128)} %param.14) | copy-start | bytes 388
  7.2 4.7 %copy-start.5 = (s32[4,4]{1,0:T(4,128)S(1)}, s32[4,4]{1,0:T(4,128)}, u32[]{:S(2)}) copy-start(s32[4,4]{1,0:T(4,128)} %param.12) | copy-start | bytes 196
  7.2 4.9 %copy-start.4 = (s32[4,4]{1,0:T(4,128)S(1)}, s32[4,4]{1,0:T(4,128)}, u32[]{:S(2)}) copy-start(s32[4,4]{1,0:T(4,128)} %param.13) | copy-start | bytes 196
  7.2 47.1 %copy-start.2 = (f32[512]{0:T(512)S(1)}, f32[512]{0:T(512)}, u32[]{:S(2)}) copy-start(f32[512]{0:T(512)} %param.15) | copy-start | bytes 6148
  7.2 47.8 %copy-start.1 = (bf16[4,4,128,128]{3,2,1,0:T(8,128)(2,1)S(1)}, bf16[4,4,128,128]{3,2,1,0:T(8,128)(2,1)}, u32[]{:S(2)}) copy-start(bf16[4,4,128,128]{3,2,1,0:T(8,128)(2,1)} %param.11) | copy-start | bytes 1572868
  7.2 165.9 %all-gather.2.cloned.1.call-start = ((), (), s32[]{:S(2)}) async-start(), calls=%async_computation | async-start | bytes 1081344 | tf_op jit(solution)/shard_map/all_gather | solution.py:87
Sparse Core Ops, SparseCore 0:
  122.6 50.5 all-gather.1
where the time goes:
time: 247 us
  blocking collectives  159 us (64%)
  waiting for transfers between devices  50.7 us (21%)
  matrix products  16.2 us (7%)
  between operations  14.2 us (6%)
  other arithmetic  6.63 us (3%)
    all_gather x2, blocking collectives, accumulate(): values_part = lax.all_gather(values, ('det', 'tm'), axis=0, tiled=True)  81 us
    all_gather x1, waiting for transfers between devices, shards(): shard_part = lax.all_gather(map_half, ('det', 'tm'), axis=0, tiled=True)  50.7 us
    unnamed x1, blocking collectives  42 us
    psum x2, blocking collectives, clean_data(): lax.psum(jnp.dot(mode_vectors.T, filtered, precision=hi).astype(jnp.bfloa...  35.5 us
    dot_general x2, matrix products, filter_rows(): jnp.dot(shaped, inverse, preferred_element_type=jnp.float32) / FLEN  5.8 us
  transfers between devices with their start and end apart: 1, of which 1 were waited for; matrix products, arithmetic and copies ran while one was open for 0% of the time, Pallas kernels for 0%

commit v1 on v0

v1 whole, which is shorter than its diff:
```python
import functools
import math

import jax
import jax.numpy as jnp
import numpy as np
from jax import lax
from jax.experimental import pallas as pl
from jax.experimental.pallas import tpu as pltpu
from jax.sharding import PartitionSpec as P

F32 = jnp.float32
BF16 = jnp.bfloat16
LANES = 128
BASE = 128
DIGITS = 3
EXT = 16
NN = (((1,), (0,)), ((), ()))
NT = (((1,), (1,)), ((), ()))


def mm(a, b, dims=NN):
    return lax.dot_general(a, b, dims, preferred_element_type=F32)


def split(x):
    hi = x.astype(BF16)
    return hi, (x - hi.astype(F32)).astype(BF16)


def iota(shape, axis):
    return lax.broadcasted_iota(jnp.int32, shape, axis)


def cosine_table(flen, rows):
    f = np.arange(rows)[:, None]
    n = np.arange(flen)[None, :]
    scale = np.where((f == 0) | (f == flen // 2), 1.0, 2.0) / flen
    scale = np.where(f <= flen // 2, scale, 0.0)
    return (scale * np.cos(2.0 * math.pi * ((f * n) % flen) / flen)).astype(np.float32)


def sums_kernel(modes, ts_ref, flag_ref, v_ref, g_ref, msg_ref, acc1, acc2, small):
    step = pl.program_id(0)
    chunk, samples = ts_ref.shape
    keep = (1 - flag_ref[...]).astype(F32)
    x_hi, x_lo = split(ts_ref[...] * keep)
    v = v_ref[...]
    vt = v.T
    g = g_ref[...]
    row = iota((EXT, chunk), 0)
    left1 = jnp.concatenate([vt, jnp.where(row < 2, g, 0.0)], axis=0)
    left2 = jnp.concatenate([vt * g, jnp.where((row >= 2) & (row < 4), g * g, 0.0)], axis=0)
    hi1, lo1 = split(left1)
    hi2, lo2 = split(left2)
    n = modes + EXT
    both = mm(jnp.concatenate([hi1, lo1], axis=0), x_hi)
    part1 = both[:n] + both[n:] + mm(hi1, x_lo)
    both = mm(jnp.concatenate([hi2, lo2], axis=0), keep.astype(BF16))
    part2 = both[:n] + both[n:]
    u_row = (row >= 4) & (row < 6)
    v_wide = jnp.concatenate([v, jnp.zeros((chunk, LANES - modes), F32)], axis=1)
    u_part = lax.dot_general(
        jnp.where(u_row, g, 0.0), v_wide, NN, precision=lax.Precision.HIGHEST, preferred_element_type=F32
    )
    square = jnp.sum(g * g, axis=1, keepdims=True)
    r = iota((EXT, LANES), 0)
    here = (r >= 4) & (r < 6) & (iota((EXT, LANES), 1) == modes)
    u_part = u_part + jnp.where(here, square, 0.0)

    @pl.when(step == 0)
    def _():
        acc1[...] = part1
        acc2[...] = part2
        small[...] = u_part

    @pl.when(step > 0)
    def _():
        acc1[...] += part1
        acc2[...] += part2
        small[...] += u_part

    @pl.when(step == pl.num_programs(0) - 1)
    def _():
        msg_ref[0:modes] = acc1[0:modes].astype(BF16)
        msg_ref[modes : 2 * modes] = acc2[0:modes].astype(BF16)
        wide = jnp.concatenate([small[...], jnp.zeros((EXT, samples - LANES), F32)], axis=1)
        ext = acc1[modes:] + acc2[modes:] + wide
        hi = ext.astype(BF16).astype(F32)
        odd = iota((EXT, samples), 0) % 2 == 1
        msg_ref[2 * modes :] = jnp.where(odd, ext - hi, hi).astype(BF16)


def prep_kernel(seg, kblk, tids_ref, offs_ref, owner_ref, pos_ref, gain_ref, cos_ref, point_ref, v_ref,
                hhi_ref, hlo_ref, v3_ref, geo_ref, own_ref):
    flen = cos_ref.shape[1]
    gain8 = jnp.broadcast_to(gain_ref[...], (8, gain_ref.shape[1]))
    h = lax.dot_general(gain8, cos_ref[...], NN, precision=lax.Precision.HIGHEST, preferred_element_type=F32)
    base = jnp.broadcast_to(h[0:1], (LANES, flen))
    base = pltpu.roll(base, 0, 1, stride=1, stride_axis=0)
    base_hi, base_lo = split(base)
    blocks = flen // LANES
    for a in range(blocks):
        for b in range(blocks):
            c = (b - a) % blocks
            to = (slice(a * LANES, (a + 1) * LANES), slice(b * LANES, (b + 1) * LANES))
            hhi_ref[to] = base_hi[:, c * LANES : (c + 1) * LANES]
            hlo_ref[to] = base_lo[:, c * LANES : (c + 1) * LANES]
    vt = v_ref[...].T
    vhi = vt.astype(BF16).astype(F32)
    pad = jnp.zeros((LANES - 3 * vt.shape[0], vt.shape[1]), F32)
    v3_ref[...] = jnp.concatenate([vhi, vhi, vt - vhi, pad], axis=0).T.astype(BF16)
    listed = seg * kblk
    row16 = iota((listed, LANES), 0)
    lane16 = iota((listed, LANES), 1)
    first = pos_ref[0] * listed
    lane_blocks = pos_ref[1]
    squares = jnp.zeros((listed, LANES), F32)
    ids = jnp.zeros((listed, LANES), F32)
    own = jnp.zeros((listed, LANES), F32)
    for k in range(kblk):
        for s in range(seg):
            j = k * seg + s
            p = point_ref[s, k].astype(F32)
            squares = jnp.where(row16 == j, jnp.sum(p * p, axis=0, keepdims=True), squares)
            target = owner_ref[tids_ref[s, k]] * LANES + offs_ref[s, k]
            own = jnp.where(row16 == j, target.astype(F32), own)
            place = first + j
            digit = target
            for d in range(DIGITS):
                at = (row16 == d * lane_blocks + place // LANES) & (lane16 == place % LANES)
                ids = jnp.where(at, (digit % BASE).astype(F32), ids)
                digit = digit // BASE
    geo_ref[0:listed] = squares.astype(BF16)
    geo_ref[listed:] = ids.astype(BF16)
    own_ref[...] = own


def matvec(b, hhi, hlo):
    hi, lo = split(b)
    row = iota((EXT, b.shape[1]), 0)
    left = jnp.where(row == 0, hi.astype(F32), jnp.where(row == 1, lo.astype(F32), 0.0)).astype(BF16)
    z = mm(left, hhi) + mm(left, hlo)
    return z[0:1] + z[1:2]


def project(z, point_ref, seg, kblk):
    samples = z.shape[1]
    listed = seg * kblk
    hi, lo = split(z)
    row = iota((2 * listed, samples), 0)
    lane = iota((2 * listed, samples), 1)
    wide = jnp.where(row < listed, hi.astype(F32), lo.astype(F32))
    wide = jnp.where(lane // (samples // seg) == row % seg, wide, 0.0)
    out = jnp.zeros((2 * listed, point_ref.shape[3]), F32)
    for k in range(kblk):
        left = jnp.where((row % listed) // seg == k, wide, 0.0).astype(BF16)
        out = out + mm(left, point_ref[:, k].reshape(samples, -1))
    return out[:listed] + out[listed:]


def first_kernel(modes, seg, kblk, m0, m1, m2, m3, hhi_ref, hlo_ref, point_ref, geo_ref,
                 bq_ref, vec_ref, send_ref):
    tot = m0[...].astype(F32) + m1[...].astype(F32) + m2[...].astype(F32) + m3[...].astype(F32)
    bq_ref[...] = tot[0 : 2 * modes]
    ext = tot[2 * modes :]
    u_row = ext[4:5, 0:LANES] + ext[5:6, 0:LANES]
    u_col = jnp.sum(jnp.where(iota((modes, LANES), 0) == iota((modes, LANES), 1), u_row, 0.0), axis=1, keepdims=True)
    square = jnp.sum(jnp.where(iota((1, LANES), 1) == modes, u_row, 0.0), axis=1, keepdims=True)
    b1 = ext[0:1] + ext[1:2] - jnp.sum(u_col * tot[0:modes], axis=0, keepdims=True)
    b2 = ext[2:3] + ext[3:4] - jnp.sum(u_col * tot[modes : 2 * modes], axis=0, keepdims=True)
    row = iota((8, b1.shape[1]), 0)
    vec_ref[...] = jnp.where(row == 0, b1, jnp.where(row == 1, b2, jnp.where(row == 2, square, 0.0)))
    z = matvec(b1, hhi_ref[...], hlo_ref[...])
    proj = project(z, point_ref, seg, kblk).astype(BF16)
    geo = geo_ref[...]
    listed = seg * kblk
    for t in range(send_ref.shape[0]):
        send_ref[t, 0:listed] = proj
        send_ref[t, listed:] = geo


def lane_ids(all_ref, listed, blocks, b):
    ids = jnp.sum(all_ref[:, 2 * listed :].astype(F32), axis=0)
    out = ids[b : b + 1]
    for d in range(1, DIGITS):
        out = out + float(BASE**d) * ids[d * blocks + b : d * blocks + b + 1]
    return out


def second_kernel(seg, kblk, all_ref, own_ref, vec_ref, hhi_ref, hlo_ref, point_ref, sig_ref, send_ref):
    listed = seg * kblk
    blocks = all_ref.shape[0] * listed // LANES
    samples = vec_ref.shape[1]
    per = LANES // listed
    own = own_ref[...]
    psum = jnp.zeros((listed, LANES), F32)
    wsum = jnp.zeros((listed, LANES), F32)
    for b in range(blocks):
        same = (own == lane_ids(all_ref, listed, blocks, b)).astype(F32).astype(BF16)
        part = all_ref[b * per : (b + 1) * per]
        psum = psum + mm(same, part[:, 0:listed].reshape(LANES, LANES))
        wsum = wsum + mm(same, part[:, listed : 2 * listed].reshape(LANES, LANES))
    square = vec_ref[2:3, 0:LANES]
    fetched = (psum / (1.0 + square * wsum)).astype(BF16)
    row = iota((listed, samples), 0)
    lane = iota((listed, samples), 1)
    spread = jnp.zeros((listed, samples), F32)
    for k in range(kblk):
        out = mm(fetched, point_ref[:, k].reshape(samples, -1), NT)
        spread = spread + jnp.where((row // seg == k) & (lane // (samples // seg) == row % seg), out, 0.0)
    sig = jnp.sum(spread, axis=0, keepdims=True)
    sig_ref[...] = jnp.broadcast_to(sig, sig_ref.shape)
    z = matvec(vec_ref[0:1] - vec_ref[1:2] * sig, hhi_ref[...], hlo_ref[...])
    proj = project(z, point_ref, seg, kblk).astype(BF16)
    for t in range(send_ref.shape[0]):
        send_ref[t] = proj


def clean_kernel(modes, ts_ref, flag_ref, g_ref, v3_ref, bq_ref, sig_ref, hhi_ref, hlo_ref, out_ref):
    chunk = ts_ref.shape[0]
    sig = sig_ref[0:1]
    q_hi, q_lo = split(bq_ref[0:modes] - bq_ref[modes : 2 * modes] * sig)
    pad = jnp.zeros((LANES - 3 * modes, q_hi.shape[1]), BF16)
    q3 = jnp.concatenate([q_hi, q_lo, q_hi, pad], axis=0)
    eye = iota((chunk, chunk), 0) == iota((chunk, chunk), 1)
    g_col = jnp.sum(jnp.where(eye, g_ref[...], 0.0), axis=1, keepdims=True)
    keep = (1 - flag_ref[...]).astype(F32)
    rest = (ts_ref[...] - g_col * sig) * keep - mm(v3_ref[...], q3)
    rest = rest.astype(BF16)
    out_ref[...] = (mm(rest, hhi_ref[...]) + mm(rest, hlo_ref[...])).astype(BF16)


def tile_kernel(seg, kblk, first_ref, all_ref, all2_ref, vec_ref, out_ref):
    listed = seg * kblk
    blocks = all_ref.shape[0] * listed // LANES
    per = LANES // listed
    psum1 = jnp.zeros((LANES, LANES), F32)
    psum2 = jnp.zeros((LANES, LANES), F32)
    wsum = jnp.zeros((LANES, LANES), F32)
    mine = (iota((LANES, LANES), 0) + first_ref[0]).astype(F32)
    for b in range(blocks):
        same = (mine == lane_ids(all_ref, listed, blocks, b)).astype(F32).astype(BF16)
        part = all_ref[b * per : (b + 1) * per]
        psum1 = psum1 + mm(same, part[:, 0:listed].reshape(LANES, LANES))
        wsum = wsum + mm(same, part[:, listed : 2 * listed].reshape(LANES, LANES))
        psum2 = psum2 + mm(same, all2_ref[b * per : (b + 1) * per].reshape(LANES, LANES))
    wsum = 1.0 + vec_ref[2:3, 0:LANES] * wsum
    out_ref[0] = (psum1 / wsum + psum2 / wsum) * jnp.sqrt(wsum)


VM = pl.BlockSpec(memory_space=pltpu.VMEM)
SM = pl.BlockSpec(memory_space=pltpu.SMEM)


def shape(dims, dtype=F32):
    return jax.ShapeDtypeStruct(dims, dtype)


def others(x, axis, n):
    if n & (n - 1) == 0:
        pairs = [[(i, i ^ k) for i in range(n)] for k in range(1, n)]
    else:
        pairs = [[(i, (i + k) % n) for i in range(n)] for k in range(1, n)]
    return [lax.ppermute(x, axis, p) for p in pairs]


def shards(n_det, n_tm, timestream, sample_flags, pointing, tile_ids, block_offsets, tile_owner, det_gains,
           mode_vectors, filter_gain):
    dets, samples = timestream.shape
    modes = mode_vectors.shape[1]
    seg, kblk = tile_ids.shape
    listed = seg * kblk
    chunk = LANES
    grid = (dets // chunk,)
    g = det_gains.reshape(1, dets)
    msg = pl.pallas_call(
        functools.partial(sums_kernel, modes),
        grid=grid,
        in_specs=[
            pl.BlockSpec((chunk, samples), lambda i: (i, 0)),
            pl.BlockSpec((chunk, samples), lambda i: (i, 0)),
            pl.BlockSpec((chunk, modes), lambda i: (i, 0)),
            pl.BlockSpec((1, chunk), lambda i: (0, i)),
        ],
        out_specs=pl.BlockSpec((2 * modes + EXT, samples), lambda i: (0, 0)),
        out_shape=shape((2 * modes + EXT, samples), BF16),
        scratch_shapes=[
            pltpu.VMEM((modes + EXT, samples), F32),
            pltpu.VMEM((modes + EXT, samples), F32),
            pltpu.VMEM((EXT, LANES), F32),
        ],
        name="sums",
    )(timestream, sample_flags, mode_vectors, g)
    parts = [msg] + others(msg, "det", n_det)

    rows = -(-filter_gain.shape[0] // LANES) * LANES
    gain = jnp.pad(filter_gain, (0, rows - filter_gain.shape[0])).reshape(1, rows)
    tm_at = lax.axis_index("tm")
    place = jnp.stack([tm_at, jnp.int32(n_tm * listed // LANES)]).astype(jnp.int32)
    hhi, hlo, v3, geo, own = pl.pallas_call(
        functools.partial(prep_kernel, seg, kblk),
        in_specs=[SM, SM, SM, SM, VM, VM, VM, VM],
        out_specs=[VM] * 5,
        out_shape=[
            shape((samples, samples), BF16),
            shape((samples, samples), BF16),
            shape((dets, LANES), BF16),
            shape((2 * listed, LANES), BF16),
            shape((listed, LANES)),
        ],
        cost_estimate=pl.CostEstimate(flops=10**8, bytes_accessed=3 * 10**6, transcendentals=0),
        name="prep",
    )(tile_ids, block_offsets, tile_owner, place, gain, jnp.asarray(cosine_table(samples, rows)), pointing,
      mode_vectors)

    bq, vec, send = pl.pallas_call(
        functools.partial(first_kernel, modes, seg, kblk),
        in_specs=[VM] * 8,
        out_specs=[VM] * 3,
        out_shape=[
            shape((2 * modes, samples)),
            shape((8, samples)),
            shape((n_tm, 3 * listed, LANES), BF16),
        ],
        name="first",
    )(*parts, hhi, hlo, pointing, geo)
    everyone = lax.all_to_all(send, "tm", 0, 0)

    sig, send = pl.pallas_call(
        functools.partial(second_kernel, seg, kblk),
        in_specs=[VM] * 6,
        out_specs=[VM] * 2,
        out_shape=[shape((8, samples)), shape((n_tm, listed, LANES), BF16)],
        name="second",
    )(everyone, own, vec, hhi, hlo, pointing)
    everyone2 = lax.all_to_all(send, "tm", 0, 0)

    cleaned = pl.pallas_call(
        functools.partial(clean_kernel, modes),
        grid=grid,
        in_specs=[
            pl.BlockSpec((chunk, samples), lambda i: (i, 0)),
            pl.BlockSpec((chunk, samples), lambda i: (i, 0)),
            pl.BlockSpec((1, chunk), lambda i: (0, i)),
            pl.BlockSpec((chunk, LANES), lambda i: (i, 0)),
            pl.BlockSpec((2 * modes, samples), lambda i: (0, 0)),
            pl.BlockSpec((8, samples), lambda i: (0, 0)),
            pl.BlockSpec((samples, samples), lambda i: (0, 0)),
            pl.BlockSpec((samples, samples), lambda i: (0, 0)),
        ],
        out_specs=pl.BlockSpec((chunk, samples), lambda i: (i, 0)),
        out_shape=shape((dets, samples), BF16),
        cost_estimate=pl.CostEstimate(flops=10**9, bytes_accessed=4 * 10**6, transcendentals=0),
        name="clean",
    )(timestream, sample_flags, g, v3, bq, sig, hhi, hlo)

    first_row = (lax.axis_index(("det", "tm")) * LANES).reshape(1).astype(jnp.int32)
    tile = pl.pallas_call(
        functools.partial(tile_kernel, seg, kblk),
        in_specs=[SM, VM, VM, VM],
        out_specs=VM,
        out_shape=shape((1, LANES, LANES)),
        name="tile",
    )(first_row, everyone, everyone2, vec)
    return tile, cleaned


def solution(mesh):
    return jax.shard_map(
        functools.partial(shards, mesh.shape["det"], mesh.shape["tm"]),
        mesh=mesh,
        in_specs=(
            P("det", "tm"),
            P("det", "tm"),
            P("tm", None, None, None),
            P("tm", None),
            P("tm", None),
            P(),
            P("det"),
            P("det", None),
            P(),
        ),
        out_specs=(P(("det", "tm"), None, None), P("det", "tm")),
        check_vma=False,
    )
```

time: 247 us -> 46 us (0.19)
  blocking collectives: 159 us -> 0 us
  waiting for transfers between devices: 50.7 us -> 7.64 us
  Pallas kernels: 0 us -> 18.9 us
  matrix products: 16.2 us -> 0 us
  between operations: 14.2 us -> 0.68 us
  starting transfers between devices: 0.04 us -> 12.8 us
  other arithmetic: 6.63 us -> 0.65 us
  local copies, waits for them, and re-layouts: 0.55 us -> 4.79 us
    all_gather x2 -> x0, blocking collectives: 81 us -> none  [accumulate(): values_part = lax.all_gather(values, ('det', 'tm'), axis=0, tiled=True)]
    all_gather x1 -> x0, waiting for transfers between devices: 50.7 us -> none  [shards(): shard_part = lax.all_gather(map_half, ('det', 'tm'), axis=0, tiled=True)]
    unnamed x1 -> x0, blocking collectives: 42 us -> none
    psum x2 -> x0, blocking collectives: 35.5 us -> none  [clean_data(): lax.psum(jnp.dot(mode_vectors.T, filtered, precision=hi).astype(jnp.bfloa...]
    pallas_call x0 -> x6, Pallas kernels: none -> 18.9 us  [the longest x1 4.8 us: shards(): pl.pallas_call(functools.partial(clean_kernel, modes), grid=grid, in_spec...]
    dot_general x14 -> x0, matrix products: 16.2 us -> none  [the longest x2 5.8 us: filter_rows(): jnp.dot(shaped, inverse, preferred_element_type=jnp.float32) / FLEN]
    all_to_all x0 -> x2, starting transfers between devices: none -> 8.27 us  [the longest x1 4.93 us: shards(): everyone = lax.all_to_all(send, 'tm', 0, 0)]
    all_to_all x0 -> x2, waiting for transfers between devices: none -> 7.18 us  [the longest x1 6.31 us: shards(): everyone = lax.all_to_all(send, 'tm', 0, 0)]
  transfers between devices with their start and end apart: 1 -> 5, of which waited for: 1 -> 3; matrix products, arithmetic and copies ran while one was open for 0% -> 3% of each run, Pallas kernels for 0% -> 17%
where the time goes in v1:
time: 46 us; the launch traced here: 45.5 us
  Pallas kernels  18.9 us (41%)
  starting transfers between devices  12.8 us (28%)
  waiting for transfers between devices  7.64 us (17%)
  local copies, waits for them, and re-layouts  4.79 us (10%)
  between operations  0.68 us (1%)
  other arithmetic  0.65 us (1%)
    all_to_all x1, waiting for transfers between devices, shards(): everyone = lax.all_to_all(send, 'tm', 0, 0)  6.31 us
    all_to_all x1, starting transfers between devices, shards(): everyone = lax.all_to_all(send, 'tm', 0, 0)  4.93 us
    pallas_call x1, Pallas kernels, shards(): pl.pallas_call(functools.partial(clean_kernel, modes), grid=grid, in_spec...  4.8 us
    ppermute x3, starting transfers between devices, others(): return [lax.ppermute(x, axis, p) for p in pairs]  4.49 us
    unnamed x13, local copies, waits for them, and re-layouts  4.21 us
    pallas_call x1, Pallas kernels, shards(): pl.pallas_call(functools.partial(sums_kernel, modes), grid=grid, in_specs...  3.76 us
    all_to_all x1, starting transfers between devices, shards(): everyone2 = lax.all_to_all(send, 'tm', 0, 0)  3.34 us
    pallas_call x1, Pallas kernels, shards(): pl.pallas_call(functools.partial(prep_kernel, seg, kblk), in_specs=[SM, S...  3.14 us
  transfers between devices with their start and end apart: 5, of which 3 were waited for; matrix products, arithmetic and copies ran while one was open for 3% of the time, Pallas kernels for 17%

profile of v1, /device:TPU:0, one launch (start us, length us, event | category | flops | bytes accessed | tf_op | source)
XLA Modules:
  0.0 45.5 jit_solution(5741858028381047929)
XLA Ops:
  0.6 1.7 %copy.12.v_ref = f32[512,32]{1,0:T(8,128)} copy(f32[512,32]{0,1:T(8,128)} %param.17) | data formatting | bytes 131072 | tf_op args[7]
  2.3 3.8 %sums.1.m0 = bf16[80,512]{1,0:T(8,128)(2,1)} custom-call(f32[512,512]{1,0:T(8,128)} %ts_ref.3, s32[512,512]{1,0:T(8,128)} %flag_ref.3, f32[512,32]{1,0:T(8,128)} %copy.12.v_ref, f32[1,512]{1,0:T(1,128)} %bitcast.3), custom_call_target="tpu_custom_call" | custom-call | tf_op jit(solution)/shard_map/sums/pallas_call | solution.py:277
  6.1 3.0 %collective-permute-start = (bf16[80,512]{1,0:T(8,128)(2,1)}, bf16[80,512]{1,0:T(8,128)(2,1)S(1)}, u32[]{:S(2)}, u32[]{:S(2)}) collective-permute-start(bf16[80,512]{1,0:T(8,128)(2,1)} %sums.1.m0), channel_id=1, source_target_pairs={{0,8},{8,0},{16,24},{24,16},{1,9},{9,1},{17,25},{25,17},{2,10},{10... | collective-permute-start | bytes 245768 | tf_op jit(solution)/shard_map/ppermute | solution.py:265
  9.0 1.5 %collective-permute-start.1 = (bf16[80,512]{1,0:T(8,128)(2,1)}, bf16[80,512]{1,0:T(8,128)(2,1)S(1)}, u32[]{:S(2)}, u32[]{:S(2)}) collective-permute-start(bf16[80,512]{1,0:T(8,128)(2,1)} %sums.1.m0), channel_id=1, source_target_pairs={{0,16},{8,24},{16,0},{24,8},{1,17},{9,25},{17,1},{25,9},{2,18},{10... | collective-permute-start | bytes 245768 | tf_op jit(solution)/shard_map/ppermute | solution.py:265
  10.6 0.0 collective-permute-start.2
  10.6 0.0 copy-start.5
  10.6 0.7 %copy-done.5 = f32[257]{0:T(512)S(1)} copy-done((f32[257]{0:T(512)S(1)}, f32[257]{0:T(512)}, u32[]{:S(2)}) %copy-start.5) | copy-done | bytes 1052
  11.2 0.6 %reshape.15.gain_ref = f32[1,384]{1,0:T(1,128)} reshape(f32[384]{0:T(512)S(1)} %pad.4) | data formatting | bytes 3072 | tf_op jit(solution)/shard_map/reshape | solution.py:298
  11.8 0.7 %pad_add_fusion.pos_ref = s32[2]{0:T(128)} fusion(s32[1]{0:T(128)} %constant.17.clone.1, s32[1]{0:T(128)} %bitcast.2), kind=kLoop, calls=%fused_computation | loop fusion | flops 2 | bytes 16 | tf_op jit(solution)/shard_map/stack | solution.py:300
  12.5 3.1 %prep.1 = (bf16[512,512]{1,0:T(8,128)(2,1)}, bf16[512,512]{1,0:T(8,128)(2,1)}, bf16[512,128]{1,0:T(8,128)(2,1)}, bf16[32,128]{1,0:T(8,128)(2,1)}, f32[16,128]{1,0:T(8,128)}) custom-call(s32[4,4]{1,0:T(4,128)} %tids_ref.1, s32[4,4]{1,0:T(4,128)} %offs_ref.1, s32[32]{0:T(128)} %owner_ref.1, s32[2]{0:T(128)} %pad_add_fusion.pos_ref, ...), custom_call_target="tpu_custom_call" | custom-call | flops 100000000 | bytes 3000000 | tf_op jit(solution)/shard_map/prep/pallas_call | solution.py:301
  15.6 0.0 collective-permute-done.m1
  15.6 0.0 copy-start.2
  15.6 0.0 collective-permute-done.1.m2
  15.6 0.0 copy-start.3
  15.6 0.5 %collective-permute-done.2.m3 = bf16[80,512]{1,0:T(8,128)(2,1)S(1)} collective-permute-done((bf16[80,512]{1,0:T(8,128)(2,1)}, bf16[80,512]{1,0:T(8,128)(2,1)S(1)}, u32[]{:S(2)}, u32[]{:S(2)}) %collective-permute-start.2) | collective-permute-done | bytes 81952 | tf_op jit(solution)/shard_map/ppermute | solution.py:265
  16.1 0.0 copy-start.4
  16.1 0.1 copy-done.2
  16.2 0.0 copy-done.3
  16.3 0.5 copy-done.4
  16.7 2.7 %first.1 = (f32[64,512]{1,0:T(8,128)}, f32[8,512]{1,0:T(8,128)}, bf16[8,48,128]{2,1,0:T(8,128)(2,1)}) custom-call(bf16[80,512]{1,0:T(8,128)(2,1)} %sums.1.m0, bf16[80,512]{1,0:T(8,128)(2,1)} %copy-done.2, bf16[80,512]{1,0:T(8,128)(2,1)} %copy-done.3, bf16[80,512]{1,0:T(8,128)(2,1)} %copy-done.4, bf16[512,512]{1,0:T(8,128)(2,1)} %get-tuple-element.12.hhi_ref, ...), custom_call_target="tpu_custom_call" | custom-call | tf_op jit(solution)/shard_map/first/pallas_call | solution.py:317
  19.4 4.9 %all-to-all-start = ((bf16[8,48,128]{2,1,0:T(8,128)(2,1)}), bf16[8,48,128]{2,1,0:T(8,128)(2,1)S(1)}, u32[]{:S(2)}, u32[]{:S(2)}) async-start(bf16[8,48,128]{2,1,0:T(8,128)(2,1)} %get-tuple-element.15), calls=%async_computation | async-start | bytes 196608 | tf_op jit(solution)/shard_map/all_to_all | solution.py:328
  24.3 6.3 %all-to-all-done.all_ref = bf16[8,48,128]{2,1,0:T(8,128)(2,1)S(1)} async-done(((bf16[8,48,128]{2,1,0:T(8,128)(2,1)}), bf16[8,48,128]{2,1,0:T(8,128)(2,1)S(1)}, u32[]{:S(2)}, u32[]{:S(2)}) %all-to-all-start) | async-done | bytes 98336 | tf_op jit(solution)/shard_map/all_to_all | solution.py:328
  30.6 0.0 copy-start
  30.6 0.6 %copy-done = bf16[8,48,128]{2,1,0:T(8,128)(2,1)} copy-done((bf16[8,48,128]{2,1,0:T(8,128)(2,1)}, bf16[8,48,128]{2,1,0:T(8,128)(2,1)S(1)}, u32[]{:S(2)}) %copy-start) | copy-done | bytes 98328
  31.3 2.8 %second.1 = (f32[8,512]{1,0:T(8,128)}, bf16[8,16,128]{2,1,0:T(8,128)(2,1)}) custom-call(bf16[8,48,128]{2,1,0:T(8,128)(2,1)} %copy-done, f32[16,128]{1,0:T(8,128)} %get-tuple-element.16.own_ref, f32[8,512]{1,0:T(8,128)} %get-tuple-element.17.vec_ref, bf16[512,512]{1,0:T(8,128)(2,1)} %get-tuple-element.12.hhi_ref, bf16[512,512]{1,0:T(8,128)(2,1)} %get-tuple-element.13.hlo_ref, ...), custom_call_target="tpu_custom_call" | custom-call | tf_op jit(solution)/shard_map/second/pallas_call | solution.py:330
  34.1 3.3 %all-to-all-start.1 = ((bf16[8,16,128]{2,1,0:T(8,128)(2,1)}), bf16[8,16,128]{2,1,0:T(8,128)(2,1)S(1)}, u32[]{:S(2)}, u32[]{:S(2)}) async-start(bf16[8,16,128]{2,1,0:T(8,128)(2,1)} %get-tuple-element.18), calls=%async_computation.1 | async-start | bytes 65536 | tf_op jit(solution)/shard_map/all_to_all | solution.py:337
  37.5 4.8 %clean.1 = bf16[512,512]{1,0:T(8,128)(2,1)} custom-call(f32[512,512]{1,0:T(8,128)} %ts_ref.3, s32[512,512]{1,0:T(8,128)} %flag_ref.3, f32[1,512]{1,0:T(1,128)} %bitcast.4, bf16[512,128]{1,0:T(8,128)(2,1)} %get-tuple-element.19.v3_ref, f32[64,512]{1,0:T(8,128)} %get-tuple-element.20.bq_ref, f32[8,512]{1,0:T(8,128)} %get-tuple-element.21.sig_ref, ...), custom_call_target="tpu_custom_call" | custom-call | flops 1000000000 | bytes 4000000 | tf_op jit(solution)/shard_map/clean/pallas_call | solution.py:339
  42.3 0.9 %all-to-all-done.1.all2_ref = bf16[8,16,128]{2,1,0:T(8,128)(2,1)S(1)} async-done(((bf16[8,16,128]{2,1,0:T(8,128)(2,1)}), bf16[8,16,128]{2,1,0:T(8,128)(2,1)S(1)}, u32[]{:S(2)}, u32[]{:S(2)}) %all-to-all-start.1) | async-done | bytes 32800 | tf_op jit(solution)/shard_map/all_to_all | solution.py:337
  43.1 0.0 copy-start.1
  43.1 0.6 %copy-done.1 = bf16[8,16,128]{2,1,0:T(8,128)(2,1)} copy-done((bf16[8,16,128]{2,1,0:T(8,128)(2,1)}, bf16[8,16,128]{2,1,0:T(8,128)(2,1)S(1)}, u32[]{:S(2)}) %copy-start.1) | copy-done | bytes 32792
  43.7 1.7 %tile.1 = f32[1,128,128]{2,1,0:T(8,128)} custom-call(s32[1]{0:T(128)} %bitcast.first_ref, bf16[8,48,128]{2,1,0:T(8,128)(2,1)} %copy-done, bf16[8,16,128]{2,1,0:T(8,128)(2,1)} %copy-done.1, f32[8,512]{1,0:T(8,128)} %get-tuple-element.17.vec_ref), custom_call_target="tpu_custom_call" | custom-call | tf_op jit(solution)/shard_map/tile/pallas_call | solution.py:359
  (1 shorter events, 0.0 us)
Async XLA Ops:
  6.1 9.5 %collective-permute-start = (bf16[80,512]{1,0:T(8,128)(2,1)}, bf16[80,512]{1,0:T(8,128)(2,1)S(1)}, u32[]{:S(2)}, u32[]{:S(2)}) collective-permute-start(bf16[80,512]{1,0:T(8,128)(2,1)} %sums.1.m0), channel_id=1, source_target_pairs={{0,8},{8,0},{16,24},{24,16},{1,9},{9,1},{17,25},{25,17},{2,10},{10... | collective-permute-start | bytes 245768 | tf_op jit(solution)/shard_map/ppermute | solution.py:265
  9.0 6.6 %collective-permute-start.1 = (bf16[80,512]{1,0:T(8,128)(2,1)}, bf16[80,512]{1,0:T(8,128)(2,1)S(1)}, u32[]{:S(2)}, u32[]{:S(2)}) collective-permute-start(bf16[80,512]{1,0:T(8,128)(2,1)} %sums.1.m0), channel_id=1, source_target_pairs={{0,16},{8,24},{16,0},{24,8},{1,17},{9,25},{17,1},{25,9},{2,18},{10... | collective-permute-start | bytes 245768 | tf_op jit(solution)/shard_map/ppermute | solution.py:265
  10.6 5.6 %collective-permute-start.2 = (bf16[80,512]{1,0:T(8,128)(2,1)}, bf16[80,512]{1,0:T(8,128)(2,1)S(1)}, u32[]{:S(2)}, u32[]{:S(2)}) collective-permute-start(bf16[80,512]{1,0:T(8,128)(2,1)} %sums.1.m0), channel_id=1, source_target_pairs={{0,24},{8,16},{16,8},{24,0},{1,25},{9,17},{17,9},{25,1},{2,26},{10... | collective-permute-start | bytes 245768 | tf_op jit(solution)/shard_map/ppermute | solution.py:265
  10.6 0.7 %copy-start.5 = (f32[257]{0:T(512)S(1)}, f32[257]{0:T(512)}, u32[]{:S(2)}) copy-start(f32[257]{0:T(512)} %param.18) | copy-start | bytes 3088
  15.6 0.6 %copy-start.2 = (bf16[80,512]{1,0:T(8,128)(2,1)}, bf16[80,512]{1,0:T(8,128)(2,1)S(1)}, u32[]{:S(2)}) copy-start(bf16[80,512]{1,0:T(8,128)(2,1)S(1)} %collective-permute-done.m1) | copy-start | bytes 245764
  15.6 0.6 %copy-start.3 = (bf16[80,512]{1,0:T(8,128)(2,1)}, bf16[80,512]{1,0:T(8,128)(2,1)S(1)}, u32[]{:S(2)}) copy-start(bf16[80,512]{1,0:T(8,128)(2,1)S(1)} %collective-permute-done.1.m2) | copy-start | bytes 245764
  16.1 0.6 %copy-start.4 = (bf16[80,512]{1,0:T(8,128)(2,1)}, bf16[80,512]{1,0:T(8,128)(2,1)S(1)}, u32[]{:S(2)}) copy-start(bf16[80,512]{1,0:T(8,128)(2,1)S(1)} %collective-permute-done.2.m3) | copy-start | bytes 245764
  19.4 11.2 %all-to-all-start = ((bf16[8,48,128]{2,1,0:T(8,128)(2,1)}), bf16[8,48,128]{2,1,0:T(8,128)(2,1)S(1)}, u32[]{:S(2)}, u32[]{:S(2)}) async-start(bf16[8,48,128]{2,1,0:T(8,128)(2,1)} %get-tuple-element.15), calls=%async_computation | async-start | bytes 196608 | tf_op jit(solution)/shard_map/all_to_all | solution.py:328
  30.6 0.6 %copy-start = (bf16[8,48,128]{2,1,0:T(8,128)(2,1)}, bf16[8,48,128]{2,1,0:T(8,128)(2,1)S(1)}, u32[]{:S(2)}) copy-start(bf16[8,48,128]{2,1,0:T(8,128)(2,1)S(1)} %all-to-all-done.all_ref) | copy-start | bytes 294916
  34.1 9.0 %all-to-all-start.1 = ((bf16[8,16,128]{2,1,0:T(8,128)(2,1)}), bf16[8,16,128]{2,1,0:T(8,128)(2,1)S(1)}, u32[]{:S(2)}, u32[]{:S(2)}) async-start(bf16[8,16,128]{2,1,0:T(8,128)(2,1)} %get-tuple-element.18), calls=%async_computation.1 | async-start | bytes 65536 | tf_op jit(solution)/shard_map/all_to_all | solution.py:337
  43.1 0.6 %copy-start.1 = (bf16[8,16,128]{2,1,0:T(8,128)(2,1)}, bf16[8,16,128]{2,1,0:T(8,128)(2,1)S(1)}, u32[]{:S(2)}) copy-start(bf16[8,16,128]{2,1,0:T(8,128)(2,1)S(1)} %all-to-all-done.1.all2_ref) | copy-start | bytes 98308

commit v2 on v1

v2 whole, which is shorter than its diff:
```python
import functools
import math

import jax
import jax.numpy as jnp
import numpy as np
from jax import lax
from jax.experimental import pallas as pl
from jax.experimental.pallas import tpu as pltpu
from jax.sharding import PartitionSpec as P

F32 = jnp.float32
BF16 = jnp.bfloat16
LANES = 128
BASE = 128
EXT = 16
NN = (((1,), (0,)), ((), ()))
NT = (((1,), (1,)), ((), ()))


def mm(a, b, dims=NN):
    return lax.dot_general(a, b, dims, preferred_element_type=F32)


def split(x):
    hi = x.astype(BF16)
    return hi, (x - hi.astype(F32)).astype(BF16)


def iota(shape, axis):
    return lax.broadcasted_iota(jnp.int32, shape, axis)


def cosine_table(flen, rows):
    f = np.arange(rows)[:, None]
    n = np.arange(flen)[None, :]
    scale = np.where((f == 0) | (f == flen // 2), 1.0, 2.0) / flen
    scale = np.where(f <= flen // 2, scale, 0.0)
    return (scale * np.cos(2.0 * math.pi * ((f * n) % flen) / flen)).astype(np.float32)


def sums_kernel(modes, parts, ts_hbm, flag_hbm, v_hbm, g_hbm, msg_ref, ts_ref, keep_ref, v_ref, g_ref, flag_ref, sem,
                small_sem):
    dets, samples = ts_ref.shape
    chunk = dets // parts
    smalls = [
        pltpu.make_async_copy(v_hbm, v_ref, small_sem.at[0]),
        pltpu.make_async_copy(g_hbm, g_ref, small_sem.at[1]),
    ]
    for copy in smalls:
        copy.start()
    pairs = []
    for i in range(parts):
        rows = pl.ds(i * chunk, chunk)
        pairs.append(
            (
                pltpu.make_async_copy(ts_hbm.at[rows], ts_ref.at[rows], sem.at[0, i]),
                pltpu.make_async_copy(flag_hbm.at[rows], flag_ref.at[rows], sem.at[1, i]),
            )
        )
    for pair in pairs:
        for copy in pair:
            copy.start()
    for copy in smalls:
        copy.wait()
    vt = v_ref[...]
    g = g_ref[...]
    row = iota((EXT, dets), 0)
    left1 = jnp.concatenate([vt, jnp.where(row < 2, g, 0.0)], axis=0)
    left2 = jnp.concatenate([vt * g, jnp.where((row >= 2) & (row < 4), g * g, 0.0)], axis=0)
    hi1, lo1 = split(left1)
    hi2, lo2 = split(left2)
    left1 = jnp.concatenate([hi1, lo1], axis=0)
    left2 = jnp.concatenate([hi2, lo2], axis=0)
    u = jnp.sum(vt * g, axis=1, keepdims=True)
    square = jnp.sum(g * g, axis=1, keepdims=True)
    lane = iota((modes, samples), 1)
    u = jnp.sum(jnp.where(lane == iota((modes, samples), 0), u, 0.0), axis=0, keepdims=True)
    u = jnp.where(iota((1, samples), 1) == modes, square, u)
    n = modes + EXT
    acc1 = jnp.zeros((n, samples), F32)
    acc2 = jnp.zeros((n, samples), F32)
    for i in range(parts):
        for copy in pairs[i]:
            copy.wait()
        at = slice(i * chunk, (i + 1) * chunk)
        keep = (1 - flag_ref[at]).astype(F32)
        keep_ref[at] = keep.astype(BF16)
        x_hi, x_lo = split(ts_ref[at] * keep)
        both = mm(left1[:, at], x_hi)
        acc1 = acc1 + (both[:n] + both[n:]) + mm(hi1[:, at], x_lo)
        both = mm(left2[:, at], keep.astype(BF16))
        acc2 = acc2 + (both[:n] + both[n:])
    msg_ref[0:modes] = acc1[0:modes].astype(BF16)
    msg_ref[modes : 2 * modes] = acc2[0:modes].astype(BF16)
    row = iota((EXT, samples), 0)
    ext = acc1[modes:] + acc2[modes:] + jnp.where((row >= 4) & (row < 6), u, 0.0)
    hi = ext.astype(BF16).astype(F32)
    msg_ref[2 * modes :] = jnp.where(row % 2 == 1, ext - hi, hi).astype(BF16)


def prep_kernel(seg, kblk, lane_blocks, digits, tids_ref, offs_ref, owner_ref, gain_ref, cos_ref, point_ref, v_ref,
                h2_ref, pn_ref, pt_ref, v3_ref, geo_ref, own_ref, wide_ref):
    flen = cos_ref.shape[1]
    wide_ref[...] = jnp.zeros_like(wide_ref)
    wide_ref[0:1, 0 : gain_ref.shape[1]] = gain_ref[...]
    h = lax.dot_general(wide_ref[...], cos_ref[...], NN, precision=lax.Precision.HIGHEST, preferred_element_type=F32)
    base = jnp.broadcast_to(h[0:1], (LANES, flen))
    base = pltpu.roll(base, 0, 1, stride=1, stride_axis=0)
    base_hi, base_lo = split(base)
    blocks = flen // LANES
    for a in range(blocks):
        for b in range(blocks):
            c = (b - a) % blocks
            to = slice(b * LANES, (b + 1) * LANES)
            h2_ref[a * LANES : (a + 1) * LANES, to] = base_hi[:, c * LANES : (c + 1) * LANES]
            h2_ref[flen + a * LANES : flen + (a + 1) * LANES, to] = base_lo[:, c * LANES : (c + 1) * LANES]
    vt = v_ref[...]
    vhi = vt.astype(BF16).astype(F32)
    pad = jnp.zeros((LANES - 3 * vt.shape[0], vt.shape[1]), F32)
    v3_ref[...] = jnp.concatenate([vhi, vhi, vt - vhi, pad], axis=0).T.astype(BF16)
    listed = seg * kblk
    row16 = iota((listed, LANES), 0)
    first = lax.axis_index("tm") * listed
    squares = jnp.zeros((listed, LANES), F32)
    ext = geo_ref.shape[0] - listed
    row_x = iota((ext, LANES), 0)
    lane_x = iota((ext, LANES), 1)
    ids = jnp.zeros((ext, LANES), F32)
    own = jnp.zeros((listed, LANES), F32)
    for k in range(kblk):
        for s in range(seg):
            j = k * seg + s
            p = point_ref[s, k]
            span, tile = p.shape
            pn_ref[s * span : (s + 1) * span, k * tile : (k + 1) * tile] = p
            pt_ref[k * tile : (k + 1) * tile, s * span : (s + 1) * span] = p.T
            p = p.astype(F32)
            squares = jnp.where(row16 == j, jnp.sum(p * p, axis=0, keepdims=True), squares)
            target = owner_ref[tids_ref[s, k]] * LANES + offs_ref[s, k]
            own = jnp.where(row16 == j, target.astype(F32), own)
            place = first + j
            digit = target
            for d in range(digits):
                at = (row_x == d * lane_blocks + place // LANES) & (lane_x == place % LANES)
                ids = jnp.where(at, (digit % BASE).astype(F32), ids)
                digit = digit // BASE
    geo_ref[0:listed] = squares.astype(BF16)
    geo_ref[listed:] = ids.astype(BF16)
    own_ref[...] = own


def filtered(b, h2_ref):
    flen = b.shape[1]
    hi, lo = split(b)
    row = iota((EXT, flen), 0)
    left = jnp.where(row == 0, hi.astype(F32), jnp.where(row == 1, lo.astype(F32), 0.0)).astype(BF16)
    z = mm(left, h2_ref[0:flen]) + mm(left, h2_ref[flen:])
    return z[0:1] + z[1:2]


def project(z, pn_ref, seg, kblk):
    samples = z.shape[1]
    listed = seg * kblk
    hi, lo = split(z)
    row = iota((2 * listed, samples), 0)
    lane = iota((2 * listed, samples), 1)
    wide = jnp.where(row < listed, hi.astype(F32), lo.astype(F32))
    wide = jnp.where(lane // (samples // seg) == row % seg, wide, 0.0).astype(BF16)
    out = mm(wide, pn_ref[...])
    out = out[:listed] + out[listed:]
    row = iota((listed, LANES), 0)
    proj = out[:, 0:LANES]
    for k in range(1, kblk):
        proj = jnp.where(row // seg == k, out[:, k * LANES : (k + 1) * LANES], proj)
    return proj


def first_kernel(modes, seg, kblk, m0, m1, m2, m3, h2_ref, pn_ref, geo_ref,
                 bq_ref, vec_ref, send_ref):
    tot = m0[...].astype(F32) + m1[...].astype(F32) + m2[...].astype(F32) + m3[...].astype(F32)
    bq_ref[...] = tot[0 : 2 * modes]
    ext = tot[2 * modes :]
    u_row = ext[4:5, 0:LANES] + ext[5:6, 0:LANES]
    u_col = jnp.sum(jnp.where(iota((modes, LANES), 0) == iota((modes, LANES), 1), u_row, 0.0), axis=1, keepdims=True)
    square = jnp.sum(jnp.where(iota((1, LANES), 1) == modes, u_row, 0.0), axis=1, keepdims=True)
    b1 = ext[0:1] + ext[1:2] - jnp.sum(u_col * tot[0:modes], axis=0, keepdims=True)
    b2 = ext[2:3] + ext[3:4] - jnp.sum(u_col * tot[modes : 2 * modes], axis=0, keepdims=True)
    row = iota((8, b1.shape[1]), 0)
    vec_ref[...] = jnp.where(row == 0, b1, jnp.where(row == 1, b2, jnp.where(row == 2, square, 0.0)))
    z = filtered(b1, h2_ref)
    proj = project(z, pn_ref, seg, kblk).astype(BF16)
    geo = geo_ref[...]
    listed = seg * kblk
    for t in range(send_ref.shape[0]):
        send_ref[t, 0:listed] = proj
        send_ref[t, listed:] = geo


def lane_ids(all_ref, listed, blocks, digits, b):
    ids = jnp.sum(all_ref[:, 2 * listed :].astype(F32), axis=0)
    out = ids[b : b + 1]
    for d in range(1, digits):
        out = out + float(BASE**d) * ids[d * blocks + b : d * blocks + b + 1]
    return out


def second_kernel(seg, kblk, digits, all_ref, own_ref, vec_ref, h2_ref, pn_ref, pt_ref, sig_ref, send_ref):
    listed = seg * kblk
    blocks = all_ref.shape[0] * listed // LANES
    samples = vec_ref.shape[1]
    per = LANES // listed
    own = own_ref[...]
    psum = jnp.zeros((listed, LANES), F32)
    wsum = jnp.zeros((listed, LANES), F32)
    for b in range(blocks):
        same = (own == lane_ids(all_ref, listed, blocks, digits, b)).astype(F32).astype(BF16)
        part = all_ref[b * per : (b + 1) * per]
        psum = psum + mm(same, part[:, 0:listed].reshape(LANES, LANES))
        wsum = wsum + mm(same, part[:, listed : 2 * listed].reshape(LANES, LANES))
    square = vec_ref[2:3, 0:LANES]
    fetched = (psum / (1.0 + square * wsum)).astype(BF16)
    row = iota((listed, LANES), 0)
    wide = [jnp.where(row // seg == k, fetched.astype(F32), 0.0).astype(BF16) for k in range(kblk)]
    spread = mm(jnp.concatenate(wide, axis=1), pt_ref[...])
    row = iota((listed, samples), 0)
    lane = iota((listed, samples), 1)
    sig = jnp.sum(jnp.where(lane // (samples // seg) == row % seg, spread, 0.0), axis=0, keepdims=True)
    sig_ref[...] = jnp.broadcast_to(sig, sig_ref.shape)
    z = filtered(vec_ref[0:1] - vec_ref[1:2] * sig, h2_ref)
    proj = project(z, pn_ref, seg, kblk).astype(BF16)
    for t in range(send_ref.shape[0]):
        send_ref[t] = proj


def clean_kernel(seg, kblk, digits, modes, parts, ts_ref, keep_ref, g_ref, v3_ref, bq_ref, sig_ref, h2_ref,
                 all_ref, vec_ref, out_hbm, base_ref, scale_ref, same_ref, out_ref, sem):
    dets, samples = ts_ref.shape
    chunk = dets // parts
    sig = sig_ref[0:1]
    q_hi, q_lo = split(bq_ref[0:modes] - bq_ref[modes : 2 * modes] * sig)
    pad = jnp.zeros((LANES - 3 * modes, samples), BF16)
    q3 = jnp.concatenate([q_hi, q_lo, q_hi, pad], axis=0)
    eye = iota((chunk, chunk), 0) == iota((chunk, chunk), 1)
    copies = []
    for i in range(parts):
        at = slice(i * chunk, (i + 1) * chunk)
        g_col = jnp.sum(jnp.where(eye, g_ref[:, at], 0.0), axis=1, keepdims=True)
        rest = (ts_ref[at] - g_col * sig) * keep_ref[at].astype(F32) - mm(v3_ref[at], q3)
        rest = rest.astype(BF16)
        out_ref[at] = (mm(rest, h2_ref[0:samples]) + mm(rest, h2_ref[samples:])).astype(BF16)
        rows = pl.ds(i * chunk, chunk)
        copy = pltpu.make_async_copy(out_ref.at[rows], out_hbm.at[rows], sem.at[i])
        copy.start()
        copies.append(copy)
    listed = seg * kblk
    blocks = all_ref.shape[0] * listed // LANES
    per = LANES // listed
    psum = jnp.zeros((LANES, LANES), F32)
    wsum = jnp.zeros((LANES, LANES), F32)
    first = (lax.axis_index("det") * lax.axis_size("tm") + lax.axis_index("tm")) * LANES
    mine = (iota((LANES, LANES), 0) + first).astype(F32)
    for b in range(blocks):
        same = (mine == lane_ids(all_ref, listed, blocks, digits, b)).astype(F32).astype(BF16)
        same_ref[b] = same
        part = all_ref[b * per : (b + 1) * per]
        psum = psum + mm(same, part[:, 0:listed].reshape(LANES, LANES))
        wsum = wsum + mm(same, part[:, listed : 2 * listed].reshape(LANES, LANES))
    wsum = 1.0 + vec_ref[2:3, 0:LANES] * wsum
    scale = jnp.sqrt(wsum) / wsum
    scale_ref[...] = scale
    base_ref[...] = psum * scale
    for copy in copies:
        copy.wait()


def tile_kernel(all2_ref, base_ref, scale_ref, same_ref, out_ref):
    per = LANES // all2_ref.shape[1]
    psum = jnp.zeros((LANES, LANES), F32)
    for b in range(same_ref.shape[0]):
        psum = psum + mm(same_ref[b], all2_ref[b * per : (b + 1) * per].reshape(LANES, LANES))
    out_ref[0] = base_ref[...] + psum * scale_ref[...]


VM = pl.BlockSpec(memory_space=pltpu.VMEM)
HB = pl.BlockSpec(memory_space=pltpu.HBM)
SM = pl.BlockSpec(memory_space=pltpu.SMEM)
GRANT = pltpu.CompilerParams(vmem_limit_bytes=12 * 2**20)


def shape(dims, dtype=F32):
    return jax.ShapeDtypeStruct(dims, dtype)


def others(x, axis, n):
    if n & (n - 1) == 0:
        pairs = [[(i, i ^ k) for i in range(n)] for k in range(1, n)]
    else:
        pairs = [[(i, (i + k) % n) for i in range(n)] for k in range(1, n)]
    return [lax.ppermute(x, axis, p) for p in pairs]


def shards(n_det, n_tm, timestream, sample_flags, pointing, tile_ids, block_offsets, tile_owner, det_gains,
           mode_vectors, filter_gain):
    dets, samples = timestream.shape
    modes = mode_vectors.shape[1]
    seg, kblk = tile_ids.shape
    listed = seg * kblk
    parts = dets // LANES
    lane_blocks = n_tm * listed // LANES
    digits = -(-int(tile_owner.shape[0] * LANES - 1).bit_length() // 7)
    id_rows = -(-digits * lane_blocks // 8) * 8
    inputs = (timestream, sample_flags, mode_vectors.T, det_gains.reshape(1, dets))
    msg, ts, keep, vt, g = pl.pallas_call(
        functools.partial(sums_kernel, modes, parts),
        in_specs=[HB] * 4,
        out_specs=[VM] * 5,
        out_shape=[
            shape((2 * modes + EXT, samples), BF16),
            shape((dets, samples)),
            shape((dets, samples), BF16),
            shape((modes, dets)),
            shape((1, dets)),
        ],
        scratch_shapes=[
            pltpu.VMEM((dets, samples), jnp.int32),
            pltpu.SemaphoreType.DMA((2, parts)),
            pltpu.SemaphoreType.DMA((2,)),
        ],
        compiler_params=GRANT,
        name="sums",
    )(*(pltpu.with_memory_space_constraint(x, pltpu.HBM) for x in inputs))
    parts_of_all = [msg] + others(msg, "det", n_det)

    rows = -(-filter_gain.shape[0] // LANES) * LANES
    h2, pn, pt, v3, geo, own = pl.pallas_call(
        functools.partial(prep_kernel, seg, kblk, lane_blocks, digits),
        in_specs=[SM, SM, SM, VM, VM, VM, VM],
        out_specs=[VM] * 6,
        out_shape=[
            shape((2 * samples, samples), BF16),
            shape((samples, kblk * LANES), BF16),
            shape((kblk * LANES, samples), BF16),
            shape((dets, LANES), BF16),
            shape((listed + id_rows, LANES), BF16),
            shape((listed, LANES)),
        ],
        scratch_shapes=[pltpu.VMEM((8, rows), F32)],
        cost_estimate=pl.CostEstimate(flops=10**8, bytes_accessed=3 * 10**6, transcendentals=0),
        compiler_params=GRANT,
        name="prep",
    )(tile_ids, block_offsets, tile_owner, filter_gain.reshape(1, -1), jnp.asarray(cosine_table(samples, rows)),
      pointing, vt)

    bq, vec, send = pl.pallas_call(
        functools.partial(first_kernel, modes, seg, kblk),
        in_specs=[VM] * 7,
        out_specs=[VM] * 3,
        out_shape=[
            shape((2 * modes, samples)),
            shape((8, samples)),
            shape((n_tm, 2 * listed + id_rows, LANES), BF16),
        ],
        compiler_params=GRANT,
        name="first",
    )(*parts_of_all, h2, pn, geo)
    everyone = lax.all_to_all(send, "tm", 0, 0)

    sig, send = pl.pallas_call(
        functools.partial(second_kernel, seg, kblk, digits),
        in_specs=[VM] * 6,
        out_specs=[VM] * 2,
        out_shape=[shape((8, samples)), shape((n_tm, listed, LANES), BF16)],
        compiler_params=GRANT,
        name="second",
    )(everyone, own, vec, h2, pn, pt)
    everyone2 = lax.all_to_all(send, "tm", 0, 0)

    cleaned, base, scale, same = pl.pallas_call(
        functools.partial(clean_kernel, seg, kblk, digits, modes, parts),
        in_specs=[VM] * 9,
        out_specs=[HB, VM, VM, VM],
        out_shape=[
            shape((dets, samples), BF16),
            shape((LANES, LANES)),
            shape((LANES, LANES)),
            shape((lane_blocks, LANES, LANES), BF16),
        ],
        scratch_shapes=[pltpu.VMEM((dets, samples), BF16), pltpu.SemaphoreType.DMA((parts,))],
        cost_estimate=pl.CostEstimate(flops=10**9, bytes_accessed=4 * 10**6, transcendentals=0),
        compiler_params=GRANT,
        name="clean",
    )(ts, keep, g, v3, bq, sig, h2, everyone, vec)

    tile = pl.pallas_call(
        tile_kernel,
        in_specs=[VM] * 4,
        out_specs=VM,
        out_shape=shape((1, LANES, LANES)),
        compiler_params=GRANT,
        name="tile",
    )(everyone2, base, scale, same)
    return tile, cleaned


def solution(mesh):
    return jax.shard_map(
        functools.partial(shards, mesh.shape["det"], mesh.shape["tm"]),
        mesh=mesh,
        in_specs=(
            P("det", "tm"),
            P("det", "tm"),
            P("tm", None, None, None),
            P("tm", None),
            P("tm", None),
            P(),
            P("det"),
            P("det", None),
            P(),
        ),
        out_specs=(P(("det", "tm"), None, None), P("det", "tm")),
        check_vma=False,
    )
```

time: 46 us -> 34.5 us (0.75)
  blocking collectives: 0 us -> 10.8 us
  Pallas kernels: 18.9 us -> 8.19 us
  starting transfers between devices: 12.8 us -> 7.97 us
  local copies, waits for them, and re-layouts: 4.79 us -> 0.65 us
  waiting for transfers between devices: 7.64 us -> 5.96 us
  other arithmetic: 0.65 us -> 0 us
    all_to_all x0 -> x1, blocking collectives: none -> 10.8 us  [shards(): everyone = lax.all_to_all(send, 'tm', 0, 0)]
    pallas_call x5, Pallas kernels: 16.3 us -> 7.7 us  [the longest x1 2.28 us: shards(): pl.pallas_call(functools.partial(sums_kernel, modes, parts), in_specs=[HB...]
    all_to_all x1 -> x0, waiting for transfers between devices: 6.31 us -> none  [shards(): everyone = lax.all_to_all(send, 'tm', 0, 0)]
    all_to_all x1 -> x0, starting transfers between devices: 4.93 us -> none  [shards(): everyone = lax.all_to_all(send, 'tm', 0, 0)]
    unnamed x13 -> x12, local copies, waits for them, and re-layouts: 4.21 us -> 0.65 us
    all_to_all x1, waiting for transfers between devices: 0.87 us -> 3.69 us  [shards(): everyone2 = lax.all_to_all(send, 'tm', 0, 0)]
    pallas_call x1, Pallas kernels: 2.66 us -> 0.48 us  [shards(): pl.pallas_call(functools.partial(first_kernel, modes, seg, kblk), in_spec...]
    ppermute x3, waiting for transfers between devices: 0.46 us -> 2.26 us  [others(): return [lax.ppermute(x, axis, p) for p in pairs]]
  transfers between devices with their start and end apart: 5 -> 4, of which waited for: 3 -> 3; matrix products, arithmetic and copies ran while one was open for 3% -> 0% of each run, Pallas kernels for 17% -> 10%
where the time goes in v2:
time: 34.5 us; the launch traced here: 34.3 us
  blocking collectives  10.8 us (31%)
  Pallas kernels  8.19 us (24%)
  starting transfers between devices  7.97 us (23%)
  waiting for transfers between devices  5.96 us (17%)
  between operations  0.74 us (2%)
  local copies, waits for them, and re-layouts  0.65 us (2%)
    all_to_all x1, blocking collectives, shards(): everyone = lax.all_to_all(send, 'tm', 0, 0)  10.8 us
    ppermute x3, starting transfers between devices, others(): return [lax.ppermute(x, axis, p) for p in pairs]  4.63 us
    all_to_all x1, waiting for transfers between devices, shards(): everyone2 = lax.all_to_all(send, 'tm', 0, 0)  3.69 us
    all_to_all x1, starting transfers between devices, shards(): everyone2 = lax.all_to_all(send, 'tm', 0, 0)  3.34 us
    pallas_call x1, Pallas kernels, shards(): pl.pallas_call(functools.partial(sums_kernel, modes, parts), in_specs=[HB...  2.28 us
    ppermute x3, waiting for transfers between devices, others(): return [lax.ppermute(x, axis, p) for p in pairs]  2.26 us
    pallas_call x1, Pallas kernels, shards(): pl.pallas_call(functools.partial(clean_kernel, seg, kblk, digits, modes,...  1.97 us
    pallas_call x1, Pallas kernels, shards(): pl.pallas_call(functools.partial(prep_kernel, seg, kblk, lane_blocks, dig...  1.36 us
  transfers between devices with their start and end apart: 4, of which 3 were waited for; matrix products, arithmetic and copies ran while one was open for 0% of the time, Pallas kernels for 10%

profile of v2, /device:TPU:0, one launch (start us, length us, event | category | flops | bytes accessed | tf_op | source)
XLA Modules:
  0.0 34.3 jit_solution(18378790153536349782)
XLA Ops:
  0.6 0.0 copy-start.5
  0.6 0.0 copy-start
  0.7 0.0 copy-start.1
  0.7 2.3 %sums.1 = (bf16[80,512]{1,0:T(8,128)(2,1)S(1)}, f32[512,512]{1,0:T(8,128)S(1)}, bf16[512,512]{1,0:T(8,128)(2,1)S(1)}, f32[32,512]{1,0:T(8,128)S(1)}, f32[1,512]{1,0:T(1,128)S(1)}) custom-call(f32[512,512]{1,0:T(8,128)} %ts_hbm.1, s32[512,512]{1,0:T(8,128)} %flag_hbm.1, f32[32,512]{1,0:T(8,128)} %bitcast.2, f32[1,512]{1,0:T(1,128)} %bitcast.3), custom_call_target="tpu_custom_call" | custom-call | tf_op jit(solution)/shard_map/sums/pallas_call | solution.py:314
  3.0 0.0 copy-start.2
  3.0 0.0 copy-start.3
  3.0 4.0 %collective-permute-start.2 = (bf16[80,512]{1,0:T(8,128)(2,1)S(1)}, bf16[80,512]{1,0:T(8,128)(2,1)S(1)}, u32[]{:S(2)}, u32[]{:S(2)}) collective-permute-start(bf16[80,512]{1,0:T(8,128)(2,1)S(1)} %get-tuple-element.22.m0), channel_id=1, source_target_pairs={{0,24},{8,16},{16,8},{24,0},{1,25},{9,17},{17,9},{25,1},{2,26},{10... | collective-permute-start | bytes 245768 | tf_op jit(solution)/shard_map/ppermute | solution.py:300
  7.0 0.5 %collective-permute-start.1 = (bf16[80,512]{1,0:T(8,128)(2,1)S(1)}, bf16[80,512]{1,0:T(8,128)(2,1)S(1)}, u32[]{:S(2)}, u32[]{:S(2)}) collective-permute-start(bf16[80,512]{1,0:T(8,128)(2,1)S(1)} %get-tuple-element.22.m0), channel_id=1, source_target_pairs={{0,16},{8,24},{16,0},{24,8},{1,17},{9,25},{17,1},{25,9},{2,18},{10... | collective-permute-start | bytes 245768 | tf_op jit(solution)/shard_map/ppermute | solution.py:300
  7.5 0.1 collective-permute-start
  7.6 0.0 copy-done.5
  7.6 0.0 copy-start.4
  7.6 0.0 copy-done
  7.6 0.0 copy-done.1
  7.6 0.0 copy-done.2
  7.6 0.0 copy-done.3
  7.6 0.6 %copy-done.4 = s32[32]{0:T(128)S(1)} copy-done((s32[32]{0:T(128)S(1)}, s32[32]{0:T(128)}, u32[]{:S(2)}) %copy-start.4) | copy-done | bytes 152
  8.3 1.4 %prep.1 = (bf16[1024,512]{1,0:T(8,128)(2,1)S(1)}, bf16[512,512]{1,0:T(8,128)(2,1)S(1)}, bf16[512,512]{1,0:T(8,128)(2,1)S(1)}, bf16[512,128]{1,0:T(8,128)(2,1)S(1...) custom-call(s32[4,4]{1,0:T(4,128)S(1)} %copy-done.2, s32[4,4]{1,0:T(4,128)S(1)} %copy-done.3, s32[32]{0:T(128)S(1)} %copy-done.4, ...), custom_call_target="tpu_custom_call" | custom-call | flops 100000000 | bytes 3000000 | tf_op jit(solution)/shard_map/prep/pallas_call | solution.py:336
  9.6 0.0 collective-permute-done.2.m3
  9.6 1.8 %collective-permute-done.1.m2 = bf16[80,512]{1,0:T(8,128)(2,1)S(1)} collective-permute-done((bf16[80,512]{1,0:T(8,128)(2,1)S(1)}, bf16[80,512]{1,0:T(8,128)(2,1)S(1)}, u32[]{:S(2)}, u32[]{:S(2)}) %collective-permute-start.1) | collective-permute-done | bytes 81952 | tf_op jit(solution)/shard_map/ppermute | solution.py:300
  11.4 0.5 %collective-permute-done.m1 = bf16[80,512]{1,0:T(8,128)(2,1)S(1)} collective-permute-done((bf16[80,512]{1,0:T(8,128)(2,1)S(1)}, bf16[80,512]{1,0:T(8,128)(2,1)S(1)}, u32[]{:S(2)}, u32[]{:S(2)}) %collective-permute-start) | collective-permute-done | bytes 81952 | tf_op jit(solution)/shard_map/ppermute | solution.py:300
  11.9 0.5 %first.1 = (f32[64,512]{1,0:T(8,128)S(1)}, f32[8,512]{1,0:T(8,128)S(1)}, bf16[8,40,128]{2,1,0:T(8,128)(2,1)S(1)}) custom-call(bf16[80,512]{1,0:T(8,128)(2,1)S(1)} %get-tuple-element.22.m0, bf16[80,512]{1,0:T(8,128)(2,1)S(1)} %collective-permute-done.m1, bf16[80,512]{1,0:T(8,128)(2,1)S(1)} %collective-permute-done.1.m2, ...), custom_call_target="tpu_custom_call" | custom-call | tf_op jit(solution)/shard_map/first/pallas_call | solution.py:355
  12.4 10.8 %all_to_all.10.all_ref = bf16[8,40,128]{2,1,0:T(8,128)(2,1)S(1)} all-to-all(bf16[8,40,128]{2,1,0:T(8,128)(2,1)S(1)} %get-tuple-element.27), channel_id=1, replica_groups=mesh['det'=4,'tm'=8] {'tm'}, dimensions={0} | all-to-all | bytes 163840 | tf_op jit(solution)/shard_map/all_to_all | solution.py:367
  23.2 1.3 %second.1 = (f32[8,512]{1,0:T(8,128)S(1)}, bf16[8,16,128]{2,1,0:T(8,128)(2,1)}) custom-call(bf16[8,40,128]{2,1,0:T(8,128)(2,1)S(1)} %all_to_all.10.all_ref, f32[16,128]{1,0:T(8,128)S(1)} %get-tuple-element.28.own_ref, f32[8,512]{1,0:T(8,128)S(1)} %get-tuple-element.29.vec_ref, bf16[1024,512]{1,0:T(8,128)(2,1)S(1)} %get-tuple-element.24.h2_ref, ...), custom_call_target="tpu_custom_call" | custom-call | tf_op jit(solution)/shard_map/second/pallas_call | solution.py:369
  24.5 3.3 %all-to-all-start.1 = ((bf16[8,16,128]{2,1,0:T(8,128)(2,1)}), bf16[8,16,128]{2,1,0:T(8,128)(2,1)S(1)}, u32[]{:S(2)}, u32[]{:S(2)}) async-start(bf16[8,16,128]{2,1,0:T(8,128)(2,1)} %get-tuple-element.31), calls=%async_computation.1 | async-start | bytes 65536 | tf_op jit(solution)/shard_map/all_to_all | solution.py:377
  27.8 2.0 %clean.1 = (bf16[512,512]{1,0:T(8,128)(2,1)}, f32[128,128]{1,0:T(8,128)S(1)}, f32[128,128]{1,0:T(8,128)S(1)}, bf16[1,128,128]{2,1,0:T(8,128)(2,1)S(1)}) custom-call(f32[512,512]{1,0:T(8,128)S(1)} %get-tuple-element.32.ts_ref, bf16[512,512]{1,0:T(8,128)(2,1)S(1)} %get-tuple-element.33.keep_ref, f32[1,512]{1,0:T(1,128)S(1)} %get-tuple-element.34.g_ref, ...), custom_call_target="tpu_custom_call" | custom-call | flops 1000000000 | bytes 4000000 | tf_op jit(solution)/shard_map/clean/pallas_call | solution.py:379
  29.8 3.7 %all-to-all-done.1.all2_ref = bf16[8,16,128]{2,1,0:T(8,128)(2,1)S(1)} async-done(((bf16[8,16,128]{2,1,0:T(8,128)(2,1)}), bf16[8,16,128]{2,1,0:T(8,128)(2,1)S(1)}, u32[]{:S(2)}, u32[]{:S(2)}) %all-to-all-start.1) | async-done | bytes 32800 | tf_op jit(solution)/shard_map/all_to_all | solution.py:377
  33.5 0.8 %tile.1 = f32[1,128,128]{2,1,0:T(8,128)} custom-call(bf16[8,16,128]{2,1,0:T(8,128)(2,1)S(1)} %all-to-all-done.1.all2_ref, f32[128,128]{1,0:T(8,128)S(1)} %get-tuple-element.38.base_ref, f32[128,128]{1,0:T(8,128)S(1)} %get-tuple-element.39.scale_ref, bf16[1,128,128]{2,1,0:T(8,128)(2,1)S(1)} %get-tuple-element.40.same_ref), custom_call_target="tpu_custom_call" | custom-call | tf_op jit(solution)/shard_map/tile/pallas_call | solution.py:395
  (1 shorter events, 0.0 us)
Async XLA Ops:
  0.6 7.0 %copy-start.5 = (f32[257]{0:T(512)S(1)}, f32[257]{0:T(512)}, u32[]{:S(2)}) copy-start(f32[257]{0:T(512)} %param.18) | copy-start | bytes 3088
  0.6 7.0 %copy-start = (f32[384,512]{1,0:T(8,128)S(1)}, f32[384,512]{1,0:T(8,128)}, u32[]{:S(2)}) copy-start(f32[384,512]{1,0:T(8,128)} %constant.2.clone.cos_ref) | copy-start | bytes 2359300
  0.7 7.0 %copy-start.1 = (bf16[4,4,128,128]{3,2,1,0:T(8,128)(2,1)S(1)}, bf16[4,4,128,128]{3,2,1,0:T(8,128)(2,1)}, u32[]{:S(2)}) copy-start(bf16[4,4,128,128]{3,2,1,0:T(8,128)(2,1)} %point_ref.1) | copy-start | bytes 1572868
  3.0 4.7 %copy-start.2 = (s32[4,4]{1,0:T(4,128)S(1)}, s32[4,4]{1,0:T(4,128)}, u32[]{:S(2)}) copy-start(s32[4,4]{1,0:T(4,128)} %tids_ref.1) | copy-start | bytes 196
  3.0 4.7 %copy-start.3 = (s32[4,4]{1,0:T(4,128)S(1)}, s32[4,4]{1,0:T(4,128)}, u32[]{:S(2)}) copy-start(s32[4,4]{1,0:T(4,128)} %offs_ref.1) | copy-start | bytes 196
  3.0 6.7 %collective-permute-start.2 = (bf16[80,512]{1,0:T(8,128)(2,1)S(1)}, bf16[80,512]{1,0:T(8,128)(2,1)S(1)}, u32[]{:S(2)}, u32[]{:S(2)}) collective-permute-start(bf16[80,512]{1,0:T(8,128)(2,1)S(1)} %get-tuple-element.22.m0), channel_id=1, source_target_pairs={{0,24},{8,16},{16,8},{24,0},{1,25},{9,17},{17,9},{25,1},{2,26},{10... | collective-permute-start | bytes 245768 | tf_op jit(solution)/shard_map/ppermute | solution.py:300
  7.0 4.4 %collective-permute-start.1 = (bf16[80,512]{1,0:T(8,128)(2,1)S(1)}, bf16[80,512]{1,0:T(8,128)(2,1)S(1)}, u32[]{:S(2)}, u32[]{:S(2)}) collective-permute-start(bf16[80,512]{1,0:T(8,128)(2,1)S(1)} %get-tuple-element.22.m0), channel_id=1, source_target_pairs={{0,16},{8,24},{16,0},{24,8},{1,17},{9,25},{17,1},{25,9},{2,18},{10... | collective-permute-start | bytes 245768 | tf_op jit(solution)/shard_map/ppermute | solution.py:300
  7.5 4.4 %collective-permute-start = (bf16[80,512]{1,0:T(8,128)(2,1)S(1)}, bf16[80,512]{1,0:T(8,128)(2,1)S(1)}, u32[]{:S(2)}, u32[]{:S(2)}) collective-permute-start(bf16[80,512]{1,0:T(8,128)(2,1)S(1)} %get-tuple-element.22.m0), channel_id=1, source_target_pairs={{0,8},{8,0},{16,24},{24,16},{1,9},{9,1},{17,25},{25,17},{2,10},{10... | collective-permute-start | bytes 245768 | tf_op jit(solution)/shard_map/ppermute | solution.py:300
  7.6 0.7 %copy-start.4 = (s32[32]{0:T(128)S(1)}, s32[32]{0:T(128)}, u32[]{:S(2)}) copy-start(s32[32]{0:T(128)} %owner_ref.1) | copy-start | bytes 388
  24.5 9.0 %all-to-all-start.1 = ((bf16[8,16,128]{2,1,0:T(8,128)(2,1)}), bf16[8,16,128]{2,1,0:T(8,128)(2,1)S(1)}, u32[]{:S(2)}, u32[]{:S(2)}) async-start(bf16[8,16,128]{2,1,0:T(8,128)(2,1)} %get-tuple-element.31), calls=%async_computation.1 | async-start | bytes 65536 | tf_op jit(solution)/shard_map/all_to_all | solution.py:377

commit v3 on v2

--- a/solution.py
+++ b/solution.py
@@ -14,6 +14,7 @@
 LANES = 128
 BASE = 128
 EXT = 16
+MORE = 8
 NN = (((1,), (0,)), ((), ()))
 NT = (((1,), (1,)), ((), ()))
 
@@ -39,30 +40,14 @@
     return (scale * np.cos(2.0 * math.pi * ((f * n) % flen) / flen)).astype(np.float32)
 
 
-def sums_kernel(modes, parts, ts_hbm, flag_hbm, v_hbm, g_hbm, msg_ref, ts_ref, keep_ref, v_ref, g_ref, flag_ref, sem,
-                small_sem):
+def sums_kernel(modes, ts_hbm, flag_hbm, v_hbm, g_hbm, msg_ref, ts_ref, keep_ref, v_ref, g_ref, flag_ref, sem):
     dets, samples = ts_ref.shape
-    chunk = dets // parts
-    smalls = [
-        pltpu.make_async_copy(v_hbm, v_ref, small_sem.at[0]),
-        pltpu.make_async_copy(g_hbm, g_ref, small_sem.at[1]),
-    ]
-    for copy in smalls:
+    streams = [(v_hbm, v_ref), (g_hbm, g_ref), (flag_hbm, flag_ref), (ts_hbm, ts_ref)]
+    copies = [pltpu.make_async_copy(a, b, sem.at[i]) for i, (a, b) in enumerate(streams)]
+    for copy in copies:
         copy.start()
-    pairs = []
-    for i in range(parts):
-        rows = pl.ds(i * chunk, chunk)
-        pairs.append(
-            (
-                pltpu.make_async_copy(ts_hbm.at[rows], ts_ref.at[rows], sem.at[0, i]),
-                pltpu.make_async_copy(flag_hbm.at[rows], flag_ref.at[rows], sem.at[1, i]),
-            )
-        )
-    for pair in pairs:
-        for copy in pair:
-            copy.start()
-    for copy in smalls:
-        copy.wait()
+    copies[0].wait()
+    copies[1].wait()
     vt = v_ref[...]
     g = g_ref[...]
     row = iota((EXT, dets), 0)
@@ -78,30 +63,37 @@
     u = jnp.sum(jnp.where(lane == iota((modes, samples), 0), u, 0.0), axis=0, keepdims=True)
     u = jnp.where(iota((1, samples), 1) == modes, square, u)
     n = modes + EXT
-    acc1 = jnp.zeros((n, samples), F32)
-    acc2 = jnp.zeros((n, samples), F32)
-    for i in range(parts):
-        for copy in pairs[i]:
-            copy.wait()
-        at = slice(i * chunk, (i + 1) * chunk)
-        keep = (1 - flag_ref[at]).astype(F32)
-        keep_ref[at] = keep.astype(BF16)
-        x_hi, x_lo = split(ts_ref[at] * keep)
-        both = mm(left1[:, at], x_hi)
-        acc1 = acc1 + (both[:n] + both[n:]) + mm(hi1[:, at], x_lo)
-        both = mm(left2[:, at], keep.astype(BF16))
-        acc2 = acc2 + (both[:n] + both[n:])
+    copies[2].wait()
+    keep = (1 - flag_ref[...]).astype(F32)
+    keep_ref[...] = keep.astype(BF16)
+    both = mm(left2, keep.astype(BF16))
+    acc2 = both[:n] + both[n:]
+    copies[3].wait()
+    x_hi, x_lo = split(ts_ref[...] * keep_ref[...].astype(F32))
+    both = mm(left1, x_hi)
+    acc1 = both[:n] + both[n:] + mm(hi1, x_lo)
     msg_ref[0:modes] = acc1[0:modes].astype(BF16)
     msg_ref[modes : 2 * modes] = acc2[0:modes].astype(BF16)
-    row = iota((EXT, samples), 0)
-    ext = acc1[modes:] + acc2[modes:] + jnp.where((row >= 4) & (row < 6), u, 0.0)
+    row = iota((MORE, samples), 0)
+    ext = acc1[modes : modes + MORE] + acc2[modes : modes + MORE] + jnp.where((row >= 4) & (row < 6), u, 0.0)
     hi = ext.astype(BF16).astype(F32)
     msg_ref[2 * modes :] = jnp.where(row % 2 == 1, ext - hi, hi).astype(BF16)
 
 
-def prep_kernel(seg, kblk, lane_blocks, digits, tids_ref, offs_ref, owner_ref, gain_ref, cos_ref, point_ref, v_ref,
-                h2_ref, pn_ref, pt_ref, v3_ref, geo_ref, own_ref, wide_ref):
+def prep_kernel(seg, kblk, lane_blocks, digits, tids_hbm, offs_hbm, owner_hbm, cos_hbm, point_hbm, gain_ref, v_ref,
+                h2_ref, toep_ref, pn_ref, pt_ref, v3_ref, geo_ref, own_ref,
+                tids_ref, offs_ref, owner_ref, cos_ref, point_ref, wide_ref, sem):
+    streams = [(cos_hbm, cos_ref), (point_hbm, point_ref), (tids_hbm, tids_ref), (offs_hbm, offs_ref),
+               (owner_hbm, owner_ref)]
+    copies = [pltpu.make_async_copy(a, b, sem.at[i]) for i, (a, b) in enumerate(streams)]
+    for copy in copies:
+        copy.start()
     flen = cos_ref.shape[1]
+    vt = v_ref[...]
+    vhi = vt.astype(BF16).astype(F32)
+    pad = jnp.zeros((LANES - 3 * vt.shape[0], vt.shape[1]), F32)
+    v3_ref[...] = jnp.concatenate([vhi, vhi, vt - vhi, pad], axis=0).T.astype(BF16)
+    copies[0].wait()
     wide_ref[...] = jnp.zeros_like(wide_ref)
     wide_ref[0:1, 0 : gain_ref.shape[1]] = gain_ref[...]
     h = lax.dot_general(wide_ref[...], cos_ref[...], NN, precision=lax.Precision.HIGHEST, preferred_element_type=F32)
@@ -115,10 +107,12 @@
             to = slice(b * LANES, (b + 1) * LANES)
             h2_ref[a * LANES : (a + 1) * LANES, to] = base_hi[:, c * LANES : (c + 1) * LANES]
             h2_ref[flen + a * LANES : flen + (a + 1) * LANES, to] = base_lo[:, c * LANES : (c + 1) * LANES]
-    vt = v_ref[...]
-    vhi = vt.astype(BF16).astype(F32)
-    pad = jnp.zeros((LANES - 3 * vt.shape[0], vt.shape[1]), F32)
-    v3_ref[...] = jnp.concatenate([vhi, vhi, vt - vhi, pad], axis=0).T.astype(BF16)
+    for c in range(blocks):
+        at = slice(c * LANES, (c + 1) * LANES)
+        toep_ref[at, 0:LANES] = base_hi[:, at]
+        toep_ref[at, LANES : 2 * LANES] = base_lo[:, at]
+    for copy in copies[1:]:
+        copy.wait()
     listed = seg * kblk
     row16 = iota((listed, LANES), 0)
     first = lax.axis_index("tm") * listed
@@ -150,24 +144,36 @@
     own_ref[...] = own
 
 
-def filtered(b, h2_ref):
+def filtered(b, toep_ref):
     flen = b.shape[1]
+    blocks = flen // LANES
+    rows = -(-2 * blocks // EXT) * EXT
     hi, lo = split(b)
-    row = iota((EXT, flen), 0)
-    left = jnp.where(row == 0, hi.astype(F32), jnp.where(row == 1, lo.astype(F32), 0.0)).astype(BF16)
-    z = mm(left, h2_ref[0:flen]) + mm(left, h2_ref[flen:])
-    return z[0:1] + z[1:2]
+    hi, lo = hi.astype(F32), lo.astype(F32)
+    row = iota((rows, LANES), 0)
+    left = []
+    for c in range(blocks):
+        block = jnp.zeros((rows, LANES), F32)
+        for m in range(blocks):
+            at = slice(m * LANES, (m + 1) * LANES)
+            a = (m + c) % blocks
+            block = jnp.where(row == a, hi[:, at], jnp.where(row == blocks + a, lo[:, at], block))
+        left.append(block.astype(BF16))
+    z = mm(jnp.concatenate(left, axis=1), toep_ref[...])
+    z = z[:, 0:LANES] + z[:, LANES:]
+    return z[0:blocks] + z[blocks : 2 * blocks]
 
 
 def project(z, pn_ref, seg, kblk):
-    samples = z.shape[1]
     listed = seg * kblk
     hi, lo = split(z)
-    row = iota((2 * listed, samples), 0)
-    lane = iota((2 * listed, samples), 1)
-    wide = jnp.where(row < listed, hi.astype(F32), lo.astype(F32))
-    wide = jnp.where(lane // (samples // seg) == row % seg, wide, 0.0).astype(BF16)
-    out = mm(wide, pn_ref[...])
+    hi, lo = hi.astype(F32), lo.astype(F32)
+    row = iota((2 * listed, LANES), 0)
+    left = []
+    for s in range(seg):
+        value = jnp.where(row < listed, hi[s : s + 1], lo[s : s + 1])
+        left.append(jnp.where(row % seg == s, value, 0.0).astype(BF16))
+    out = mm(jnp.concatenate(left, axis=1), pn_ref[...])
     out = out[:listed] + out[listed:]
     row = iota((listed, LANES), 0)
     proj = out[:, 0:LANES]
@@ -176,7 +182,7 @@
     return proj
 
 
-def first_kernel(modes, seg, kblk, m0, m1, m2, m3, h2_ref, pn_ref, geo_ref,
+def first_kernel(modes, seg, kblk, m0, m1, m2, m3, toep_ref, pn_ref, geo_ref,
                  bq_ref, vec_ref, send_ref):
     tot = m0[...].astype(F32) + m1[...].astype(F32) + m2[...].astype(F32) + m3[...].astype(F32)
     bq_ref[...] = tot[0 : 2 * modes]
@@ -188,7 +194,7 @@
     b2 = ext[2:3] + ext[3:4] - jnp.sum(u_col * tot[modes : 2 * modes], axis=0, keepdims=True)
     row = iota((8, b1.shape[1]), 0)
     vec_ref[...] = jnp.where(row == 0, b1, jnp.where(row == 1, b2, jnp.where(row == 2, square, 0.0)))
-    z = filtered(b1, h2_ref)
+    z = filtered(b1, toep_ref)
     proj = project(z, pn_ref, seg, kblk).astype(BF16)
     geo = geo_ref[...]
     listed = seg * kblk
@@ -205,7 +211,7 @@
     return out
 
 
-def second_kernel(seg, kblk, digits, all_ref, own_ref, vec_ref, h2_ref, pn_ref, pt_ref, sig_ref, send_ref):
+def second_kernel(seg, kblk, digits, all_ref, own_ref, vec_ref, toep_ref, pn_ref, pt_ref, sig_ref, send_ref):
     listed = seg * kblk
     blocks = all_ref.shape[0] * listed // LANES
     samples = vec_ref.shape[1]
@@ -227,7 +233,7 @@
     lane = iota((listed, samples), 1)
     sig = jnp.sum(jnp.where(lane // (samples // seg) == row % seg, spread, 0.0), axis=0, keepdims=True)
     sig_ref[...] = jnp.broadcast_to(sig, sig_ref.shape)
-    z = filtered(vec_ref[0:1] - vec_ref[1:2] * sig, h2_ref)
+    z = filtered(vec_ref[0:1] - vec_ref[1:2] * sig, toep_ref)
     proj = project(z, pn_ref, seg, kblk).astype(BF16)
     for t in range(send_ref.shape[0]):
         send_ref[t] = proj
@@ -306,17 +312,17 @@
     modes = mode_vectors.shape[1]
     seg, kblk = tile_ids.shape
     listed = seg * kblk
-    parts = dets // LANES
+    parts = 2
     lane_blocks = n_tm * listed // LANES
     digits = -(-int(tile_owner.shape[0] * LANES - 1).bit_length() // 7)
     id_rows = -(-digits * lane_blocks // 8) * 8
     inputs = (timestream, sample_flags, mode_vectors.T, det_gains.reshape(1, dets))
     msg, ts, keep, vt, g = pl.pallas_call(
-        functools.partial(sums_kernel, modes, parts),
+        functools.partial(sums_kernel, modes),
         in_specs=[HB] * 4,
         out_specs=[VM] * 5,
         out_shape=[
-            shape((2 * modes + EXT, samples), BF16),
+            shape((2 * modes + MORE, samples), BF16),
             shape((dets, samples)),
             shape((dets, samples), BF16),
             shape((modes, dets)),
@@ -324,8 +330,7 @@
         ],
         scratch_shapes=[
             pltpu.VMEM((dets, samples), jnp.int32),
-            pltpu.SemaphoreType.DMA((2, parts)),
-            pltpu.SemaphoreType.DMA((2,)),
+            pltpu.SemaphoreType.DMA((4,)),
         ],
         compiler_params=GRANT,
         name="sums",
@@ -333,24 +338,33 @@
     parts_of_all = [msg] + others(msg, "det", n_det)
 
     rows = -(-filter_gain.shape[0] // LANES) * LANES
-    h2, pn, pt, v3, geo, own = pl.pallas_call(
+    inputs = (tile_ids, block_offsets, tile_owner, jnp.asarray(cosine_table(samples, rows)), pointing)
+    h2, toep, pn, pt, v3, geo, own = pl.pallas_call(
         functools.partial(prep_kernel, seg, kblk, lane_blocks, digits),
-        in_specs=[SM, SM, SM, VM, VM, VM, VM],
-        out_specs=[VM] * 6,
+        in_specs=[HB] * 5 + [VM] * 2,
+        out_specs=[VM] * 7,
         out_shape=[
             shape((2 * samples, samples), BF16),
+            shape((samples, 2 * LANES), BF16),
             shape((samples, kblk * LANES), BF16),
             shape((kblk * LANES, samples), BF16),
             shape((dets, LANES), BF16),
             shape((listed + id_rows, LANES), BF16),
             shape((listed, LANES)),
         ],
-        scratch_shapes=[pltpu.VMEM((8, rows), F32)],
+        scratch_shapes=[
+            pltpu.SMEM(tile_ids.shape, jnp.int32),
+            pltpu.SMEM(block_offsets.shape, jnp.int32),
+            pltpu.SMEM(tile_owner.shape, jnp.int32),
+            pltpu.VMEM((rows, samples), F32),
+            pltpu.VMEM(pointing.shape, BF16),
+            pltpu.VMEM((8, rows), F32),
+            pltpu.SemaphoreType.DMA((5,)),
+        ],
         cost_estimate=pl.CostEstimate(flops=10**8, bytes_accessed=3 * 10**6, transcendentals=0),
         compiler_params=GRANT,
         name="prep",
-    )(tile_ids, block_offsets, tile_owner, filter_gain.reshape(1, -1), jnp.asarray(cosine_table(samples, rows)),
-      pointing, vt)
+    )(*(pltpu.with_memory_space_constraint(x, pltpu.HBM) for x in inputs), filter_gain.reshape(1, -1), vt)
 
     bq, vec, send = pl.pallas_call(
         functools.partial(first_kernel, modes, seg, kblk),
@@ -363,7 +377,7 @@
         ],
         compiler_params=GRANT,
         name="first",
-    )(*parts_of_all, h2, pn, geo)
+    )(*parts_of_all, toep, pn, geo)
     everyone = lax.all_to_all(send, "tm", 0, 0)
 
     sig, send = pl.pallas_call(
@@ -373,7 +387,7 @@
         out_shape=[shape((8, samples)), shape((n_tm, listed, LANES), BF16)],
         compiler_params=GRANT,
         name="second",
-    )(everyone, own, vec, h2, pn, pt)
+    )(everyone, own, vec, toep, pn, pt)
     everyone2 = lax.all_to_all(send, "tm", 0, 0)
 
     cleaned, base, scale, same = pl.pallas_call(

time: 34.5 us -> 34 us (0.986)
  local copies, waits for them, and re-layouts: 0.65 us -> 0.01 us
    pallas_call x1, Pallas kernels: 1.36 us -> 2.23 us  [shards(): pl.pallas_call(functools.partial(prep_kernel, seg, kblk, lane_blocks, dig...]
    unnamed x12 -> x2, local copies, waits for them, and re-layouts: 0.65 us -> 0.01 us
  transfers between devices with their start and end apart: 4 -> 4, of which waited for: 3 -> 3; matrix products, arithmetic and copies ran while one was open for 0% -> 0% of each run, Pallas kernels for 10% -> 12%
where the time goes in v3:
time: 34 us; the launch traced here: 33.7 us
  blocking collectives  10.8 us (32%)
  Pallas kernels  8.39 us (25%)
  starting transfers between devices  7.97 us (23%)
  waiting for transfers between devices  5.9 us (17%)
  between operations  0.68 us (2%)
    all_to_all x1, blocking collectives, shards(): everyone = lax.all_to_all(send, 'tm', 0, 0)  10.8 us
    ppermute x3, starting transfers between devices, others(): return [lax.ppermute(x, axis, p) for p in pairs]  4.63 us
    all_to_all x1, waiting for transfers between devices, shards(): everyone2 = lax.all_to_all(send, 'tm', 0, 0)  3.94 us
    all_to_all x1, starting transfers between devices, shards(): everyone2 = lax.all_to_all(send, 'tm', 0, 0)  3.34 us
    pallas_call x1, Pallas kernels, shards(): pl.pallas_call(functools.partial(prep_kernel, seg, kblk, lane_blocks, dig...  2.23 us
    pallas_call x1, Pallas kernels, shards(): pl.pallas_call(functools.partial(sums_kernel, modes), in_specs=[HB] * 4,...  1.98 us
    ppermute x3, waiting for transfers between devices, others(): return [lax.ppermute(x, axis, p) for p in pairs]  1.97 us
    pallas_call x1, Pallas kernels, shards(): pl.pallas_call(functools.partial(clean_kernel, seg, kblk, digits, modes,...  1.73 us
  transfers between devices with their start and end apart: 4, of which 3 were waited for; matrix products, arithmetic and copies ran while one was open for 0% of the time, Pallas kernels for 12%

profile of v3, /device:TPU:0, one launch (start us, length us, event | category | flops | bytes accessed | tf_op | source)
XLA Modules:
  0.0 33.7 jit_solution(11596944386899199791)
XLA Ops:
  0.6 0.0 copy-start
  0.6 2.0 %sums.1 = (bf16[72,512]{1,0:T(8,128)(2,1)S(1)}, f32[512,512]{1,0:T(8,128)S(1)}, bf16[512,512]{1,0:T(8,128)(2,1)S(1)}, f32[32,512]{1,0:T(8,128)S(1)}, f32[1,512]{1,0:T(1,128)S(1)}) custom-call(f32[512,512]{1,0:T(8,128)} %ts_hbm.1, s32[512,512]{1,0:T(8,128)} %flag_hbm.1, f32[32,512]{1,0:T(8,128)} %bitcast.2, f32[1,512]{1,0:T(1,128)} %bitcast.3), custom_call_target="tpu_custom_call" | custom-call | tf_op jit(solution)/shard_map/sums/pallas_call | solution.py:320
  2.6 4.0 %collective-permute-start.2 = (bf16[72,512]{1,0:T(8,128)(2,1)S(1)}, bf16[72,512]{1,0:T(8,128)(2,1)S(1)}, u32[]{:S(2)}, u32[]{:S(2)}) collective-permute-start(bf16[72,512]{1,0:T(8,128)(2,1)S(1)} %get-tuple-element.23.m0), channel_id=1, source_target_pairs={{0,24},{8,16},{16,8},{24,0},{1,25},{9,17},{17,9},{25,1},{2,26},{10... | collective-permute-start | bytes 221192 | tf_op jit(solution)/shard_map/ppermute | solution.py:306
  6.6 0.5 %collective-permute-start.1 = (bf16[72,512]{1,0:T(8,128)(2,1)S(1)}, bf16[72,512]{1,0:T(8,128)(2,1)S(1)}, u32[]{:S(2)}, u32[]{:S(2)}) collective-permute-start(bf16[72,512]{1,0:T(8,128)(2,1)S(1)} %get-tuple-element.23.m0), channel_id=1, source_target_pairs={{0,16},{8,24},{16,0},{24,8},{1,17},{9,25},{17,1},{25,9},{2,18},{10... | collective-permute-start | bytes 221192 | tf_op jit(solution)/shard_map/ppermute | solution.py:306
  7.1 0.1 collective-permute-start
  7.3 0.0 copy-done
  7.3 2.2 %prep.1 = (bf16[1024,512]{1,0:T(8,128)(2,1)S(1)}, bf16[512,256]{1,0:T(8,128)(2,1)S(1)}, bf16[512,512]{1,0:T(8,128)(2,1)S(1)}, bf16[512,512]{1,0:T(8,128)(2,1)S(1...) custom-call(s32[4,4]{1,0:T(4,128)} %tids_hbm.1, s32[4,4]{1,0:T(4,128)} %offs_hbm.1, ...), custom_call_target="tpu_custom_call" | custom-call | flops 100000000 | bytes 3000000 | tf_op jit(solution)/shard_map/prep/pallas_call | solution.py:342
  9.5 0.0 collective-permute-done.2.m3
  9.5 1.5 %collective-permute-done.1.m2 = bf16[72,512]{1,0:T(8,128)(2,1)S(1)} collective-permute-done((bf16[72,512]{1,0:T(8,128)(2,1)S(1)}, bf16[72,512]{1,0:T(8,128)(2,1)S(1)}, u32[]{:S(2)}, u32[]{:S(2)}) %collective-permute-start.1) | collective-permute-done | bytes 73760 | tf_op jit(solution)/shard_map/ppermute | solution.py:306
  11.0 0.5 %collective-permute-done.m1 = bf16[72,512]{1,0:T(8,128)(2,1)S(1)} collective-permute-done((bf16[72,512]{1,0:T(8,128)(2,1)S(1)}, bf16[72,512]{1,0:T(8,128)(2,1)S(1)}, u32[]{:S(2)}, u32[]{:S(2)}) %collective-permute-start) | collective-permute-done | bytes 73760 | tf_op jit(solution)/shard_map/ppermute | solution.py:306
  11.5 0.4 %first.1 = (f32[64,512]{1,0:T(8,128)S(1)}, f32[8,512]{1,0:T(8,128)S(1)}, bf16[8,40,128]{2,1,0:T(8,128)(2,1)S(1)}) custom-call(bf16[72,512]{1,0:T(8,128)(2,1)S(1)} %get-tuple-element.23.m0, bf16[72,512]{1,0:T(8,128)(2,1)S(1)} %collective-permute-done.m1, bf16[72,512]{1,0:T(8,128)(2,1)S(1)} %collective-permute-done.1.m2, ...), custom_call_target="tpu_custom_call" | custom-call | tf_op jit(solution)/shard_map/first/pallas_call | solution.py:369
  11.9 10.8 %all_to_all.10.all_ref = bf16[8,40,128]{2,1,0:T(8,128)(2,1)S(1)} all-to-all(bf16[8,40,128]{2,1,0:T(8,128)(2,1)S(1)} %get-tuple-element.28), channel_id=1, replica_groups=mesh['det'=4,'tm'=8] {'tm'}, dimensions={0} | all-to-all | bytes 163840 | tf_op jit(solution)/shard_map/all_to_all | solution.py:381
  22.6 1.3 %second.1 = (f32[8,512]{1,0:T(8,128)S(1)}, bf16[8,16,128]{2,1,0:T(8,128)(2,1)}) custom-call(bf16[8,40,128]{2,1,0:T(8,128)(2,1)S(1)} %all_to_all.10.all_ref, f32[16,128]{1,0:T(8,128)S(1)} %get-tuple-element.29.own_ref, f32[8,512]{1,0:T(8,128)S(1)} %get-tuple-element.30.vec_ref, bf16[512,256]{1,0:T(8,128)(2,1)S(1)} %get-tuple-element.25.toep_ref, ...), custom_call_target="tpu_custom_call" | custom-call | tf_op jit(solution)/shard_map/second/pallas_call | solution.py:383
  23.9 3.3 %all-to-all-start.1 = ((bf16[8,16,128]{2,1,0:T(8,128)(2,1)}), bf16[8,16,128]{2,1,0:T(8,128)(2,1)S(1)}, u32[]{:S(2)}, u32[]{:S(2)}) async-start(bf16[8,16,128]{2,1,0:T(8,128)(2,1)} %get-tuple-element.32), calls=%async_computation.1 | async-start | bytes 65536 | tf_op jit(solution)/shard_map/all_to_all | solution.py:391
  27.3 1.7 %clean.1 = (bf16[512,512]{1,0:T(8,128)(2,1)}, f32[128,128]{1,0:T(8,128)S(1)}, f32[128,128]{1,0:T(8,128)S(1)}, bf16[1,128,128]{2,1,0:T(8,128)(2,1)S(1)}) custom-call(f32[512,512]{1,0:T(8,128)S(1)} %get-tuple-element.33.ts_ref, bf16[512,512]{1,0:T(8,128)(2,1)S(1)} %get-tuple-element.34.keep_ref, f32[1,512]{1,0:T(1,128)S(1)} %get-tuple-element.35.g_ref, ...), custom_call_target="tpu_custom_call" | custom-call | flops 1000000000 | bytes 4000000 | tf_op jit(solution)/shard_map/clean/pallas_call | solution.py:393
  29.0 3.9 %all-to-all-done.1.all2_ref = bf16[8,16,128]{2,1,0:T(8,128)(2,1)S(1)} async-done(((bf16[8,16,128]{2,1,0:T(8,128)(2,1)}), bf16[8,16,128]{2,1,0:T(8,128)(2,1)S(1)}, u32[]{:S(2)}, u32[]{:S(2)}) %all-to-all-start.1) | async-done | bytes 32800 | tf_op jit(solution)/shard_map/all_to_all | solution.py:391
  33.0 0.8 %tile.1 = f32[1,128,128]{2,1,0:T(8,128)} custom-call(bf16[8,16,128]{2,1,0:T(8,128)(2,1)S(1)} %all-to-all-done.1.all2_ref, f32[128,128]{1,0:T(8,128)S(1)} %get-tuple-element.40.base_ref, f32[128,128]{1,0:T(8,128)S(1)} %get-tuple-element.41.scale_ref, bf16[1,128,128]{2,1,0:T(8,128)(2,1)S(1)} %get-tuple-element.42.same_ref), custom_call_target="tpu_custom_call" | custom-call | tf_op jit(solution)/shard_map/tile/pallas_call | solution.py:409
  (1 shorter events, 0.0 us)
Async XLA Ops:
  0.6 6.6 %copy-start = (f32[257]{0:T(512)S(1)}, f32[257]{0:T(512)}, u32[]{:S(2)}) copy-start(f32[257]{0:T(512)} %param.18) | copy-start | bytes 3088
  2.6 6.9 %collective-permute-start.2 = (bf16[72,512]{1,0:T(8,128)(2,1)S(1)}, bf16[72,512]{1,0:T(8,128)(2,1)S(1)}, u32[]{:S(2)}, u32[]{:S(2)}) collective-permute-start(bf16[72,512]{1,0:T(8,128)(2,1)S(1)} %get-tuple-element.23.m0), channel_id=1, source_target_pairs={{0,24},{8,16},{16,8},{24,0},{1,25},{9,17},{17,9},{25,1},{2,26},{10... | collective-permute-start | bytes 221192 | tf_op jit(solution)/shard_map/ppermute | solution.py:306
  6.6 4.4 %collective-permute-start.1 = (bf16[72,512]{1,0:T(8,128)(2,1)S(1)}, bf16[72,512]{1,0:T(8,128)(2,1)S(1)}, u32[]{:S(2)}, u32[]{:S(2)}) collective-permute-start(bf16[72,512]{1,0:T(8,128)(2,1)S(1)} %get-tuple-element.23.m0), channel_id=1, source_target_pairs={{0,16},{8,24},{16,0},{24,8},{1,17},{9,25},{17,1},{25,9},{2,18},{10... | collective-permute-start | bytes 221192 | tf_op jit(solution)/shard_map/ppermute | solution.py:306
  7.1 4.4 %collective-permute-start = (bf16[72,512]{1,0:T(8,128)(2,1)S(1)}, bf16[72,512]{1,0:T(8,128)(2,1)S(1)}, u32[]{:S(2)}, u32[]{:S(2)}) collective-permute-start(bf16[72,512]{1,0:T(8,128)(2,1)S(1)} %get-tuple-element.23.m0), channel_id=1, source_target_pairs={{0,8},{8,0},{16,24},{24,16},{1,9},{9,1},{17,25},{25,17},{2,10},{10... | collective-permute-start | bytes 221192 | tf_op jit(solution)/shard_map/ppermute | solution.py:306
  23.9 9.0 %all-to-all-start.1 = ((bf16[8,16,128]{2,1,0:T(8,128)(2,1)}), bf16[8,16,128]{2,1,0:T(8,128)(2,1)S(1)}, u32[]{:S(2)}, u32[]{:S(2)}) async-start(bf16[8,16,128]{2,1,0:T(8,128)(2,1)} %get-tuple-element.32), calls=%async_computation.1 | async-start | bytes 65536 | tf_op jit(solution)/shard_map/all_to_all | solution.py:391

commit v4 on v3

--- a/solution.py
+++ b/solution.py
@@ -14,6 +14,7 @@
 LANES = 128
 BASE = 128
 EXT = 16
+EARLY = 2
 MORE = 8
 NN = (((1,), (0,)), ((), ()))
 NT = (((1,), (1,)), ((), ()))
@@ -239,26 +240,20 @@
         send_ref[t] = proj
 
 
-def clean_kernel(seg, kblk, digits, modes, parts, ts_ref, keep_ref, g_ref, v3_ref, bq_ref, sig_ref, h2_ref,
-                 all_ref, vec_ref, out_hbm, base_ref, scale_ref, same_ref, out_ref, sem):
-    dets, samples = ts_ref.shape
-    chunk = dets // parts
+def clean_rows(modes, at, ts_ref, keep_ref, g_ref, v3_ref, bq_ref, sig_ref, h2_ref):
+    samples = ts_ref.shape[1]
     sig = sig_ref[0:1]
     q_hi, q_lo = split(bq_ref[0:modes] - bq_ref[modes : 2 * modes] * sig)
     pad = jnp.zeros((LANES - 3 * modes, samples), BF16)
     q3 = jnp.concatenate([q_hi, q_lo, q_hi, pad], axis=0)
-    eye = iota((chunk, chunk), 0) == iota((chunk, chunk), 1)
-    copies = []
-    for i in range(parts):
-        at = slice(i * chunk, (i + 1) * chunk)
-        g_col = jnp.sum(jnp.where(eye, g_ref[:, at], 0.0), axis=1, keepdims=True)
-        rest = (ts_ref[at] - g_col * sig) * keep_ref[at].astype(F32) - mm(v3_ref[at], q3)
-        rest = rest.astype(BF16)
-        out_ref[at] = (mm(rest, h2_ref[0:samples]) + mm(rest, h2_ref[samples:])).astype(BF16)
-        rows = pl.ds(i * chunk, chunk)
-        copy = pltpu.make_async_copy(out_ref.at[rows], out_hbm.at[rows], sem.at[i])
-        copy.start()
-        copies.append(copy)
+    eye = iota((at.stop - at.start,) * 2, 0) == iota((at.stop - at.start,) * 2, 1)
+    g_col = jnp.sum(jnp.where(eye, g_ref[:, at], 0.0), axis=1, keepdims=True)
+    rest = (ts_ref[at] - g_col * sig) * keep_ref[at].astype(F32) - mm(v3_ref[at], q3)
+    rest = rest.astype(BF16)
+    return (mm(rest, h2_ref[0:samples]) + mm(rest, h2_ref[samples:])).astype(BF16)
+
+
+def tile_parts(seg, kblk, digits, all_ref, vec_ref, base_ref, scale_ref, same_ref):
     listed = seg * kblk
     blocks = all_ref.shape[0] * listed // LANES
     per = LANES // listed
@@ -276,8 +271,26 @@
     scale = jnp.sqrt(wsum) / wsum
     scale_ref[...] = scale
     base_ref[...] = psum * scale
-    for copy in copies:
-        copy.wait()
+
+
+def early_kernel(seg, kblk, digits, modes, ts_ref, keep_ref, g_ref, v3_ref, bq_ref, sig_ref, h2_ref, all_ref, vec_ref,
+                 early_ref, base_ref, scale_ref, same_ref):
+    rows = slice(0, early_ref.shape[0])
+    early_ref[...] = clean_rows(modes, rows, ts_ref, keep_ref, g_ref, v3_ref, bq_ref, sig_ref, h2_ref)
+    tile_parts(seg, kblk, digits, all_ref, vec_ref, base_ref, scale_ref, same_ref)
+
+
+def late_kernel(modes, ts_ref, keep_ref, g_ref, v3_ref, bq_ref, sig_ref, h2_ref, early_ref, after_ref, out_hbm,
+                late_ref, sem):
+    cut = early_ref.shape[0]
+    first = pltpu.make_async_copy(early_ref, out_hbm.at[pl.ds(0, cut)], sem.at[0])
+    first.start()
+    rows = slice(cut, ts_ref.shape[0])
+    late_ref[...] = clean_rows(modes, rows, ts_ref, keep_ref, g_ref, v3_ref, bq_ref, sig_ref, h2_ref)
+    second = pltpu.make_async_copy(late_ref, out_hbm.at[pl.ds(cut, late_ref.shape[0])], sem.at[1])
+    second.start()
+    first.wait()
+    second.wait()
 
 
 def tile_kernel(all2_ref, base_ref, scale_ref, same_ref, out_ref):
@@ -288,6 +301,27 @@
     out_ref[0] = base_ref[...] + psum * scale_ref[...]
 
 
+def pair_tile_kernel(send_ref, near_ref, far_ref, mate_ref, base_ref, scale_ref, same_ref, out_ref, all_ref):
+    t = lax.axis_index("tm")
+    core = t % 2
+    far, other = 6 - 2 * core, 4 + 2 * core
+    mate = jnp.bitwise_xor(t, 1)
+    arrived = [
+        (send_ref, t),
+        (near_ref, jnp.bitwise_xor(t, 2)),
+        (far_ref, jnp.bitwise_xor(t, far)),
+        (mate_ref, jnp.bitwise_xor(mate, other)),
+    ]
+    for ref, at in arrived:
+        all_ref[at] = ref[0]
+        all_ref[jnp.bitwise_xor(at, 1)] = ref[1]
+    blocks, per = same_ref.shape[0], LANES // all_ref.shape[1]
+    psum = jnp.zeros((LANES, LANES), F32)
+    for b in range(blocks):
+        psum = psum + mm(same_ref[b], all_ref[b * per : (b + 1) * per].reshape(LANES, LANES))
+    out_ref[0] = base_ref[...] + psum * scale_ref[...]
+
+
 VM = pl.BlockSpec(memory_space=pltpu.VMEM)
 HB = pl.BlockSpec(memory_space=pltpu.HBM)
 SM = pl.BlockSpec(memory_space=pltpu.SMEM)
@@ -312,7 +346,6 @@
     modes = mode_vectors.shape[1]
     seg, kblk = tile_ids.shape
     listed = seg * kblk
-    parts = 2
     lane_blocks = n_tm * listed // LANES
     digits = -(-int(tile_owner.shape[0] * LANES - 1).bit_length() // 7)
     id_rows = -(-digits * lane_blocks // 8) * 8
@@ -380,40 +413,65 @@
     )(*parts_of_all, toep, pn, geo)
     everyone = lax.all_to_all(send, "tm", 0, 0)
 
+    paired = n_tm == 8
     sig, send = pl.pallas_call(
         functools.partial(second_kernel, seg, kblk, digits),
         in_specs=[VM] * 6,
         out_specs=[VM] * 2,
-        out_shape=[shape((8, samples)), shape((n_tm, listed, LANES), BF16)],
+        out_shape=[shape((8, samples)), shape((1 if paired else n_tm, listed, LANES), BF16)],
         compiler_params=GRANT,
         name="second",
     )(everyone, own, vec, toep, pn, pt)
-    everyone2 = lax.all_to_all(send, "tm", 0, 0)
-
-    cleaned, base, scale, same = pl.pallas_call(
-        functools.partial(clean_kernel, seg, kblk, digits, modes, parts),
+    mates = [(i, i ^ 1) for i in range(n_tm)]
+    if paired:
+        mate = lax.ppermute(send, "tm", mates)
+
+    cut = EARLY * dets // 4
+    operands = (ts, keep, g, v3, bq, sig, h2)
+    early, base, scale, same = pl.pallas_call(
+        functools.partial(early_kernel, seg, kblk, digits, modes),
         in_specs=[VM] * 9,
-        out_specs=[HB, VM, VM, VM],
+        out_specs=[VM] * 4,
         out_shape=[
-            shape((dets, samples), BF16),
+            shape((cut, samples), BF16),
             shape((LANES, LANES)),
             shape((LANES, LANES)),
             shape((lane_blocks, LANES, LANES), BF16),
         ],
-        scratch_shapes=[pltpu.VMEM((dets, samples), BF16), pltpu.SemaphoreType.DMA((parts,))],
-        cost_estimate=pl.CostEstimate(flops=10**9, bytes_accessed=4 * 10**6, transcendentals=0),
-        compiler_params=GRANT,
-        name="clean",
-    )(ts, keep, g, v3, bq, sig, h2, everyone, vec)
+        cost_estimate=pl.CostEstimate(flops=5 * 10**8, bytes_accessed=2 * 10**6, transcendentals=0),
+        compiler_params=GRANT,
+        name="early",
+    )(*operands, everyone, vec)
+    if paired:
+        mate, early, base = lax.optimization_barrier((mate, early, base))
+        both = jnp.concatenate([send, mate], axis=0)
+        near = lax.ppermute(both, "tm", [(i, i ^ 2) for i in range(n_tm)])
+        after = lax.ppermute(both, "tm", [(i, i ^ (6 - 2 * (i % 2))) for i in range(n_tm)])
+        arrived = (both, near, after, lax.ppermute(after, "tm", mates))
+        last, scratch = pair_tile_kernel, [pltpu.VMEM((n_tm, listed, LANES), BF16)]
+    else:
+        arrived = (lax.all_to_all(send, "tm", 0, 0),)
+        after, last, scratch = vec, tile_kernel, []
+    cleaned = pl.pallas_call(
+        functools.partial(late_kernel, modes),
+        in_specs=[VM] * 9,
+        out_specs=HB,
+        out_shape=shape((dets, samples), BF16),
+        scratch_shapes=[pltpu.VMEM((dets - cut, samples), BF16), pltpu.SemaphoreType.DMA((2,))],
+        cost_estimate=pl.CostEstimate(flops=5 * 10**8, bytes_accessed=2 * 10**6, transcendentals=0),
+        compiler_params=GRANT,
+        name="late",
+    )(*operands, early, after)
 
     tile = pl.pallas_call(
-        tile_kernel,
-        in_specs=[VM] * 4,
+        last,
+        in_specs=[VM] * (len(arrived) + 3),
         out_specs=VM,
         out_shape=shape((1, LANES, LANES)),
+        scratch_shapes=scratch,
         compiler_params=GRANT,
         name="tile",
-    )(everyone2, base, scale, same)
+    )(*arrived, base, scale, same)
     return tile, cleaned
 
 

time: 34 us -> 32.3 us (0.950)
  starting transfers between devices: 7.97 us -> 5.69 us
  waiting for transfers between devices: 5.9 us -> 6.92 us
  Pallas kernels: 8.39 us -> 7.97 us
    ppermute x0 -> x4, waiting for transfers between devices: none -> 4.95 us  [the longest x1 4.4 us: shards(): lax.ppermute(both, 'tm', [(i, i ^ 6 - 2 * (i % 2)) for i in range(n_tm)])]
    all_to_all x1 -> x0, waiting for transfers between devices: 3.94 us -> none  [shards(): everyone2 = lax.all_to_all(send, 'tm', 0, 0)]
    all_to_all x1 -> x0, starting transfers between devices: 3.34 us -> none  [shards(): everyone2 = lax.all_to_all(send, 'tm', 0, 0)]
    ppermute x0 -> x4, starting transfers between devices: none -> 1.06 us  [the longest x1 1.05 us: shards(): lax.ppermute(both, 'tm', [(i, i ^ 6 - 2 * (i % 2)) for i in range(n_tm)])]
    pallas_call x1, Pallas kernels: 1.29 us -> 0.66 us  [shards(): pl.pallas_call(functools.partial(second_kernel, seg, kblk, digits), in_sp...]
    pallas_call x2 -> x3, Pallas kernels: 2.5 us -> 2.71 us  [the longest x1 1.29 us: shards(): pl.pallas_call(functools.partial(late_kernel, modes), in_specs=[VM] * 9,...]
  transfers between devices with their start and end apart: 4 -> 7, of which waited for: 3 -> 4; matrix products, arithmetic and copies ran while one was open for 0% -> 0% of each run, Pallas kernels for 12% -> 13%
where the time goes in v4:
time: 32.3 us; the launch traced here: 32.1 us
  blocking collectives  10.8 us (33%)
  Pallas kernels  7.97 us (25%)
  waiting for transfers between devices  6.92 us (21%)
  starting transfers between devices  5.69 us (18%)
  between operations  0.7 us (2%)
    all_to_all x1, blocking collectives, shards(): everyone = lax.all_to_all(send, 'tm', 0, 0)  10.8 us
    ppermute x3, starting transfers between devices, others(): return [lax.ppermute(x, axis, p) for p in pairs]  4.63 us
    ppermute x1, waiting for transfers between devices, shards(): lax.ppermute(both, 'tm', [(i, i ^ 6 - 2 * (i % 2)) for i in range(n_tm)])  4.4 us
    pallas_call x1, Pallas kernels, shards(): pl.pallas_call(functools.partial(prep_kernel, seg, kblk, lane_blocks, dig...  2.23 us
    pallas_call x1, Pallas kernels, shards(): pl.pallas_call(functools.partial(sums_kernel, modes), in_specs=[HB] * 4,...  1.98 us
    ppermute x3, waiting for transfers between devices, others(): return [lax.ppermute(x, axis, p) for p in pairs]  1.97 us
    pallas_call x1, Pallas kernels, shards(): pl.pallas_call(functools.partial(late_kernel, modes), in_specs=[VM] * 9,...  1.29 us
    ppermute x1, starting transfers between devices, shards(): lax.ppermute(both, 'tm', [(i, i ^ 6 - 2 * (i % 2)) for i in range(n_tm)])  1.05 us
  transfers between devices with their start and end apart: 7, of which 4 were waited for; matrix products, arithmetic and copies ran while one was open for 0% of the time, Pallas kernels for 13%

profile of v4, /device:TPU:0, one launch (start us, length us, event | category | flops | bytes accessed | tf_op | source)
XLA Modules:
  0.0 32.1 jit_solution(10143092420386308359)
XLA Ops:
  0.6 0.0 copy-start
  0.6 2.0 %sums.1 = (bf16[72,512]{1,0:T(8,128)(2,1)S(1)}, f32[512,512]{1,0:T(8,128)S(1)}, bf16[512,512]{1,0:T(8,128)(2,1)S(1)}, f32[32,512]{1,0:T(8,128)S(1)}, f32[1,512]{1,0:T(1,128)S(1)}) custom-call(f32[512,512]{1,0:T(8,128)} %ts_hbm.1, s32[512,512]{1,0:T(8,128)} %flag_hbm.1, f32[32,512]{1,0:T(8,128)} %bitcast.2, f32[1,512]{1,0:T(1,128)} %bitcast.3), custom_call_target="tpu_custom_call" | custom-call | tf_op jit(solution)/shard_map/sums/pallas_call | solution.py:353
  2.6 4.0 %collective-permute-start.2 = (bf16[72,512]{1,0:T(8,128)(2,1)S(1)}, bf16[72,512]{1,0:T(8,128)(2,1)S(1)}, u32[]{:S(2)}, u32[]{:S(2)}) collective-permute-start(bf16[72,512]{1,0:T(8,128)(2,1)S(1)} %get-tuple-element.26.m0), channel_id=1, source_target_pairs={{0,24},{8,16},{16,8},{24,0},{1,25},{9,17},{17,9},{25,1},{2,26},{10... | collective-permute-start | bytes 221192 | tf_op jit(solution)/shard_map/ppermute | solution.py:340
  6.6 0.5 %collective-permute-start.1 = (bf16[72,512]{1,0:T(8,128)(2,1)S(1)}, bf16[72,512]{1,0:T(8,128)(2,1)S(1)}, u32[]{:S(2)}, u32[]{:S(2)}) collective-permute-start(bf16[72,512]{1,0:T(8,128)(2,1)S(1)} %get-tuple-element.26.m0), channel_id=1, source_target_pairs={{0,16},{8,24},{16,0},{24,8},{1,17},{9,25},{17,1},{25,9},{2,18},{10... | collective-permute-start | bytes 221192 | tf_op jit(solution)/shard_map/ppermute | solution.py:340
  7.1 0.1 collective-permute-start
  7.3 0.0 copy-done
  7.3 2.2 %prep.1 = (bf16[1024,512]{1,0:T(8,128)(2,1)S(1)}, bf16[512,256]{1,0:T(8,128)(2,1)S(1)}, bf16[512,512]{1,0:T(8,128)(2,1)S(1)}, bf16[512,512]{1,0:T(8,128)(2,1)S(1...) custom-call(s32[4,4]{1,0:T(4,128)} %tids_hbm.1, s32[4,4]{1,0:T(4,128)} %offs_hbm.1, ...), custom_call_target="tpu_custom_call" | custom-call | flops 100000000 | bytes 3000000 | tf_op jit(solution)/shard_map/prep/pallas_call | solution.py:375
  9.5 0.0 collective-permute-done.2.m3
  9.5 1.5 %collective-permute-done.1.m2 = bf16[72,512]{1,0:T(8,128)(2,1)S(1)} collective-permute-done((bf16[72,512]{1,0:T(8,128)(2,1)S(1)}, bf16[72,512]{1,0:T(8,128)(2,1)S(1)}, u32[]{:S(2)}, u32[]{:S(2)}) %collective-permute-start.1) | collective-permute-done | bytes 73760 | tf_op jit(solution)/shard_map/ppermute | solution.py:340
  11.0 0.5 %collective-permute-done.m1 = bf16[72,512]{1,0:T(8,128)(2,1)S(1)} collective-permute-done((bf16[72,512]{1,0:T(8,128)(2,1)S(1)}, bf16[72,512]{1,0:T(8,128)(2,1)S(1)}, u32[]{:S(2)}, u32[]{:S(2)}) %collective-permute-start) | collective-permute-done | bytes 73760 | tf_op jit(solution)/shard_map/ppermute | solution.py:340
  11.5 0.4 %first.1 = (f32[64,512]{1,0:T(8,128)S(1)}, f32[8,512]{1,0:T(8,128)S(1)}, bf16[8,40,128]{2,1,0:T(8,128)(2,1)S(1)}) custom-call(bf16[72,512]{1,0:T(8,128)(2,1)S(1)} %get-tuple-element.26.m0, bf16[72,512]{1,0:T(8,128)(2,1)S(1)} %collective-permute-done.m1, bf16[72,512]{1,0:T(8,128)(2,1)S(1)} %collective-permute-done.1.m2, ...), custom_call_target="tpu_custom_call" | custom-call | tf_op jit(solution)/shard_map/first/pallas_call | solution.py:402
  11.9 10.8 %all_to_all.5.all_ref = bf16[8,40,128]{2,1,0:T(8,128)(2,1)S(1)} all-to-all(bf16[8,40,128]{2,1,0:T(8,128)(2,1)S(1)} %get-tuple-element.31), channel_id=1, replica_groups=mesh['det'=4,'tm'=8] {'tm'}, dimensions={0} | all-to-all | bytes 163840 | tf_op jit(solution)/shard_map/all_to_all | solution.py:414
  22.6 0.7 %second.1 = (f32[8,512]{1,0:T(8,128)S(1)}, bf16[1,16,128]{2,1,0:T(8,128)(2,1)S(1)}) custom-call(bf16[8,40,128]{2,1,0:T(8,128)(2,1)S(1)} %all_to_all.5.all_ref, f32[16,128]{1,0:T(8,128)S(1)} %get-tuple-element.32.own_ref, f32[8,512]{1,0:T(8,128)S(1)} %get-tuple-element.33.vec_ref, bf16[512,256]{1,0:T(8,128)(2,1)S(1)} %get-tuple-element.28.toep_ref, ...), custom_call_target="tpu_custom_call" | custom-call | tf_op jit(solution)/shard_map/second/pallas_call | solution.py:417
  23.3 0.0 collective-permute-start.3
  23.3 0.6 %early.1 = (bf16[256,512]{1,0:T(8,128)(2,1)S(1)}, f32[128,128]{1,0:T(8,128)S(1)}, f32[128,128]{1,0:T(8,128)S(1)}, bf16[1,128,128]{2,1,0:T(8,128)(2,1)S(1)}) custom-call(f32[512,512]{1,0:T(8,128)S(1)} %get-tuple-element.36.ts_ref, bf16[512,512]{1,0:T(8,128)(2,1)S(1)} %get-tuple-element.37.keep_ref, f32[1,512]{1,0:T(1,128)S(1)} %get-tuple-element.38.g_ref, ...), custom_call_target="tpu_custom_call" | custom-call | flops 500000000 | bytes 2000000 | tf_op jit(solution)/shard_map/early/pallas_call | solution.py:431
  23.9 0.6 %collective-permute-done.3 = bf16[1,16,128]{2,1,0:T(8,128)(2,1)S(1)} collective-permute-done((bf16[1,16,128]{2,1,0:T(8,128)(2,1)S(1)}, bf16[1,16,128]{2,1,0:T(8,128)(2,1)S(1)}, u32[]{:S(2)}, u32[]{:S(2)}) %collective-permute-start.3) | collective-permute-done | bytes 4128 | tf_op jit(solution)/shard_map/ppermute | solution.py:427
  24.5 1.1 %collective-permute-start.5 = (bf16[2,16,128]{2,1,0:T(8,128)(2,1)S(1)}, bf16[2,16,128]{2,1,0:T(8,128)(2,1)S(1)}, u32[]{:S(2)}, u32[]{:S(2)}) collective-permute-start(bf16[2,16,128]{2,1,0:T(8,128)(2,1)S(1)} %constant_dynamic-update-slice_fusion.send_ref), channel_id=1, source_target_pairs={{0,6},{1,5},{2,4},{3,7},{4,2},{5,1},{6,0},{7,3},{8,14},{9,13},{10,... | collective-permute-start | bytes 24584 | tf_op jit(solution)/shard_map/ppermute | solution.py:449
  25.5 0.0 collective-permute-start.4
  25.6 4.4 %collective-permute-done.5.far_ref.after_ref = bf16[2,16,128]{2,1,0:T(8,128)(2,1)S(1)} collective-permute-done((bf16[2,16,128]{2,1,0:T(8,128)(2,1)S(1)}, bf16[2,16,128]{2,1,0:T(8,128)(2,1)S(1)}, u32[]{:S(2)}, u32[]{:S(2)}) %collective-permute-start.5) | collective-permute-done | bytes 8224 | tf_op jit(solution)/shard_map/ppermute | solution.py:449
  29.9 0.0 collective-permute-start.6
  30.0 1.3 %late.1 = bf16[512,512]{1,0:T(8,128)(2,1)} custom-call(f32[512,512]{1,0:T(8,128)S(1)} %get-tuple-element.36.ts_ref, bf16[512,512]{1,0:T(8,128)(2,1)S(1)} %get-tuple-element.37.keep_ref, f32[1,512]{1,0:T(1,128)S(1)} %get-tuple-element.38.g_ref, bf16[512,128]{1,0:T(8,128)(2,1)S(1)} %get-tuple-element.39.v3_ref, f32[64,512]{1,0:T(8,128)S(1)} %get-tuple-element.40.bq_ref, ...), custom_call_target="tpu_custom_call" | custom-call | flops 500000000 | bytes 2000000 | tf_op jit(solution)/shard_map/late/pallas_call | solution.py:455
  31.3 0.0 collective-permute-done.4.near_ref
  31.3 0.0 collective-permute-done.6.mate_ref
  31.3 0.8 %tile.1 = f32[1,128,128]{2,1,0:T(8,128)} custom-call(bf16[2,16,128]{2,1,0:T(8,128)(2,1)S(1)} %constant_dynamic-update-slice_fusion.send_ref, bf16[2,16,128]{2,1,0:T(8,128)(2,1)S(1)} %collective-permute-done.4.near_ref, bf16[2,16,128]{2,1,0:T(8,128)(2,1)S(1)} %collective-permute-done.5.far_ref.after_ref, ...), custom_call_target="tpu_custom_call" | custom-call | tf_op jit(solution)/shard_map/tile/pallas_call | solution.py:466
  (3 shorter events, 0.0 us)
Async XLA Ops:
  0.6 6.6 %copy-start = (f32[257]{0:T(512)S(1)}, f32[257]{0:T(512)}, u32[]{:S(2)}) copy-start(f32[257]{0:T(512)} %param.18) | copy-start | bytes 3088
  2.6 6.9 %collective-permute-start.2 = (bf16[72,512]{1,0:T(8,128)(2,1)S(1)}, bf16[72,512]{1,0:T(8,128)(2,1)S(1)}, u32[]{:S(2)}, u32[]{:S(2)}) collective-permute-start(bf16[72,512]{1,0:T(8,128)(2,1)S(1)} %get-tuple-element.26.m0), channel_id=1, source_target_pairs={{0,24},{8,16},{16,8},{24,0},{1,25},{9,17},{17,9},{25,1},{2,26},{10... | collective-permute-start | bytes 221192 | tf_op jit(solution)/shard_map/ppermute | solution.py:340
  6.6 4.4 %collective-permute-start.1 = (bf16[72,512]{1,0:T(8,128)(2,1)S(1)}, bf16[72,512]{1,0:T(8,128)(2,1)S(1)}, u32[]{:S(2)}, u32[]{:S(2)}) collective-permute-start(bf16[72,512]{1,0:T(8,128)(2,1)S(1)} %get-tuple-element.26.m0), channel_id=1, source_target_pairs={{0,16},{8,24},{16,0},{24,8},{1,17},{9,25},{17,1},{25,9},{2,18},{10... | collective-permute-start | bytes 221192 | tf_op jit(solution)/shard_map/ppermute | solution.py:340
  7.1 4.4 %collective-permute-start = (bf16[72,512]{1,0:T(8,128)(2,1)S(1)}, bf16[72,512]{1,0:T(8,128)(2,1)S(1)}, u32[]{:S(2)}, u32[]{:S(2)}) collective-permute-start(bf16[72,512]{1,0:T(8,128)(2,1)S(1)} %get-tuple-element.26.m0), channel_id=1, source_target_pairs={{0,8},{8,0},{16,24},{24,16},{1,9},{9,1},{17,25},{25,17},{2,10},{10... | collective-permute-start | bytes 221192 | tf_op jit(solution)/shard_map/ppermute | solution.py:340
  23.3 1.2 %collective-permute-start.3 = (bf16[1,16,128]{2,1,0:T(8,128)(2,1)S(1)}, bf16[1,16,128]{2,1,0:T(8,128)(2,1)S(1)}, u32[]{:S(2)}, u32[]{:S(2)}) collective-permute-start(bf16[1,16,128]{2,1,0:T(8,128)(2,1)S(1)} %get-tuple-element.35), channel_id=1, source_target_pairs={{0,1},{1,0},{2,3},{3,2},{4,5},{5,4},{6,7},{7,6},{8,9},{9,8},{10,11... | collective-permute-start | bytes 12296 | tf_op jit(solution)/shard_map/ppermute | solution.py:427
  24.5 5.4 %collective-permute-start.5 = (bf16[2,16,128]{2,1,0:T(8,128)(2,1)S(1)}, bf16[2,16,128]{2,1,0:T(8,128)(2,1)S(1)}, u32[]{:S(2)}, u32[]{:S(2)}) collective-permute-start(bf16[2,16,128]{2,1,0:T(8,128)(2,1)S(1)} %constant_dynamic-update-slice_fusion.send_ref), channel_id=1, source_target_pairs={{0,6},{1,5},{2,4},{3,7},{4,2},{5,1},{6,0},{7,3},{8,14},{9,13},{10,... | collective-permute-start | bytes 24584 | tf_op jit(solution)/shard_map/ppermute | solution.py:449
  25.5 5.7 %collective-permute-start.4 = (bf16[2,16,128]{2,1,0:T(8,128)(2,1)S(1)}, bf16[2,16,128]{2,1,0:T(8,128)(2,1)S(1)}, u32[]{:S(2)}, u32[]{:S(2)}) collective-permute-start(bf16[2,16,128]{2,1,0:T(8,128)(2,1)S(1)} %constant_dynamic-update-slice_fusion.send_ref), channel_id=1, source_target_pairs={{0,2},{1,3},{2,0},{3,1},{4,6},{5,7},{6,4},{7,5},{8,10},{9,11},{10,... | collective-permute-start | bytes 24584 | tf_op jit(solution)/shard_map/ppermute | solution.py:448
  29.9 1.3 %collective-permute-start.6 = (bf16[2,16,128]{2,1,0:T(8,128)(2,1)S(1)}, bf16[2,16,128]{2,1,0:T(8,128)(2,1)S(1)}, u32[]{:S(2)}, u32[]{:S(2)}) collective-permute-start(bf16[2,16,128]{2,1,0:T(8,128)(2,1)S(1)} %collective-permute-done.5.far_ref.after_ref), channel_id=1, source_target_pairs={{0,1},{1,0},{2,3},{3,2},{4,5},{5,4},{6,7},{7,6},{8,9},{9,8},{10,11... | collective-permute-start | bytes 24584 | tf_op jit(solution)/shard_map/ppermute | solution.py:450

commit v5 on v4

--- a/solution.py
+++ b/solution.py
@@ -82,7 +82,7 @@
 
 
 def prep_kernel(seg, kblk, lane_blocks, digits, tids_hbm, offs_hbm, owner_hbm, cos_hbm, point_hbm, gain_ref, v_ref,
-                h2_ref, toep_ref, pn_ref, pt_ref, v3_ref, geo_ref, own_ref,
+                h2_ref, toep_ref, pnt_ref, v3_ref, geo_ref, own_ref,
                 tids_ref, offs_ref, owner_ref, cos_ref, point_ref, wide_ref, sem):
     streams = [(cos_hbm, cos_ref), (point_hbm, point_ref), (tids_hbm, tids_ref), (offs_hbm, offs_ref),
                (owner_hbm, owner_ref)]
@@ -128,8 +128,8 @@
             j = k * seg + s
             p = point_ref[s, k]
             span, tile = p.shape
-            pn_ref[s * span : (s + 1) * span, k * tile : (k + 1) * tile] = p
-            pt_ref[k * tile : (k + 1) * tile, s * span : (s + 1) * span] = p.T
+            pnt_ref[s * span : (s + 1) * span, k * tile : (k + 1) * tile] = p
+            pnt_ref[flen + k * tile : flen + (k + 1) * tile, s * span : (s + 1) * span] = p.T
             p = p.astype(F32)
             squares = jnp.where(row16 == j, jnp.sum(p * p, axis=0, keepdims=True), squares)
             target = owner_ref[tids_ref[s, k]] * LANES + offs_ref[s, k]
@@ -145,27 +145,32 @@
     own_ref[...] = own
 
 
-def filtered(b, toep_ref):
-    flen = b.shape[1]
-    blocks = flen // LANES
-    rows = -(-2 * blocks // EXT) * EXT
-    hi, lo = split(b)
-    hi, lo = hi.astype(F32), lo.astype(F32)
+def filtered(vectors, toep_ref):
+    blocks = vectors[0].shape[1] // LANES
+    rows = -(-2 * blocks * len(vectors) // EXT) * EXT
     row = iota((rows, LANES), 0)
+    halves = []
+    for b in vectors:
+        hi, lo = split(b)
+        halves += [hi.astype(F32), lo.astype(F32)]
     left = []
     for c in range(blocks):
         block = jnp.zeros((rows, LANES), F32)
-        for m in range(blocks):
-            at = slice(m * LANES, (m + 1) * LANES)
-            a = (m + c) % blocks
-            block = jnp.where(row == a, hi[:, at], jnp.where(row == blocks + a, lo[:, at], block))
+        for i, half in enumerate(halves):
+            for m in range(blocks):
+                to = i * blocks + (m + c) % blocks
+                block = jnp.where(row == to, half[:, m * LANES : (m + 1) * LANES], block)
         left.append(block.astype(BF16))
     z = mm(jnp.concatenate(left, axis=1), toep_ref[...])
     z = z[:, 0:LANES] + z[:, LANES:]
-    return z[0:blocks] + z[blocks : 2 * blocks]
-
-
-def project(z, pn_ref, seg, kblk):
+    out = []
+    for i in range(len(vectors)):
+        at = 2 * i * blocks
+        out.append(z[at : at + blocks] + z[at + blocks : at + 2 * blocks])
+    return out
+
+
+def project(z, pn, seg, kblk):
     listed = seg * kblk
     hi, lo = split(z)
     hi, lo = hi.astype(F32), lo.astype(F32)
@@ -174,7 +179,7 @@
     for s in range(seg):
         value = jnp.where(row < listed, hi[s : s + 1], lo[s : s + 1])
         left.append(jnp.where(row % seg == s, value, 0.0).astype(BF16))
-    out = mm(jnp.concatenate(left, axis=1), pn_ref[...])
+    out = mm(jnp.concatenate(left, axis=1), pn)
     out = out[:listed] + out[listed:]
     row = iota((listed, LANES), 0)
     proj = out[:, 0:LANES]
@@ -183,7 +188,7 @@
     return proj
 
 
-def first_kernel(modes, seg, kblk, m0, m1, m2, m3, toep_ref, pn_ref, geo_ref,
+def first_kernel(modes, seg, kblk, m0, m1, m2, m3, toep_ref, pnt_ref, geo_ref,
                  bq_ref, vec_ref, send_ref):
     tot = m0[...].astype(F32) + m1[...].astype(F32) + m2[...].astype(F32) + m3[...].astype(F32)
     bq_ref[...] = tot[0 : 2 * modes]
@@ -195,13 +200,21 @@
     b2 = ext[2:3] + ext[3:4] - jnp.sum(u_col * tot[modes : 2 * modes], axis=0, keepdims=True)
     row = iota((8, b1.shape[1]), 0)
     vec_ref[...] = jnp.where(row == 0, b1, jnp.where(row == 1, b2, jnp.where(row == 2, square, 0.0)))
-    z = filtered(b1, toep_ref)
-    proj = project(z, pn_ref, seg, kblk).astype(BF16)
+    (z,) = filtered([b1], toep_ref)
+    proj = project(z, pnt_ref[0 : b1.shape[1]], seg, kblk).astype(BF16)
     geo = geo_ref[...]
     listed = seg * kblk
     for t in range(send_ref.shape[0]):
         send_ref[t, 0:listed] = proj
-        send_ref[t, listed:] = geo
+        send_ref[t, listed : listed + geo.shape[0]] = geo
+    if send_ref.shape[1] > listed + geo.shape[0]:
+        blocks = b1.shape[1] // LANES
+        row = iota((4 * blocks, LANES), 0)
+        tail = jnp.zeros((4 * blocks, LANES), F32)
+        for i, half in enumerate(split(b1) + split(b2)):
+            for m in range(blocks):
+                tail = jnp.where(row == i * blocks + m, half[:, m * LANES : (m + 1) * LANES].astype(F32), tail)
+        send_ref[0, listed + geo.shape[0] :] = tail.astype(BF16)
 
 
 def lane_ids(all_ref, listed, blocks, digits, b):
@@ -212,32 +225,86 @@
     return out
 
 
-def second_kernel(seg, kblk, digits, all_ref, own_ref, vec_ref, toep_ref, pn_ref, pt_ref, sig_ref, send_ref):
-    listed = seg * kblk
-    blocks = all_ref.shape[0] * listed // LANES
-    samples = vec_ref.shape[1]
+def fetch(all_ref, own, vec_ref, listed, blocks, digits):
     per = LANES // listed
-    own = own_ref[...]
-    psum = jnp.zeros((listed, LANES), F32)
-    wsum = jnp.zeros((listed, LANES), F32)
+    psum = jnp.zeros((own.shape[0], LANES), F32)
+    wsum = jnp.zeros((own.shape[0], LANES), F32)
     for b in range(blocks):
         same = (own == lane_ids(all_ref, listed, blocks, digits, b)).astype(F32).astype(BF16)
         part = all_ref[b * per : (b + 1) * per]
         psum = psum + mm(same, part[:, 0:listed].reshape(LANES, LANES))
         wsum = wsum + mm(same, part[:, listed : 2 * listed].reshape(LANES, LANES))
-    square = vec_ref[2:3, 0:LANES]
-    fetched = (psum / (1.0 + square * wsum)).astype(BF16)
+    return (psum / (1.0 + vec_ref[2:3, 0:LANES] * wsum)).astype(BF16).astype(F32)
+
+
+def signal(fetched, pt, seg, kblk):
+    samples = pt.shape[1]
+    listed = seg * kblk
     row = iota((listed, LANES), 0)
-    wide = [jnp.where(row // seg == k, fetched.astype(F32), 0.0).astype(BF16) for k in range(kblk)]
-    spread = mm(jnp.concatenate(wide, axis=1), pt_ref[...])
+    wide = [jnp.where(row // seg == k, fetched, 0.0).astype(BF16) for k in range(kblk)]
+    spread = mm(jnp.concatenate(wide, axis=1), pt)
     row = iota((listed, samples), 0)
     lane = iota((listed, samples), 1)
-    sig = jnp.sum(jnp.where(lane // (samples // seg) == row % seg, spread, 0.0), axis=0, keepdims=True)
+    return jnp.sum(jnp.where(lane // (samples // seg) == row % seg, spread, 0.0), axis=0, keepdims=True)
+
+
+def second_kernel(seg, kblk, digits, all_ref, own_ref, vec_ref, toep_ref, pnt_ref, sig_ref, send_ref):
+    listed = seg * kblk
+    blocks = all_ref.shape[0] * listed // LANES
+    samples = vec_ref.shape[1]
+    fetched = fetch(all_ref, own_ref[...], vec_ref, listed, blocks, digits)
+    sig = signal(fetched, pnt_ref[samples:], seg, kblk)
     sig_ref[...] = jnp.broadcast_to(sig, sig_ref.shape)
-    z = filtered(vec_ref[0:1] - vec_ref[1:2] * sig, toep_ref)
-    proj = project(z, pn_ref, seg, kblk).astype(BF16)
+    (z,) = filtered([vec_ref[0:1] - vec_ref[1:2] * sig], toep_ref)
+    proj = project(z, pnt_ref[0:samples], seg, kblk).astype(BF16)
     for t in range(send_ref.shape[0]):
         send_ref[t] = proj
+
+
+def assemble(pair_ref, near_ref, far_ref, cross_ref, all_ref):
+    t = lax.axis_index("tm")
+    core = t % 2
+    far, other = 6 - 2 * core, 4 + 2 * core
+    arrived = [
+        (pair_ref, t),
+        (near_ref, jnp.bitwise_xor(t, 2)),
+        (far_ref, jnp.bitwise_xor(t, far)),
+        (cross_ref, jnp.bitwise_xor(jnp.bitwise_xor(t, 1), other)),
+    ]
+    for ref, at in arrived:
+        all_ref[at] = ref[0]
+        all_ref[jnp.bitwise_xor(at, 1)] = ref[1]
+
+
+def pair_second_kernel(seg, kblk, digits, pair_ref, near_ref, far_ref, cross_ref, mate_ref, vec_ref, toep_ref, pnt_ref,
+                       mate_pnt_ref, all_ref, sig_ref, send_ref):
+    assemble(pair_ref, near_ref, far_ref, cross_ref, all_ref)
+    listed = seg * kblk
+    blocks = all_ref.shape[0] * listed // LANES
+    samples = vec_ref.shape[1]
+    t = lax.axis_index("tm")
+    mate = t + 1 - 2 * (t % 2)
+    row = iota((2 * listed, LANES), 0)
+    listing = jnp.where(row < listed, t * listed + row, mate * listed + row - listed)
+    lane = iota((2 * listed, LANES), 1)
+    own = jnp.zeros((2 * listed, 1), F32)
+    for b in range(blocks):
+        ids = lane_ids(all_ref, listed, blocks, digits, b)
+        own = own + jnp.sum(jnp.where(listing == lane + b * LANES, ids, 0.0), axis=1, keepdims=True)
+    fetched = fetch(all_ref, own, vec_ref, listed, blocks, digits)
+    sig = signal(fetched[0:listed], pnt_ref[samples:], seg, kblk)
+    mate_sig = signal(fetched[listed:], mate_pnt_ref[samples:], seg, kblk)
+    sig_ref[...] = jnp.broadcast_to(sig, sig_ref.shape)
+    rest = vec_ref[0:1] - vec_ref[1:2] * sig
+    cuts = samples // LANES
+    tail = mate_ref[0, pair_ref.shape[1] :].astype(F32)
+    halves = [
+        jnp.concatenate([tail[i * cuts + m : i * cuts + m + 1] for m in range(cuts)], axis=1) for i in range(4)
+    ]
+    mate_rest = halves[0] + halves[1] - (halves[2] + halves[3]) * mate_sig
+    z, mate_z = filtered([rest, mate_rest], toep_ref)
+    send_ref[0] = project(z, pnt_ref[0:samples], seg, kblk).astype(BF16)
+    send_ref[1] = project(mate_z, mate_pnt_ref[0:samples], seg, kblk).astype(BF16)
 
 
 def clean_rows(modes, at, ts_ref, keep_ref, g_ref, v3_ref, bq_ref, sig_ref, h2_ref):
@@ -301,20 +368,8 @@
     out_ref[0] = base_ref[...] + psum * scale_ref[...]
 
 
-def pair_tile_kernel(send_ref, near_ref, far_ref, mate_ref, base_ref, scale_ref, same_ref, out_ref, all_ref):
-    t = lax.axis_index("tm")
-    core = t % 2
-    far, other = 6 - 2 * core, 4 + 2 * core
-    mate = jnp.bitwise_xor(t, 1)
-    arrived = [
-        (send_ref, t),
-        (near_ref, jnp.bitwise_xor(t, 2)),
-        (far_ref, jnp.bitwise_xor(t, far)),
-        (mate_ref, jnp.bitwise_xor(mate, other)),
-    ]
-    for ref, at in arrived:
-        all_ref[at] = ref[0]
-        all_ref[jnp.bitwise_xor(at, 1)] = ref[1]
+def pair_tile_kernel(pair_ref, near_ref, far_ref, cross_ref, base_ref, scale_ref, same_ref, out_ref, all_ref):
+    assemble(pair_ref, near_ref, far_ref, cross_ref, all_ref)
     blocks, per = same_ref.shape[0], LANES // all_ref.shape[1]
     psum = jnp.zeros((LANES, LANES), F32)
     for b in range(blocks):
@@ -372,15 +427,14 @@
 
     rows = -(-filter_gain.shape[0] // LANES) * LANES
     inputs = (tile_ids, block_offsets, tile_owner, jnp.asarray(cosine_table(samples, rows)), pointing)
-    h2, toep, pn, pt, v3, geo, own = pl.pallas_call(
+    h2, toep, pnt, v3, geo, own = pl.pallas_call(
         functools.partial(prep_kernel, seg, kblk, lane_blocks, digits),
         in_specs=[HB] * 5 + [VM] * 2,
-        out_specs=[VM] * 7,
+        out_specs=[VM] * 6,
         out_shape=[
             shape((2 * samples, samples), BF16),
             shape((samples, 2 * LANES), BF16),
-            shape((samples, kblk * LANES), BF16),
-            shape((kblk * LANES, samples), BF16),
+            shape((2 * samples, samples), BF16),
             shape((dets, LANES), BF16),
             shape((listed + id_rows, LANES), BF16),
             shape((listed, LANES)),
@@ -399,32 +453,57 @@
         name="prep",
     )(*(pltpu.with_memory_space_constraint(x, pltpu.HBM) for x in inputs), filter_gain.reshape(1, -1), vt)
 
+    paired = n_tm == 8
+    mates = [(i, i ^ 1) for i in range(n_tm)]
+
+    def spread(pair):
+        near = lax.ppermute(pair, "tm", [(i, i ^ 2) for i in range(n_tm)])
+        far = lax.ppermute(pair, "tm", [(i, i ^ (6 - 2 * (i % 2))) for i in range(n_tm)])
+        return pair, near, far, lax.ppermute(far, "tm", mates)
+
+    block = 2 * listed + id_rows
+    first_shape = (1, block + 4 * samples // LANES, LANES) if paired else (n_tm, block, LANES)
     bq, vec, send = pl.pallas_call(
         functools.partial(first_kernel, modes, seg, kblk),
         in_specs=[VM] * 7,
         out_specs=[VM] * 3,
-        out_shape=[
-            shape((2 * modes, samples)),
-            shape((8, samples)),
-            shape((n_tm, 2 * listed + id_rows, LANES), BF16),
-        ],
+        out_shape=[shape((2 * modes, samples)), shape((8, samples)), shape(first_shape, BF16)],
         compiler_params=GRANT,
         name="first",
-    )(*parts_of_all, toep, pn, geo)
-    everyone = lax.all_to_all(send, "tm", 0, 0)
-
-    paired = n_tm == 8
-    sig, send = pl.pallas_call(
-        functools.partial(second_kernel, seg, kblk, digits),
-        in_specs=[VM] * 6,
-        out_specs=[VM] * 2,
-        out_shape=[shape((8, samples)), shape((1 if paired else n_tm, listed, LANES), BF16)],
-        compiler_params=GRANT,
-        name="second",
-    )(everyone, own, vec, toep, pn, pt)
-    mates = [(i, i ^ 1) for i in range(n_tm)]
+    )(*parts_of_all, toep, pnt, geo)
     if paired:
         mate = lax.ppermute(send, "tm", mates)
+        pair = jnp.concatenate([send[:, :block], mate[:, :block]], axis=0)
+        late_pnt, pair = lax.optimization_barrier((pnt, pair))
+        arrived = spread(pair)
+        mate_pnt = lax.ppermute(late_pnt, "tm", mates)
+        everyone, sig, send = pl.pallas_call(
+            functools.partial(pair_second_kernel, seg, kblk, digits),
+            in_specs=[VM] * 9,
+            out_specs=[VM] * 3,
+            out_shape=[
+                shape((n_tm, block, LANES), BF16),
+                shape((8, samples)),
+                shape((2, listed, LANES), BF16),
+            ],
+            compiler_params=GRANT,
+            name="second",
+        )(*arrived, mate, vec, toep, pnt, mate_pnt)
+        arrived = spread(send)
+        after = arrived[2]
+        last, scratch = pair_tile_kernel, [pltpu.VMEM((n_tm, listed, LANES), BF16)]
+    else:
+        everyone = lax.all_to_all(send, "tm", 0, 0)
+        sig, send = pl.pallas_call(
+            functools.partial(second_kernel, seg, kblk, digits),
+            in_specs=[VM] * 5,
+            out_specs=[VM] * 2,
+            out_shape=[shape((8, samples)), shape((n_tm, listed, LANES), BF16)],
+            compiler_params=GRANT,
+            name="second",
+        )(everyone, own, vec, toep, pnt)
+        arrived = (lax.all_to_all(send, "tm", 0, 0),)
+        after, last, scratch = vec, tile_kernel, []
 
     cut = EARLY * dets // 4
     operands = (ts, keep, g, v3, bq, sig, h2)
@@ -442,16 +521,6 @@
         compiler_params=GRANT,
         name="early",
     )(*operands, everyone, vec)
-    if paired:
-        mate, early, base = lax.optimization_barrier((mate, early, base))
-        both = jnp.concatenate([send, mate], axis=0)
-        near = lax.ppermute(both, "tm", [(i, i ^ 2) for i in range(n_tm)])
-        after = lax.ppermute(both, "tm", [(i, i ^ (6 - 2 * (i % 2))) for i in range(n_tm)])
-        arrived = (both, near, after, lax.ppermute(after, "tm", mates))
-        last, scratch = pair_tile_kernel, [pltpu.VMEM((n_tm, listed, LANES), BF16)]
-    else:
-        arrived = (lax.all_to_all(send, "tm", 0, 0),)
-        after, last, scratch = vec, tile_kernel, []
     cleaned = pl.pallas_call(
         functools.partial(late_kernel, modes),
         in_specs=[VM] * 9,

time: 32.3 us -> 29.3 us (0.907)
  blocking collectives: 10.8 us -> 0 us
  starting transfers between devices: 5.69 us -> 11.4 us
  waiting for transfers between devices: 6.92 us -> 8.14 us
  Pallas kernels: 7.97 us -> 8.84 us
    all_to_all x1 -> x0, blocking collectives: 10.8 us -> none  [shards(): everyone = lax.all_to_all(send, 'tm', 0, 0)]
    ppermute x3 -> x7, starting transfers between devices: 1.06 us -> 6.8 us  [the longest x2 6.61 us: spread(): lax.ppermute(pair, 'tm', [(i, i ^ 6 - 2 * (i % 2)) for i in range(n_tm)])]
    ppermute x3 -> x7, waiting for transfers between devices: 4.4 us -> 5.64 us  [the longest x2 3.92 us: spread(): lax.ppermute(pair, 'tm', [(i, i ^ 6 - 2 * (i % 2)) for i in range(n_tm)])]
    pallas_call x1, Pallas kernels: 2.23 us -> 2.87 us  [shards(): pl.pallas_call(functools.partial(prep_kernel, seg, kblk, lane_blocks, dig...]
    ppermute x3, waiting for transfers between devices: 1.97 us -> 1.33 us  [others(): return [lax.ppermute(x, axis, p) for p in pairs]]
    ppermute x1, waiting for transfers between devices: 0.55 us -> 1.18 us  [shards(): mate = lax.ppermute(send, 'tm', mates)]
  transfers between devices with their start and end apart: 7 -> 11, of which waited for: 4 -> 6; matrix products, arithmetic and copies ran while one was open for 0% -> 0% of each run, Pallas kernels for 13% -> 16%
where the time goes in v5:
time: 29.3 us; the launch traced here: 29.2 us
  starting transfers between devices  11.4 us (39%)
  Pallas kernels  8.84 us (30%)
  waiting for transfers between devices  8.14 us (28%)
  between operations  0.72 us (2%)
    ppermute x2, starting transfers between devices, spread(): lax.ppermute(pair, 'tm', [(i, i ^ 6 - 2 * (i % 2)) for i in range(n_tm)])  6.61 us
    ppermute x3, starting transfers between devices, others(): return [lax.ppermute(x, axis, p) for p in pairs]  4.63 us
    ppermute x2, waiting for transfers between devices, spread(): lax.ppermute(pair, 'tm', [(i, i ^ 6 - 2 * (i % 2)) for i in range(n_tm)])  3.92 us
    pallas_call x1, Pallas kernels, shards(): pl.pallas_call(functools.partial(prep_kernel, seg, kblk, lane_blocks, dig...  2.87 us
    pallas_call x1, Pallas kernels, shards(): pl.pallas_call(functools.partial(sums_kernel, modes), in_specs=[HB] * 4,...  1.99 us
    ppermute x2, waiting for transfers between devices, spread(): near = lax.ppermute(pair, 'tm', [(i, i ^ 2) for i in range(n_tm)])  1.71 us
    ppermute x3, waiting for transfers between devices, others(): return [lax.ppermute(x, axis, p) for p in pairs]  1.33 us
    pallas_call x1, Pallas kernels, shards(): pl.pallas_call(functools.partial(late_kernel, modes), in_specs=[VM] * 9,...  1.29 us
  transfers between devices with their start and end apart: 11, of which 6 were waited for; matrix products, arithmetic and copies ran while one was open for 0% of the time, Pallas kernels for 16%

profile of v5, /device:TPU:0, one launch (start us, length us, event | category | flops | bytes accessed | tf_op | source)
XLA Modules:
  0.0 29.2 jit_solution(13449002535907227494)
XLA Ops:
  0.6 0.0 copy-start
  0.6 2.0 %sums.1 = (bf16[72,512]{1,0:T(8,128)(2,1)S(1)}, f32[512,512]{1,0:T(8,128)S(1)}, bf16[512,512]{1,0:T(8,128)(2,1)S(1)}, f32[32,512]{1,0:T(8,128)S(1)}, f32[1,512]{1,0:T(1,128)S(1)}) custom-call(f32[512,512]{1,0:T(8,128)} %ts_hbm.1, s32[512,512]{1,0:T(8,128)} %flag_hbm.1, f32[32,512]{1,0:T(8,128)} %bitcast.2, f32[1,512]{1,0:T(1,128)} %bitcast.3), custom_call_target="tpu_custom_call" | custom-call | tf_op jit(solution)/shard_map/sums/pallas_call | solution.py:408
  2.6 4.0 %collective-permute-start.2 = (bf16[72,512]{1,0:T(8,128)(2,1)S(1)}, bf16[72,512]{1,0:T(8,128)(2,1)S(1)}, u32[]{:S(2)}, u32[]{:S(2)}) collective-permute-start(bf16[72,512]{1,0:T(8,128)(2,1)S(1)} %get-tuple-element.26.m0), channel_id=1, source_target_pairs={{0,24},{8,16},{16,8},{24,0},{1,25},{9,17},{17,9},{25,1},{2,26},{10... | collective-permute-start | bytes 221192 | tf_op jit(solution)/shard_map/ppermute | solution.py:395
  6.6 0.5 %collective-permute-start.1 = (bf16[72,512]{1,0:T(8,128)(2,1)S(1)}, bf16[72,512]{1,0:T(8,128)(2,1)S(1)}, u32[]{:S(2)}, u32[]{:S(2)}) collective-permute-start(bf16[72,512]{1,0:T(8,128)(2,1)S(1)} %get-tuple-element.26.m0), channel_id=1, source_target_pairs={{0,16},{8,24},{16,0},{24,8},{1,17},{9,25},{17,1},{25,9},{2,18},{10... | collective-permute-start | bytes 221192 | tf_op jit(solution)/shard_map/ppermute | solution.py:395
  7.1 0.1 collective-permute-start
  7.3 0.0 copy-done
  7.3 2.9 %prep.1 = (bf16[1024,512]{1,0:T(8,128)(2,1)S(1)}, bf16[512,256]{1,0:T(8,128)(2,1)S(1)}, bf16[1024,512]{1,0:T(8,128)(2,1)S(1)}, bf16[512,128]{1,0:T(8,128)(2,1)S(...) custom-call(s32[4,4]{1,0:T(4,128)} %tids_hbm.1, s32[4,4]{1,0:T(4,128)} %offs_hbm.1, s32[32]{0:T(128)} %owner_hbm.1, ...), custom_call_target="tpu_custom_call" | custom-call | flops 100000000 | bytes 3000000 | tf_op jit(solution)/shard_map/prep/pallas_call | solution.py:430
  10.2 0.0 collective-permute-done.2.m3
  10.2 0.8 %collective-permute-done.1.m2 = bf16[72,512]{1,0:T(8,128)(2,1)S(1)} collective-permute-done((bf16[72,512]{1,0:T(8,128)(2,1)S(1)}, bf16[72,512]{1,0:T(8,128)(2,1)S(1)}, u32[]{:S(2)}, u32[]{:S(2)}) %collective-permute-start.1) | collective-permute-done | bytes 73760 | tf_op jit(solution)/shard_map/ppermute | solution.py:395
  11.0 0.5 %collective-permute-done.m1 = bf16[72,512]{1,0:T(8,128)(2,1)S(1)} collective-permute-done((bf16[72,512]{1,0:T(8,128)(2,1)S(1)}, bf16[72,512]{1,0:T(8,128)(2,1)S(1)}, u32[]{:S(2)}, u32[]{:S(2)}) %collective-permute-start) | collective-permute-done | bytes 73760 | tf_op jit(solution)/shard_map/ppermute | solution.py:395
  11.5 0.4 %first.1 = (f32[64,512]{1,0:T(8,128)S(1)}, f32[8,512]{1,0:T(8,128)S(1)}, bf16[1,56,128]{2,1,0:T(8,128)(2,1)S(1)}) custom-call(bf16[72,512]{1,0:T(8,128)(2,1)S(1)} %get-tuple-element.26.m0, bf16[72,512]{1,0:T(8,128)(2,1)S(1)} %collective-permute-done.m1, bf16[72,512]{1,0:T(8,128)(2,1)S(1)} %collective-permute-done.1.m2, ...), custom_call_target="tpu_custom_call" | custom-call | tf_op jit(solution)/shard_map/first/pallas_call | solution.py:466
  11.9 0.0 collective-permute-start.3
  11.9 1.2 %collective-permute-done.3.mate_ref = bf16[1,56,128]{2,1,0:T(8,128)(2,1)S(1)} collective-permute-done((bf16[1,56,128]{2,1,0:T(8,128)(2,1)S(1)}, bf16[1,56,128]{2,1,0:T(8,128)(2,1)S(1)}, u32[]{:S(2)}, u32[]{:S(2)}) %collective-permute-start.3) | collective-permute-done | bytes 14368 | tf_op jit(solution)/shard_map/ppermute | solution.py:475
  13.1 0.2 collective-permute-start.7
  13.3 3.6 %collective-permute-start.5 = (bf16[2,40,128]{2,1,0:T(8,128)(2,1)S(1)}, bf16[2,40,128]{2,1,0:T(8,128)(2,1)S(1)}, u32[]{:S(2)}, u32[]{:S(2)}) collective-permute-start(bf16[2,40,128]{2,1,0:T(8,128)(2,1)S(1)} %pad_maximum_fusion.pair_ref), channel_id=1, source_target_pairs={{0,6},{1,5},{2,4},{3,7},{4,2},{5,1},{6,0},{7,3},{8,14},{9,13},{10,... | collective-permute-start | bytes 61448 | tf_op jit(solution)/shard_map/ppermute | solution.py:461
  16.9 0.0 collective-permute-start.4
  16.9 2.1 %collective-permute-done.5.far_ref = bf16[2,40,128]{2,1,0:T(8,128)(2,1)S(1)} collective-permute-done((bf16[2,40,128]{2,1,0:T(8,128)(2,1)S(1)}, bf16[2,40,128]{2,1,0:T(8,128)(2,1)S(1)}, u32[]{:S(2)}, u32[]{:S(2)}) %collective-permute-start.5) | collective-permute-done | bytes 20512 | tf_op jit(solution)/shard_map/ppermute | solution.py:461
  19.0 0.0 collective-permute-start.6
  19.0 1.7 %collective-permute-done.4.near_ref = bf16[2,40,128]{2,1,0:T(8,128)(2,1)S(1)} collective-permute-done((bf16[2,40,128]{2,1,0:T(8,128)(2,1)S(1)}, bf16[2,40,128]{2,1,0:T(8,128)(2,1)S(1)}, u32[]{:S(2)}, u32[]{:S(2)}) %collective-permute-start.4) | collective-permute-done | bytes 20512 | tf_op jit(solution)/shard_map/ppermute | solution.py:460
  20.7 0.0 collective-permute-done.6.cross_ref
  20.7 0.0 collective-permute-done.7.mate_pnt_ref
  20.7 0.9 %second.1 = (bf16[8,40,128]{2,1,0:T(8,128)(2,1)S(1)}, f32[8,512]{1,0:T(8,128)S(1)}, bf16[2,16,128]{2,1,0:T(8,128)(2,1)S(1)}) custom-call(bf16[2,40,128]{2,1,0:T(8,128)(2,1)S(1)} %pad_maximum_fusion.pair_ref, bf16[2,40,128]{2,1,0:T(8,128)(2,1)S(1)} %collective-permute-done.4.near_ref, bf16[2,40,128]{2,1,0:T(8,128)(2,1)S(1)} %collective-permute-done.5.far_ref, ...), custom_call_target="tpu_custom_call" | custom-call | tf_op jit(solution)/shard_map/second/pallas_call | solution.py:480
  21.6 3.0 %collective-permute-start.9 = (bf16[2,16,128]{2,1,0:T(8,128)(2,1)S(1)}, bf16[2,16,128]{2,1,0:T(8,128)(2,1)S(1)}, u32[]{:S(2)}, u32[]{:S(2)}) collective-permute-start(bf16[2,16,128]{2,1,0:T(8,128)(2,1)S(1)} %get-tuple-element.33.pair_ref), channel_id=1, source_target_pairs={{0,6},{1,5},{2,4},{3,7},{4,2},{5,1},{6,0},{7,3},{8,14},{9,13},{10,... | collective-permute-start | bytes 24584 | tf_op jit(solution)/shard_map/ppermute | solution.py:461
  24.6 0.0 collective-permute-start.8
  24.6 0.6 %early.1 = (bf16[256,512]{1,0:T(8,128)(2,1)S(1)}, f32[128,128]{1,0:T(8,128)S(1)}, f32[128,128]{1,0:T(8,128)S(1)}, bf16[1,128,128]{2,1,0:T(8,128)(2,1)S(1)}) custom-call(f32[512,512]{1,0:T(8,128)S(1)} %get-tuple-element.34.ts_ref, bf16[512,512]{1,0:T(8,128)(2,1)S(1)} %get-tuple-element.35.keep_ref, f32[1,512]{1,0:T(1,128)S(1)} %get-tuple-element.36.g_ref, ...), custom_call_target="tpu_custom_call" | custom-call | flops 500000000 | bytes 2000000 | tf_op jit(solution)/shard_map/early/pallas_call | solution.py:510
  25.2 1.9 %collective-permute-done.9.far_ref.after_ref = bf16[2,16,128]{2,1,0:T(8,128)(2,1)S(1)} collective-permute-done((bf16[2,16,128]{2,1,0:T(8,128)(2,1)S(1)}, bf16[2,16,128]{2,1,0:T(8,128)(2,1)S(1)}, u32[]{:S(2)}, u32[]{:S(2)}) %collective-permute-start.9) | collective-permute-done | bytes 8224 | tf_op jit(solution)/shard_map/ppermute | solution.py:461
  27.0 0.0 collective-permute-start.10
  27.0 1.3 %late.1 = bf16[512,512]{1,0:T(8,128)(2,1)} custom-call(f32[512,512]{1,0:T(8,128)S(1)} %get-tuple-element.34.ts_ref, bf16[512,512]{1,0:T(8,128)(2,1)S(1)} %get-tuple-element.35.keep_ref, f32[1,512]{1,0:T(1,128)S(1)} %get-tuple-element.36.g_ref, bf16[512,128]{1,0:T(8,128)(2,1)S(1)} %get-tuple-element.37.v3_ref, f32[64,512]{1,0:T(8,128)S(1)} %get-tuple-element.38.bq_ref, ...), custom_call_target="tpu_custom_call" | custom-call | flops 500000000 | bytes 2000000 | tf_op jit(solution)/shard_map/late/pallas_call | solution.py:524
  28.3 0.0 collective-permute-done.8.near_ref
  28.3 0.0 collective-permute-done.10.cross_ref
  28.4 0.8 %tile.1 = f32[1,128,128]{2,1,0:T(8,128)} custom-call(bf16[2,16,128]{2,1,0:T(8,128)(2,1)S(1)} %get-tuple-element.33.pair_ref, bf16[2,16,128]{2,1,0:T(8,128)(2,1)S(1)} %collective-permute-done.8.near_ref, bf16[2,16,128]{2,1,0:T(8,128)(2,1)S(1)} %collective-permute-done.9.far_ref.after_ref, bf16[2,16,128]{2,1,0:T(8,128)(2,1)S(1)} %collective-permute-done.10.cross_ref, ...), custom_call_target="tpu_custom_call" | custom-call | tf_op jit(solution)/shard_map/tile/pallas_call | solution.py:535
  (4 shorter events, 0.0 us)
Async XLA Ops:
  0.6 6.6 %copy-start = (f32[257]{0:T(512)S(1)}, f32[257]{0:T(512)}, u32[]{:S(2)}) copy-start(f32[257]{0:T(512)} %param.18) | copy-start | bytes 3088
  2.6 7.5 %collective-permute-start.2 = (bf16[72,512]{1,0:T(8,128)(2,1)S(1)}, bf16[72,512]{1,0:T(8,128)(2,1)S(1)}, u32[]{:S(2)}, u32[]{:S(2)}) collective-permute-start(bf16[72,512]{1,0:T(8,128)(2,1)S(1)} %get-tuple-element.26.m0), channel_id=1, source_target_pairs={{0,24},{8,16},{16,8},{24,0},{1,25},{9,17},{17,9},{25,1},{2,26},{10... | collective-permute-start | bytes 221192 | tf_op jit(solution)/shard_map/ppermute | solution.py:395
  6.6 4.4 %collective-permute-start.1 = (bf16[72,512]{1,0:T(8,128)(2,1)S(1)}, bf16[72,512]{1,0:T(8,128)(2,1)S(1)}, u32[]{:S(2)}, u32[]{:S(2)}) collective-permute-start(bf16[72,512]{1,0:T(8,128)(2,1)S(1)} %get-tuple-element.26.m0), channel_id=1, source_target_pairs={{0,16},{8,24},{16,0},{24,8},{1,17},{9,25},{17,1},{25,9},{2,18},{10... | collective-permute-start | bytes 221192 | tf_op jit(solution)/shard_map/ppermute | solution.py:395
  7.1 4.4 %collective-permute-start = (bf16[72,512]{1,0:T(8,128)(2,1)S(1)}, bf16[72,512]{1,0:T(8,128)(2,1)S(1)}, u32[]{:S(2)}, u32[]{:S(2)}) collective-permute-start(bf16[72,512]{1,0:T(8,128)(2,1)S(1)} %get-tuple-element.26.m0), channel_id=1, source_target_pairs={{0,8},{8,0},{16,24},{24,16},{1,9},{9,1},{17,25},{25,17},{2,10},{10... | collective-permute-start | bytes 221192 | tf_op jit(solution)/shard_map/ppermute | solution.py:395
  11.9 1.2 %collective-permute-start.3 = (bf16[1,56,128]{2,1,0:T(8,128)(2,1)S(1)}, bf16[1,56,128]{2,1,0:T(8,128)(2,1)S(1)}, u32[]{:S(2)}, u32[]{:S(2)}) collective-permute-start(bf16[1,56,128]{2,1,0:T(8,128)(2,1)S(1)} %get-tuple-element.29), channel_id=1, source_target_pairs={{0,1},{1,0},{2,3},{3,2},{4,5},{5,4},{6,7},{7,6},{8,9},{9,8},{10,11... | collective-permute-start | bytes 43016 | tf_op jit(solution)/shard_map/ppermute | solution.py:475
  13.1 7.6 %collective-permute-start.7 = (bf16[1024,512]{1,0:T(8,128)(2,1)S(1)}, bf16[1024,512]{1,0:T(8,128)(2,1)S(1)}, u32[]{:S(2)}, u32[]{:S(2)}) collective-permute-start(bf16[1024,512]{1,0:T(8,128)(2,1)S(1)} %get-tuple-element.32.pnt_ref), channel_id=1, source_target_pairs={{0,1},{1,0},{2,3},{3,2},{4,5},{5,4},{6,7},{7,6},{8,9},{9,8},{10,11... | collective-permute-start | bytes 3145736 | tf_op jit(solution)/shard_map/ppermute | solution.py:479
  13.3 5.7 %collective-permute-start.5 = (bf16[2,40,128]{2,1,0:T(8,128)(2,1)S(1)}, bf16[2,40,128]{2,1,0:T(8,128)(2,1)S(1)}, u32[]{:S(2)}, u32[]{:S(2)}) collective-permute-start(bf16[2,40,128]{2,1,0:T(8,128)(2,1)S(1)} %pad_maximum_fusion.pair_ref), channel_id=1, source_target_pairs={{0,6},{1,5},{2,4},{3,7},{4,2},{5,1},{6,0},{7,3},{8,14},{9,13},{10,... | collective-permute-start | bytes 61448 | tf_op jit(solution)/shard_map/ppermute | solution.py:461
  16.9 3.8 %collective-permute-start.4 = (bf16[2,40,128]{2,1,0:T(8,128)(2,1)S(1)}, bf16[2,40,128]{2,1,0:T(8,128)(2,1)S(1)}, u32[]{:S(2)}, u32[]{:S(2)}) collective-permute-start(bf16[2,40,128]{2,1,0:T(8,128)(2,1)S(1)} %pad_maximum_fusion.pair_ref), channel_id=1, source_target_pairs={{0,2},{1,3},{2,0},{3,1},{4,6},{5,7},{6,4},{7,5},{8,10},{9,11},{10,... | collective-permute-start | bytes 61448 | tf_op jit(solution)/shard_map/ppermute | solution.py:460
  19.0 1.7 %collective-permute-start.6 = (bf16[2,40,128]{2,1,0:T(8,128)(2,1)S(1)}, bf16[2,40,128]{2,1,0:T(8,128)(2,1)S(1)}, u32[]{:S(2)}, u32[]{:S(2)}) collective-permute-start(bf16[2,40,128]{2,1,0:T(8,128)(2,1)S(1)} %collective-permute-done.5.far_ref), channel_id=1, source_target_pairs={{0,1},{1,0},{2,3},{3,2},{4,5},{5,4},{6,7},{7,6},{8,9},{9,8},{10,11... | collective-permute-start | bytes 61448 | tf_op jit(solution)/shard_map/ppermute | solution.py:462
  21.6 5.5 %collective-permute-start.9 = (bf16[2,16,128]{2,1,0:T(8,128)(2,1)S(1)}, bf16[2,16,128]{2,1,0:T(8,128)(2,1)S(1)}, u32[]{:S(2)}, u32[]{:S(2)}) collective-permute-start(bf16[2,16,128]{2,1,0:T(8,128)(2,1)S(1)} %get-tuple-element.33.pair_ref), channel_id=1, source_target_pairs={{0,6},{1,5},{2,4},{3,7},{4,2},{5,1},{6,0},{7,3},{8,14},{9,13},{10,... | collective-permute-start | bytes 24584 | tf_op jit(solution)/shard_map/ppermute | solution.py:461
  24.6 3.8 %collective-permute-start.8 = (bf16[2,16,128]{2,1,0:T(8,128)(2,1)S(1)}, bf16[2,16,128]{2,1,0:T(8,128)(2,1)S(1)}, u32[]{:S(2)}, u32[]{:S(2)}) collective-permute-start(bf16[2,16,128]{2,1,0:T(8,128)(2,1)S(1)} %get-tuple-element.33.pair_ref), channel_id=1, source_target_pairs={{0,2},{1,3},{2,0},{3,1},{4,6},{5,7},{6,4},{7,5},{8,10},{9,11},{10,... | collective-permute-start | bytes 24584 | tf_op jit(solution)/shard_map/ppermute | solution.py:460
  27.0 1.3 %collective-permute-start.10 = (bf16[2,16,128]{2,1,0:T(8,128)(2,1)S(1)}, bf16[2,16,128]{2,1,0:T(8,128)(2,1)S(1)}, u32[]{:S(2)}, u32[]{:S(2)}) collective-permute-start(bf16[2,16,128]{2,1,0:T(8,128)(2,1)S(1)} %collective-permute-done.9.far_ref.after_ref), channel_id=1, source_target_pairs={{0,1},{1,0},{2,3},{3,2},{4,5},{5,4},{6,7},{7,6},{8,9},{9,8},{10,11... | collective-permute-start | bytes 24584 | tf_op jit(solution)/shard_map/ppermute | solution.py:462

commit v6 on v5

--- a/solution.py
+++ b/solution.py
@@ -17,7 +17,6 @@
 EARLY = 2
 MORE = 8
 NN = (((1,), (0,)), ((), ()))
-NT = (((1,), (1,)), ((), ()))
 
 
 def mm(a, b, dims=NN):
@@ -81,8 +80,8 @@
     msg_ref[2 * modes :] = jnp.where(row % 2 == 1, ext - hi, hi).astype(BF16)
 
 
-def prep_kernel(seg, kblk, lane_blocks, digits, tids_hbm, offs_hbm, owner_hbm, cos_hbm, point_hbm, gain_ref, v_ref,
-                h2_ref, toep_ref, pnt_ref, v3_ref, geo_ref, own_ref,
+def prep_kernel(seg, kblk, digits, tids_hbm, offs_hbm, owner_hbm, cos_hbm, point_hbm, gain_ref, v_ref,
+                h2_ref, toep_ref, pnt_ref, v3_ref, geo_ref,
                 tids_ref, offs_ref, owner_ref, cos_ref, point_ref, wide_ref, sem):
     streams = [(cos_hbm, cos_ref), (point_hbm, point_ref), (tids_hbm, tids_ref), (offs_hbm, offs_ref),
                (owner_hbm, owner_ref)]
@@ -116,13 +115,11 @@
         copy.wait()
     listed = seg * kblk
     row16 = iota((listed, LANES), 0)
-    first = lax.axis_index("tm") * listed
     squares = jnp.zeros((listed, LANES), F32)
     ext = geo_ref.shape[0] - listed
     row_x = iota((ext, LANES), 0)
     lane_x = iota((ext, LANES), 1)
     ids = jnp.zeros((ext, LANES), F32)
-    own = jnp.zeros((listed, LANES), F32)
     for k in range(kblk):
         for s in range(seg):
             j = k * seg + s
@@ -133,16 +130,11 @@
             p = p.astype(F32)
             squares = jnp.where(row16 == j, jnp.sum(p * p, axis=0, keepdims=True), squares)
             target = owner_ref[tids_ref[s, k]] * LANES + offs_ref[s, k]
-            own = jnp.where(row16 == j, target.astype(F32), own)
-            place = first + j
-            digit = target
             for d in range(digits):
-                at = (row_x == d * lane_blocks + place // LANES) & (lane_x == place % LANES)
-                ids = jnp.where(at, (digit % BASE).astype(F32), ids)
-                digit = digit // BASE
+                ids = jnp.where((row_x == d) & (lane_x == j), (target % BASE).astype(F32), ids)
+                target = target // BASE
     geo_ref[0:listed] = squares.astype(BF16)
     geo_ref[listed:] = ids.astype(BF16)
-    own_ref[...] = own
 
 
 def filtered(vectors, toep_ref):
@@ -217,23 +209,42 @@
         send_ref[0, listed + geo.shape[0] :] = tail.astype(BF16)
 
 
-def lane_ids(all_ref, listed, blocks, digits, b):
-    ids = jnp.sum(all_ref[:, 2 * listed :].astype(F32), axis=0)
-    out = ids[b : b + 1]
+def row_ids(ext, digits):
+    ext = ext.astype(F32)
+    ids = ext[0:1]
     for d in range(1, digits):
-        out = out + float(BASE**d) * ids[d * blocks + b : d * blocks + b + 1]
-    return out
-
-
-def fetch(all_ref, own, vec_ref, listed, blocks, digits):
+        ids = ids + float(BASE**d) * ext[d : d + 1]
+    return ids
+
+
+def groups(refs, listed, digits):
     per = LANES // listed
+    slots = [(ref, i) for ref in refs for i in range(ref.shape[0])]
+    for b in range(len(slots) // per):
+        part = slots[b * per : (b + 1) * per]
+        row = iota((per, LANES), 0)
+        ids = jnp.zeros((per, LANES), F32)
+        for n, (ref, i) in enumerate(part):
+            ids = jnp.where(row == n, row_ids(ref[i, 2 * listed :], digits), ids)
+        ids = pltpu.roll(ids, 0, 1, stride=listed, stride_axis=0)
+        ids = jnp.sum(ids, axis=0, keepdims=True)
+        sums = jnp.concatenate([ref[i, 0:listed] for ref, i in part], axis=0)
+        squares = jnp.concatenate([ref[i, listed : 2 * listed] for ref, i in part], axis=0)
+        yield ids, sums, squares
+
+
+def upright(ids, count):
+    eye = iota((count, LANES), 0) == iota((count, LANES), 1)
+    return jnp.sum(jnp.where(eye, ids, 0.0), axis=1, keepdims=True)
+
+
+def fetch(parts, own, vec_ref):
     psum = jnp.zeros((own.shape[0], LANES), F32)
     wsum = jnp.zeros((own.shape[0], LANES), F32)
-    for b in range(blocks):
-        same = (own == lane_ids(all_ref, listed, blocks, digits, b)).astype(F32).astype(BF16)
-        part = all_ref[b * per : (b + 1) * per]
-        psum = psum + mm(same, part[:, 0:listed].reshape(LANES, LANES))
-        wsum = wsum + mm(same, part[:, listed : 2 * listed].reshape(LANES, LANES))
+    for ids, sums, squares in parts:
+        same = (own == ids).astype(F32).astype(BF16)
+        psum = psum + mm(same, sums)
+        wsum = wsum + mm(same, squares)
     return (psum / (1.0 + vec_ref[2:3, 0:LANES] * wsum)).astype(BF16).astype(F32)
 
 
@@ -248,11 +259,11 @@
     return jnp.sum(jnp.where(lane // (samples // seg) == row % seg, spread, 0.0), axis=0, keepdims=True)
 
 
-def second_kernel(seg, kblk, digits, all_ref, own_ref, vec_ref, toep_ref, pnt_ref, sig_ref, send_ref):
-    listed = seg * kblk
-    blocks = all_ref.shape[0] * listed // LANES
+def second_kernel(seg, kblk, digits, all_ref, geo_ref, vec_ref, toep_ref, pnt_ref, sig_ref, send_ref):
+    listed = seg * kblk
     samples = vec_ref.shape[1]
-    fetched = fetch(all_ref, own_ref[...], vec_ref, listed, blocks, digits)
+    own = upright(row_ids(geo_ref[listed:], digits), listed)
+    fetched = fetch(list(groups([all_ref], listed, digits)), own, vec_ref)
     sig = signal(fetched, pnt_ref[samples:], seg, kblk)
     sig_ref[...] = jnp.broadcast_to(sig, sig_ref.shape)
     (z,) = filtered([vec_ref[0:1] - vec_ref[1:2] * sig], toep_ref)
@@ -261,37 +272,12 @@
         send_ref[t] = proj
 
 
-def assemble(pair_ref, near_ref, far_ref, cross_ref, all_ref):
-    t = lax.axis_index("tm")
-    core = t % 2
-    far, other = 6 - 2 * core, 4 + 2 * core
-    arrived = [
-        (pair_ref, t),
-        (near_ref, jnp.bitwise_xor(t, 2)),
-        (far_ref, jnp.bitwise_xor(t, far)),
-        (cross_ref, jnp.bitwise_xor(jnp.bitwise_xor(t, 1), other)),
-    ]
-    for ref, at in arrived:
-        all_ref[at] = ref[0]
-        all_ref[jnp.bitwise_xor(at, 1)] = ref[1]
-
-
 def pair_second_kernel(seg, kblk, digits, pair_ref, near_ref, far_ref, cross_ref, mate_ref, vec_ref, toep_ref, pnt_ref,
-                       mate_pnt_ref, all_ref, sig_ref, send_ref):
-    assemble(pair_ref, near_ref, far_ref, cross_ref, all_ref)
-    listed = seg * kblk
-    blocks = all_ref.shape[0] * listed // LANES
+                       mate_pnt_ref, sig_ref, send_ref):
+    listed = seg * kblk
     samples = vec_ref.shape[1]
-    t = lax.axis_index("tm")
-    mate = t + 1 - 2 * (t % 2)
-    row = iota((2 * listed, LANES), 0)
-    listing = jnp.where(row < listed, t * listed + row, mate * listed + row - listed)
-    lane = iota((2 * listed, LANES), 1)
-    own = jnp.zeros((2 * listed, 1), F32)
-    for b in range(blocks):
-        ids = lane_ids(all_ref, listed, blocks, digits, b)
-        own = own + jnp.sum(jnp.where(listing == lane + b * LANES, ids, 0.0), axis=1, keepdims=True)
-    fetched = fetch(all_ref, own, vec_ref, listed, blocks, digits)
+    parts = list(groups([pair_ref, near_ref, far_ref, cross_ref], listed, digits))
+    fetched = fetch(parts, upright(parts[0][0], 2 * listed), vec_ref)
     sig = signal(fetched[0:listed], pnt_ref[samples:], seg, kblk)
     mate_sig = signal(fetched[listed:], mate_pnt_ref[samples:], seg, kblk)
     sig_ref[...] = jnp.broadcast_to(sig, sig_ref.shape)
@@ -313,67 +299,53 @@
     q_hi, q_lo = split(bq_ref[0:modes] - bq_ref[modes : 2 * modes] * sig)
     pad = jnp.zeros((LANES - 3 * modes, samples), BF16)
     q3 = jnp.concatenate([q_hi, q_lo, q_hi, pad], axis=0)
-    eye = iota((at.stop - at.start,) * 2, 0) == iota((at.stop - at.start,) * 2, 1)
+    count = at.stop - at.start
+    eye = iota((count, count), 0) == iota((count, count), 1)
     g_col = jnp.sum(jnp.where(eye, g_ref[:, at], 0.0), axis=1, keepdims=True)
     rest = (ts_ref[at] - g_col * sig) * keep_ref[at].astype(F32) - mm(v3_ref[at], q3)
     rest = rest.astype(BF16)
     return (mm(rest, h2_ref[0:samples]) + mm(rest, h2_ref[samples:])).astype(BF16)
 
 
-def tile_parts(seg, kblk, digits, all_ref, vec_ref, base_ref, scale_ref, same_ref):
-    listed = seg * kblk
-    blocks = all_ref.shape[0] * listed // LANES
-    per = LANES // listed
+def early_kernel(seg, kblk, digits, modes, *refs):
+    operands, vec_ref, all_refs, (early_ref, base_ref, scale_ref, same_ref) = refs[:7], refs[7], refs[8:-4], refs[-4:]
+    early_ref[...] = clean_rows(modes, slice(0, early_ref.shape[0]), *operands)
     psum = jnp.zeros((LANES, LANES), F32)
     wsum = jnp.zeros((LANES, LANES), F32)
     first = (lax.axis_index("det") * lax.axis_size("tm") + lax.axis_index("tm")) * LANES
     mine = (iota((LANES, LANES), 0) + first).astype(F32)
-    for b in range(blocks):
-        same = (mine == lane_ids(all_ref, listed, blocks, digits, b)).astype(F32).astype(BF16)
+    for b, (ids, sums, squares) in enumerate(groups(all_refs, seg * kblk, digits)):
+        same = (mine == ids).astype(F32).astype(BF16)
         same_ref[b] = same
-        part = all_ref[b * per : (b + 1) * per]
-        psum = psum + mm(same, part[:, 0:listed].reshape(LANES, LANES))
-        wsum = wsum + mm(same, part[:, listed : 2 * listed].reshape(LANES, LANES))
+        psum = psum + mm(same, sums)
+        wsum = wsum + mm(same, squares)
     wsum = 1.0 + vec_ref[2:3, 0:LANES] * wsum
     scale = jnp.sqrt(wsum) / wsum
     scale_ref[...] = scale
     base_ref[...] = psum * scale
 
 
-def early_kernel(seg, kblk, digits, modes, ts_ref, keep_ref, g_ref, v3_ref, bq_ref, sig_ref, h2_ref, all_ref, vec_ref,
-                 early_ref, base_ref, scale_ref, same_ref):
-    rows = slice(0, early_ref.shape[0])
-    early_ref[...] = clean_rows(modes, rows, ts_ref, keep_ref, g_ref, v3_ref, bq_ref, sig_ref, h2_ref)
-    tile_parts(seg, kblk, digits, all_ref, vec_ref, base_ref, scale_ref, same_ref)
-
-
-def late_kernel(modes, ts_ref, keep_ref, g_ref, v3_ref, bq_ref, sig_ref, h2_ref, early_ref, after_ref, out_hbm,
-                late_ref, sem):
-    cut = early_ref.shape[0]
-    first = pltpu.make_async_copy(early_ref, out_hbm.at[pl.ds(0, cut)], sem.at[0])
-    first.start()
-    rows = slice(cut, ts_ref.shape[0])
-    late_ref[...] = clean_rows(modes, rows, ts_ref, keep_ref, g_ref, v3_ref, bq_ref, sig_ref, h2_ref)
-    second = pltpu.make_async_copy(late_ref, out_hbm.at[pl.ds(cut, late_ref.shape[0])], sem.at[1])
-    second.start()
-    first.wait()
-    second.wait()
-
-
-def tile_kernel(all2_ref, base_ref, scale_ref, same_ref, out_ref):
-    per = LANES // all2_ref.shape[1]
+def late_kernel(modes, *refs):
+    operands, early_ref, (out_hbm, late_ref, sem) = refs[:7], refs[7], refs[-3:]
+    cut, dets = early_ref.shape[0], operands[0].shape[0]
+    copies = [
+        pltpu.make_async_copy(early_ref, out_hbm.at[pl.ds(0, cut)], sem.at[0]),
+        pltpu.make_async_copy(late_ref, out_hbm.at[pl.ds(cut, dets - cut)], sem.at[1]),
+    ]
+    copies[0].start()
+    late_ref[...] = clean_rows(modes, slice(cut, dets), *operands)
+    copies[1].start()
+    for copy in copies:
+        copy.wait()
+
+
+def tile_kernel(*refs):
+    all_refs, (base_ref, scale_ref, same_ref, out_ref) = refs[:-4], refs[-4:]
+    slots = [ref[i] for ref in all_refs for i in range(ref.shape[0])]
+    per = LANES // slots[0].shape[0]
     psum = jnp.zeros((LANES, LANES), F32)
     for b in range(same_ref.shape[0]):
-        psum = psum + mm(same_ref[b], all2_ref[b * per : (b + 1) * per].reshape(LANES, LANES))
-    out_ref[0] = base_ref[...] + psum * scale_ref[...]
-
-
-def pair_tile_kernel(pair_ref, near_ref, far_ref, cross_ref, base_ref, scale_ref, same_ref, out_ref, all_ref):
-    assemble(pair_ref, near_ref, far_ref, cross_ref, all_ref)
-    blocks, per = same_ref.shape[0], LANES // all_ref.shape[1]
-    psum = jnp.zeros((LANES, LANES), F32)
-    for b in range(blocks):
-        psum = psum + mm(same_ref[b], all_ref[b * per : (b + 1) * per].reshape(LANES, LANES))
+        psum = psum + mm(same_ref[b], jnp.concatenate(slots[b * per : (b + 1) * per], axis=0))
     out_ref[0] = base_ref[...] + psum * scale_ref[...]
 
 
@@ -403,7 +375,7 @@
     listed = seg * kblk
     lane_blocks = n_tm * listed // LANES
     digits = -(-int(tile_owner.shape[0] * LANES - 1).bit_length() // 7)
-    id_rows = -(-digits * lane_blocks // 8) * 8
+    id_rows = 8
     inputs = (timestream, sample_flags, mode_vectors.T, det_gains.reshape(1, dets))
     msg, ts, keep, vt, g = pl.pallas_call(
         functools.partial(sums_kernel, modes),
@@ -427,17 +399,16 @@
 
     rows = -(-filter_gain.shape[0] // LANES) * LANES
     inputs = (tile_ids, block_offsets, tile_owner, jnp.asarray(cosine_table(samples, rows)), pointing)
-    h2, toep, pnt, v3, geo, own = pl.pallas_call(
-        functools.partial(prep_kernel, seg, kblk, lane_blocks, digits),
+    h2, toep, pnt, v3, geo = pl.pallas_call(
+        functools.partial(prep_kernel, seg, kblk, digits),
         in_specs=[HB] * 5 + [VM] * 2,
-        out_specs=[VM] * 6,
+        out_specs=[VM] * 5,
         out_shape=[
             shape((2 * samples, samples), BF16),
             shape((samples, 2 * LANES), BF16),
             shape((2 * samples, samples), BF16),
             shape((dets, LANES), BF16),
             shape((listed + id_rows, LANES), BF16),
-            shape((listed, LANES)),
         ],
         scratch_shapes=[
             pltpu.SMEM(tile_ids.shape, jnp.int32),
@@ -456,11 +427,8 @@
     paired = n_tm == 8
     mates = [(i, i ^ 1) for i in range(n_tm)]
 
-    def spread(pair):
-        near = lax.ppermute(pair, "tm", [(i, i ^ 2) for i in range(n_tm)])
-        far = lax.ppermute(pair, "tm", [(i, i ^ (6 - 2 * (i % 2))) for i in range(n_tm)])
-        return pair, near, far, lax.ppermute(far, "tm", mates)
-
+    nears = [(i, i ^ 2) for i in range(n_tm)]
+    fars = [(i, i ^ (4 + 2 * (i % 2))) for i in range(n_tm)]
     block = 2 * listed + id_rows
     first_shape = (1, block + 4 * samples // LANES, LANES) if paired else (n_tm, block, LANES)
     bq, vec, send = pl.pallas_call(
@@ -472,28 +440,24 @@
         name="first",
     )(*parts_of_all, toep, pnt, geo)
     if paired:
+        mate_pnt = lax.ppermute(pnt, "tm", mates)
         mate = lax.ppermute(send, "tm", mates)
         pair = jnp.concatenate([send[:, :block], mate[:, :block]], axis=0)
-        late_pnt, pair = lax.optimization_barrier((pnt, pair))
-        arrived = spread(pair)
-        mate_pnt = lax.ppermute(late_pnt, "tm", mates)
-        everyone, sig, send = pl.pallas_call(
+        near = lax.ppermute(pair, "tm", nears)
+        far = lax.ppermute(pair, "tm", fars)
+        arrived1 = (pair, near, far, lax.ppermute(far, "tm", mates))
+        sig, send = pl.pallas_call(
             functools.partial(pair_second_kernel, seg, kblk, digits),
             in_specs=[VM] * 9,
-            out_specs=[VM] * 3,
-            out_shape=[
-                shape((n_tm, block, LANES), BF16),
-                shape((8, samples)),
-                shape((2, listed, LANES), BF16),
-            ],
+            out_specs=[VM] * 2,
+            out_shape=[shape((8, samples)), shape((2, listed, LANES), BF16)],
             compiler_params=GRANT,
             name="second",
-        )(*arrived, mate, vec, toep, pnt, mate_pnt)
-        arrived = spread(send)
-        after = arrived[2]
-        last, scratch = pair_tile_kernel, [pltpu.VMEM((n_tm, listed, LANES), BF16)]
+        )(*arrived1, mate, vec, toep, pnt, mate_pnt)
+        near = lax.ppermute(send, "tm", nears)
+        far = lax.ppermute(send, "tm", fars)
     else:
-        everyone = lax.all_to_all(send, "tm", 0, 0)
+        arrived1 = (lax.all_to_all(send, "tm", 0, 0),)
         sig, send = pl.pallas_call(
             functools.partial(second_kernel, seg, kblk, digits),
             in_specs=[VM] * 5,
@@ -501,15 +465,14 @@
             out_shape=[shape((8, samples)), shape((n_tm, listed, LANES), BF16)],
             compiler_params=GRANT,
             name="second",
-        )(everyone, own, vec, toep, pnt)
-        arrived = (lax.all_to_all(send, "tm", 0, 0),)
-        after, last, scratch = vec, tile_kernel, []
+        )(*arrived1, geo, vec, toep, pnt)
+        arrived2 = (lax.all_to_all(send, "tm", 0, 0),)
 
     cut = EARLY * dets // 4
     operands = (ts, keep, g, v3, bq, sig, h2)
     early, base, scale, same = pl.pallas_call(
         functools.partial(early_kernel, seg, kblk, digits, modes),
-        in_specs=[VM] * 9,
+        in_specs=[VM] * (8 + len(arrived1)),
         out_specs=[VM] * 4,
         out_shape=[
             shape((cut, samples), BF16),
@@ -520,7 +483,12 @@
         cost_estimate=pl.CostEstimate(flops=5 * 10**8, bytes_accessed=2 * 10**6, transcendentals=0),
         compiler_params=GRANT,
         name="early",
-    )(*operands, everyone, vec)
+    )(*operands, vec, *arrived1)
+    after = vec
+    if paired:
+        far, base = lax.optimization_barrier((far, base))
+        arrived2 = (send, near, far, lax.ppermute(far, "tm", mates))
+        after = far
     cleaned = pl.pallas_call(
         functools.partial(late_kernel, modes),
         in_specs=[VM] * 9,
@@ -533,20 +501,22 @@
     )(*operands, early, after)
 
     tile = pl.pallas_call(
-        last,
-        in_specs=[VM] * (len(arrived) + 3),
+        tile_kernel,
+        in_specs=[VM] * (len(arrived2) + 3),
         out_specs=VM,
         out_shape=shape((1, LANES, LANES)),
-        scratch_shapes=scratch,
         compiler_params=GRANT,
         name="tile",
-    )(*arrived, base, scale, same)
+    )(*arrived2, base, scale, same)
     return tile, cleaned
 
 
 def solution(mesh):
-    return jax.shard_map(
-        functools.partial(shards, mesh.shape["det"], mesh.shape["tm"]),
+    def step(*args):
+        return shards(mesh.shape["det"], mesh.shape["tm"], *args)
+
+    step = jax.shard_map(
+        step,
         mesh=mesh,
         in_specs=(
             P("det", "tm"),
@@ -562,3 +532,4 @@
         out_specs=(P(("det", "tm"), None, None), P("det", "tm")),
         check_vma=False,
     )
+    return step

time: 29.3 us -> 30.5 us (1.041)
  starting transfers between devices: 11.4 us -> 12.9 us
  local copies, waits for them, and re-layouts: 0.01 us -> 0.69 us
  Pallas kernels: 8.84 us -> 8.23 us
  waiting for transfers between devices: 8.14 us -> 7.76 us
    ppermute x7, waiting for transfers between devices: 5.64 us -> 2.37 us  [the longest x1 1.57 us: shards(): near = lax.ppermute(pair, 'tm', nears)]
    ppermute x3, waiting for transfers between devices: 1.33 us -> 4.22 us  [others(): return [lax.ppermute(x, axis, p) for p in pairs]]
    ppermute x7, starting transfers between devices: 6.8 us -> 8.73 us  [the longest x1 2.65 us: shards(): far = lax.ppermute(pair, 'tm', fars)]
    reshape x1, local copies, waits for them, and re-layouts: 0.01 us -> 0.68 us  [shards(): filter_gain.reshape(1, -1)]
    pallas_call x2, Pallas kernels: 3.66 us -> 2.99 us  [the longest x1 2.22 us: shards(): pl.pallas_call(functools.partial(prep_kernel, seg, kblk, digits), in_spec...]
    ppermute x3, starting transfers between devices: 4.63 us -> 4.15 us  [others(): return [lax.ppermute(x, axis, p) for p in pairs]]
  transfers between devices with their start and end apart: 11 -> 11, of which waited for: 6 -> 7; matrix products, arithmetic and copies ran while one was open for 0% -> 0% of each run, Pallas kernels for 16% -> 8%
where the time goes in v6:
time: 30.5 us; the launch traced here: 30.3 us
  starting transfers between devices  12.9 us (42%)
  Pallas kernels  8.23 us (27%)
  waiting for transfers between devices  7.76 us (25%)
  between operations  0.71 us (2%)
  local copies, waits for them, and re-layouts  0.69 us (2%)
    ppermute x3, waiting for transfers between devices, others(): return [lax.ppermute(x, axis, p) for p in pairs]  4.22 us
    ppermute x3, starting transfers between devices, others(): return [lax.ppermute(x, axis, p) for p in pairs]  4.15 us
    ppermute x1, starting transfers between devices, shards(): far = lax.ppermute(pair, 'tm', fars)  2.65 us
    pallas_call x1, Pallas kernels, shards(): pl.pallas_call(functools.partial(prep_kernel, seg, kblk, digits), in_spec...  2.22 us
    ppermute x1, starting transfers between devices, shards(): far = lax.ppermute(send, 'tm', fars)  2.08 us
    pallas_call x1, Pallas kernels, shards(): pl.pallas_call(functools.partial(sums_kernel, modes), in_specs=[HB] * 4,...  1.99 us
    ppermute x1, starting transfers between devices, shards(): near = lax.ppermute(send, 'tm', nears)  1.83 us
    ppermute x1, starting transfers between devices, shards(): near = lax.ppermute(pair, 'tm', nears)  1.58 us
  transfers between devices with their start and end apart: 11, of which 7 were waited for; matrix products, arithmetic and copies ran while one was open for 0% of the time, Pallas kernels for 8%

profile of v6, /device:TPU:0, one launch (start us, length us, event | category | flops | bytes accessed | tf_op | source)
XLA Modules:
  0.0 30.3 jit_solution(685652348161076750)
XLA Ops:
  0.6 0.7 %reshape.11.gain_ref = f32[1,257]{1,0:T(1,128)S(1)} reshape(f32[257]{0:T(512)} %param.18) | data formatting | bytes 2056 | tf_op jit(solution)/shard_map/reshape | solution.py:425
  1.3 2.0 %sums.1 = (bf16[72,512]{1,0:T(8,128)(2,1)S(1)}, f32[512,512]{1,0:T(8,128)S(1)}, bf16[512,512]{1,0:T(8,128)(2,1)S(1)}, f32[32,512]{1,0:T(8,128)S(1)}, f32[1,512]{1,0:T(1,128)S(1)}) custom-call(f32[512,512]{1,0:T(8,128)} %ts_hbm.1, s32[512,512]{1,0:T(8,128)} %flag_hbm.1, f32[32,512]{1,0:T(8,128)} %bitcast.2, f32[1,512]{1,0:T(1,128)} %bitcast.3), custom_call_target="tpu_custom_call" | custom-call | tf_op jit(solution)/shard_map/sums/pallas_call | solution.py:380
  3.3 2.2 %prep.1 = (bf16[1024,512]{1,0:T(8,128)(2,1)S(1)}, bf16[512,256]{1,0:T(8,128)(2,1)S(1)}, bf16[1024,512]{1,0:T(8,128)(2,1)S(1)}, bf16[512,128]{1,0:T(8,128)(2,1)S(1)}, bf16[24,128]{1,0:T(8,128)(2,1)S(1)}) custom-call(s32[4,4]{1,0:T(4,128)} %tids_hbm.1, s32[4,4]{1,0:T(4,128)} %offs_hbm.1, s32[32]{0:T(128)} %owner_hbm.1, f32[384,512]{1,0:T(8,128)} %constant.2.clone.cos_hbm, ...), custom_call_target="tpu_custom_call" | custom-call | flops 100000000 | bytes 3000000 | tf_op jit(solution)/shard_map/prep/pallas_call | solution.py:402
  5.5 0.6 %collective-permute-start.7 = (bf16[1024,512]{1,0:T(8,128)(2,1)S(1)}, bf16[1024,512]{1,0:T(8,128)(2,1)S(1)}, u32[]{:S(2)}, u32[]{:S(2)}) collective-permute-start(bf16[1024,512]{1,0:T(8,128)(2,1)S(1)} %get-tuple-element.26.pnt_ref), channel_id=1, source_target_pairs={{0,1},{1,0},{2,3},{3,2},{4,5},{5,4},{6,7},{7,6},{8,9},{9,8},{10,11... | collective-permute-start | bytes 3145736 | tf_op jit(solution)/shard_map/ppermute | solution.py:443
  6.1 3.5 %collective-permute-start.2 = (bf16[72,512]{1,0:T(8,128)(2,1)S(1)}, bf16[72,512]{1,0:T(8,128)(2,1)S(1)}, u32[]{:S(2)}, u32[]{:S(2)}) collective-permute-start(bf16[72,512]{1,0:T(8,128)(2,1)S(1)} %get-tuple-element.23.m0), channel_id=1, source_target_pairs={{0,24},{8,16},{16,8},{24,0},{1,25},{9,17},{17,9},{25,1},{2,26},{10... | collective-permute-start | bytes 221192 | tf_op jit(solution)/shard_map/ppermute | solution.py:367
  9.6 0.5 %collective-permute-start.1 = (bf16[72,512]{1,0:T(8,128)(2,1)S(1)}, bf16[72,512]{1,0:T(8,128)(2,1)S(1)}, u32[]{:S(2)}, u32[]{:S(2)}) collective-permute-start(bf16[72,512]{1,0:T(8,128)(2,1)S(1)} %get-tuple-element.23.m0), channel_id=1, source_target_pairs={{0,16},{8,24},{16,0},{24,8},{1,17},{9,25},{17,1},{25,9},{2,18},{10... | collective-permute-start | bytes 221192 | tf_op jit(solution)/shard_map/ppermute | solution.py:367
  10.1 0.1 collective-permute-start
  10.2 2.2 %collective-permute-done.2.m3 = bf16[72,512]{1,0:T(8,128)(2,1)S(1)} collective-permute-done((bf16[72,512]{1,0:T(8,128)(2,1)S(1)}, bf16[72,512]{1,0:T(8,128)(2,1)S(1)}, u32[]{:S(2)}, u32[]{:S(2)}) %collective-permute-start.2) | collective-permute-done | bytes 73760 | tf_op jit(solution)/shard_map/ppermute | solution.py:367
  12.5 1.6 %collective-permute-done.1.m2 = bf16[72,512]{1,0:T(8,128)(2,1)S(1)} collective-permute-done((bf16[72,512]{1,0:T(8,128)(2,1)S(1)}, bf16[72,512]{1,0:T(8,128)(2,1)S(1)}, u32[]{:S(2)}, u32[]{:S(2)}) %collective-permute-start.1) | collective-permute-done | bytes 73760 | tf_op jit(solution)/shard_map/ppermute | solution.py:367
  14.0 0.4 %collective-permute-done.m1 = bf16[72,512]{1,0:T(8,128)(2,1)S(1)} collective-permute-done((bf16[72,512]{1,0:T(8,128)(2,1)S(1)}, bf16[72,512]{1,0:T(8,128)(2,1)S(1)}, u32[]{:S(2)}, u32[]{:S(2)}) %collective-permute-start) | collective-permute-done | bytes 73760 | tf_op jit(solution)/shard_map/ppermute | solution.py:367
  14.5 0.4 %first.1 = (f32[64,512]{1,0:T(8,128)S(1)}, f32[8,512]{1,0:T(8,128)S(1)}, bf16[1,56,128]{2,1,0:T(8,128)(2,1)S(1)}) custom-call(bf16[72,512]{1,0:T(8,128)(2,1)S(1)} %get-tuple-element.23.m0, bf16[72,512]{1,0:T(8,128)(2,1)S(1)} %collective-permute-done.m1, bf16[72,512]{1,0:T(8,128)(2,1)S(1)} %collective-permute-done.1.m2, ...), custom_call_target="tpu_custom_call" | custom-call | tf_op jit(solution)/shard_map/first/pallas_call | solution.py:434
  14.9 0.0 collective-permute-start.3
  14.9 1.2 %collective-permute-done.3.mate_ref = bf16[1,56,128]{2,1,0:T(8,128)(2,1)S(1)} collective-permute-done((bf16[1,56,128]{2,1,0:T(8,128)(2,1)S(1)}, bf16[1,56,128]{2,1,0:T(8,128)(2,1)S(1)}, u32[]{:S(2)}, u32[]{:S(2)}) %collective-permute-start.3) | collective-permute-done | bytes 14368 | tf_op jit(solution)/shard_map/ppermute | solution.py:444
  16.1 2.7 %collective-permute-start.5 = (bf16[2,40,128]{2,1,0:T(8,128)(2,1)S(1)}, bf16[2,40,128]{2,1,0:T(8,128)(2,1)S(1)}, u32[]{:S(2)}, u32[]{:S(2)}) collective-permute-start(bf16[2,40,128]{2,1,0:T(8,128)(2,1)S(1)} %pad_maximum_fusion.pair_ref.refs_8_), channel_id=1, source_target_pairs={{0,4},{1,7},{2,6},{3,5},{4,0},{5,3},{6,2},{7,1},{8,12},{9,15},{10,... | collective-permute-start | bytes 61448 | tf_op jit(solution)/shard_map/ppermute | solution.py:447
  18.7 1.6 %collective-permute-start.4 = (bf16[2,40,128]{2,1,0:T(8,128)(2,1)S(1)}, bf16[2,40,128]{2,1,0:T(8,128)(2,1)S(1)}, u32[]{:S(2)}, u32[]{:S(2)}) collective-permute-start(bf16[2,40,128]{2,1,0:T(8,128)(2,1)S(1)} %pad_maximum_fusion.pair_ref.refs_8_), channel_id=1, source_target_pairs={{0,2},{1,3},{2,0},{3,1},{4,6},{5,7},{6,4},{7,5},{8,10},{9,11},{10,... | collective-permute-start | bytes 61448 | tf_op jit(solution)/shard_map/ppermute | solution.py:446
  20.3 0.7 %collective-permute-done.5.far_ref.refs_10_ = bf16[2,40,128]{2,1,0:T(8,128)(2,1)S(1)} collective-permute-done((bf16[2,40,128]{2,1,0:T(8,128)(2,1)S(1)}, bf16[2,40,128]{2,1,0:T(8,128)(2,1)S(1)}, u32[]{:S(2)}, u32[]{:S(2)}) %collective-permute-start.5) | collective-permute-done | bytes 20512 | tf_op jit(solution)/shard_map/ppermute | solution.py:447
  21.0 0.0 collective-permute-start.6
  21.0 1.6 %collective-permute-done.4.near_ref.refs_9_ = bf16[2,40,128]{2,1,0:T(8,128)(2,1)S(1)} collective-permute-done((bf16[2,40,128]{2,1,0:T(8,128)(2,1)S(1)}, bf16[2,40,128]{2,1,0:T(8,128)(2,1)S(1)}, u32[]{:S(2)}, u32[]{:S(2)}) %collective-permute-start.4) | collective-permute-done | bytes 20512 | tf_op jit(solution)/shard_map/ppermute | solution.py:446
  22.6 0.0 collective-permute-done.6.cross_ref.refs_11_
  22.6 0.0 collective-permute-done.7.mate_pnt_ref
  22.6 1.0 %second.1 = (f32[8,512]{1,0:T(8,128)S(1)}, bf16[2,16,128]{2,1,0:T(8,128)(2,1)S(1)}) custom-call(bf16[2,40,128]{2,1,0:T(8,128)(2,1)S(1)} %pad_maximum_fusion.pair_ref.refs_8_, bf16[2,40,128]{2,1,0:T(8,128)(2,1)S(1)} %collective-permute-done.4.near_ref.refs_9_, bf16[2,40,128]{2,1,0:T(8,128)(2,1)S(1)} %collective-permute-done.5.far_ref.refs_10_, ...), custom_call_target="tpu_custom_call" | custom-call | tf_op jit(solution)/shard_map/second/pallas_call | solution.py:449
  23.6 2.1 %collective-permute-start.9 = (bf16[2,16,128]{2,1,0:T(8,128)(2,1)S(1)}, bf16[2,16,128]{2,1,0:T(8,128)(2,1)S(1)}, u32[]{:S(2)}, u32[]{:S(2)}) collective-permute-start(bf16[2,16,128]{2,1,0:T(8,128)(2,1)S(1)} %get-tuple-element.30.refs_0_), channel_id=1, source_target_pairs={{0,4},{1,7},{2,6},{3,5},{4,0},{5,3},{6,2},{7,1},{8,12},{9,15},{10,... | collective-permute-start | bytes 24584 | tf_op jit(solution)/shard_map/ppermute | solution.py:458
  25.6 1.8 %collective-permute-start.8 = (bf16[2,16,128]{2,1,0:T(8,128)(2,1)S(1)}, bf16[2,16,128]{2,1,0:T(8,128)(2,1)S(1)}, u32[]{:S(2)}, u32[]{:S(2)}) collective-permute-start(bf16[2,16,128]{2,1,0:T(8,128)(2,1)S(1)} %get-tuple-element.30.refs_0_), channel_id=1, source_target_pairs={{0,2},{1,3},{2,0},{3,1},{4,6},{5,7},{6,4},{7,5},{8,10},{9,11},{10,... | collective-permute-start | bytes 24584 | tf_op jit(solution)/shard_map/ppermute | solution.py:457
  27.5 0.6 %early.1 = (bf16[256,512]{1,0:T(8,128)(2,1)S(1)}, f32[128,128]{1,0:T(8,128)S(1)}, f32[128,128]{1,0:T(8,128)S(1)}, bf16[1,128,128]{2,1,0:T(8,128)(2,1)S(1)}) custom-call(f32[512,512]{1,0:T(8,128)S(1)} %get-tuple-element.31.refs_0_, bf16[512,512]{1,0:T(8,128)(2,1)S(1)} %get-tuple-element.32.refs_1_, f32[1,512]{1,0:T(1,128)S(1)} %get-tuple-element.33.refs_2_, ...), custom_call_target="tpu_custom_call" | custom-call | flops 500000000 | bytes 2000000 | tf_op jit(solution)/shard_map/early/pallas_call | solution.py:473
  28.1 0.1 collective-permute-done.9.refs_2_.refs_8_
  28.1 0.0 collective-permute-start.10
  28.2 1.3 %late.1 = bf16[512,512]{1,0:T(8,128)(2,1)} custom-call(f32[512,512]{1,0:T(8,128)S(1)} %get-tuple-element.31.refs_0_, bf16[512,512]{1,0:T(8,128)(2,1)S(1)} %get-tuple-element.32.refs_1_, f32[1,512]{1,0:T(1,128)S(1)} %get-tuple-element.33.refs_2_, bf16[512,128]{1,0:T(8,128)(2,1)S(1)} %get-tuple-element.34.refs_3_, f32[64,512]{1,0:T(8,128)S(1)} %get-tuple-element.35.refs_4_, ...), custom_call_target="tpu_custom_call" | custom-call | flops 500000000 | bytes 2000000 | tf_op jit(solution)/shard_map/late/pallas_call | solution.py:492
  29.5 0.0 collective-permute-done.8.refs_1_
  29.5 0.0 collective-permute-done.10.refs_3_
  29.5 0.8 %tile.1 = f32[1,128,128]{2,1,0:T(8,128)} custom-call(bf16[2,16,128]{2,1,0:T(8,128)(2,1)S(1)} %get-tuple-element.30.refs_0_, bf16[2,16,128]{2,1,0:T(8,128)(2,1)S(1)} %collective-permute-done.8.refs_1_, bf16[2,16,128]{2,1,0:T(8,128)(2,1)S(1)} %collective-permute-done.9.refs_2_.refs_8_, bf16[2,16,128]{2,1,0:T(8,128)(2,1)S(1)} %collective-permute-done.10.refs_3_, ...), custom_call_target="tpu_custom_call" | custom-call | tf_op jit(solution)/shard_map/tile/pallas_call | solution.py:503
  (3 shorter events, 0.0 us)
Async XLA Ops:
  5.5 17.1 %collective-permute-start.7 = (bf16[1024,512]{1,0:T(8,128)(2,1)S(1)}, bf16[1024,512]{1,0:T(8,128)(2,1)S(1)}, u32[]{:S(2)}, u32[]{:S(2)}) collective-permute-start(bf16[1024,512]{1,0:T(8,128)(2,1)S(1)} %get-tuple-element.26.pnt_ref), channel_id=1, source_target_pairs={{0,1},{1,0},{2,3},{3,2},{4,5},{5,4},{6,7},{7,6},{8,9},{9,8},{10,11... | collective-permute-start | bytes 3145736 | tf_op jit(solution)/shard_map/ppermute | solution.py:443
  6.1 6.4 %collective-permute-start.2 = (bf16[72,512]{1,0:T(8,128)(2,1)S(1)}, bf16[72,512]{1,0:T(8,128)(2,1)S(1)}, u32[]{:S(2)}, u32[]{:S(2)}) collective-permute-start(bf16[72,512]{1,0:T(8,128)(2,1)S(1)} %get-tuple-element.23.m0), channel_id=1, source_target_pairs={{0,24},{8,16},{16,8},{24,0},{1,25},{9,17},{17,9},{25,1},{2,26},{10... | collective-permute-start | bytes 221192 | tf_op jit(solution)/shard_map/ppermute | solution.py:367
  9.6 4.4 %collective-permute-start.1 = (bf16[72,512]{1,0:T(8,128)(2,1)S(1)}, bf16[72,512]{1,0:T(8,128)(2,1)S(1)}, u32[]{:S(2)}, u32[]{:S(2)}) collective-permute-start(bf16[72,512]{1,0:T(8,128)(2,1)S(1)} %get-tuple-element.23.m0), channel_id=1, source_target_pairs={{0,16},{8,24},{16,0},{24,8},{1,17},{9,25},{17,1},{25,9},{2,18},{10... | collective-permute-start | bytes 221192 | tf_op jit(solution)/shard_map/ppermute | solution.py:367
  10.1 4.4 %collective-permute-start = (bf16[72,512]{1,0:T(8,128)(2,1)S(1)}, bf16[72,512]{1,0:T(8,128)(2,1)S(1)}, u32[]{:S(2)}, u32[]{:S(2)}) collective-permute-start(bf16[72,512]{1,0:T(8,128)(2,1)S(1)} %get-tuple-element.23.m0), channel_id=1, source_target_pairs={{0,8},{8,0},{16,24},{24,16},{1,9},{9,1},{17,25},{25,17},{2,10},{10... | collective-permute-start | bytes 221192 | tf_op jit(solution)/shard_map/ppermute | solution.py:367
  14.9 1.2 %collective-permute-start.3 = (bf16[1,56,128]{2,1,0:T(8,128)(2,1)S(1)}, bf16[1,56,128]{2,1,0:T(8,128)(2,1)S(1)}, u32[]{:S(2)}, u32[]{:S(2)}) collective-permute-start(bf16[1,56,128]{2,1,0:T(8,128)(2,1)S(1)} %get-tuple-element.28), channel_id=1, source_target_pairs={{0,1},{1,0},{2,3},{3,2},{4,5},{5,4},{6,7},{7,6},{8,9},{9,8},{10,11... | collective-permute-start | bytes 43016 | tf_op jit(solution)/shard_map/ppermute | solution.py:444
  16.1 5.0 %collective-permute-start.5 = (bf16[2,40,128]{2,1,0:T(8,128)(2,1)S(1)}, bf16[2,40,128]{2,1,0:T(8,128)(2,1)S(1)}, u32[]{:S(2)}, u32[]{:S(2)}) collective-permute-start(bf16[2,40,128]{2,1,0:T(8,128)(2,1)S(1)} %pad_maximum_fusion.pair_ref.refs_8_), channel_id=1, source_target_pairs={{0,4},{1,7},{2,6},{3,5},{4,0},{5,3},{6,2},{7,1},{8,12},{9,15},{10,... | collective-permute-start | bytes 61448 | tf_op jit(solution)/shard_map/ppermute | solution.py:447
  18.7 3.9 %collective-permute-start.4 = (bf16[2,40,128]{2,1,0:T(8,128)(2,1)S(1)}, bf16[2,40,128]{2,1,0:T(8,128)(2,1)S(1)}, u32[]{:S(2)}, u32[]{:S(2)}) collective-permute-start(bf16[2,40,128]{2,1,0:T(8,128)(2,1)S(1)} %pad_maximum_fusion.pair_ref.refs_8_), channel_id=1, source_target_pairs={{0,2},{1,3},{2,0},{3,1},{4,6},{5,7},{6,4},{7,5},{8,10},{9,11},{10,... | collective-permute-start | bytes 61448 | tf_op jit(solution)/shard_map/ppermute | solution.py:446
  21.0 1.6 %collective-permute-start.6 = (bf16[2,40,128]{2,1,0:T(8,128)(2,1)S(1)}, bf16[2,40,128]{2,1,0:T(8,128)(2,1)S(1)}, u32[]{:S(2)}, u32[]{:S(2)}) collective-permute-start(bf16[2,40,128]{2,1,0:T(8,128)(2,1)S(1)} %collective-permute-done.5.far_ref.refs_10_), channel_id=1, source_target_pairs={{0,1},{1,0},{2,3},{3,2},{4,5},{5,4},{6,7},{7,6},{8,9},{9,8},{10,11... | collective-permute-start | bytes 61448 | tf_op jit(solution)/shard_map/ppermute | solution.py:448
  23.6 4.6 %collective-permute-start.9 = (bf16[2,16,128]{2,1,0:T(8,128)(2,1)S(1)}, bf16[2,16,128]{2,1,0:T(8,128)(2,1)S(1)}, u32[]{:S(2)}, u32[]{:S(2)}) collective-permute-start(bf16[2,16,128]{2,1,0:T(8,128)(2,1)S(1)} %get-tuple-element.30.refs_0_), channel_id=1, source_target_pairs={{0,4},{1,7},{2,6},{3,5},{4,0},{5,3},{6,2},{7,1},{8,12},{9,15},{10,... | collective-permute-start | bytes 24584 | tf_op jit(solution)/shard_map/ppermute | solution.py:458
  25.6 3.8 %collective-permute-start.8 = (bf16[2,16,128]{2,1,0:T(8,128)(2,1)S(1)}, bf16[2,16,128]{2,1,0:T(8,128)(2,1)S(1)}, u32[]{:S(2)}, u32[]{:S(2)}) collective-permute-start(bf16[2,16,128]{2,1,0:T(8,128)(2,1)S(1)} %get-tuple-element.30.refs_0_), channel_id=1, source_target_pairs={{0,2},{1,3},{2,0},{3,1},{4,6},{5,7},{6,4},{7,5},{8,10},{9,11},{10,... | collective-permute-start | bytes 24584 | tf_op jit(solution)/shard_map/ppermute | solution.py:457
  28.1 1.4 %collective-permute-start.10 = (bf16[2,16,128]{2,1,0:T(8,128)(2,1)S(1)}, bf16[2,16,128]{2,1,0:T(8,128)(2,1)S(1)}, u32[]{:S(2)}, u32[]{:S(2)}) collective-permute-start(bf16[2,16,128]{2,1,0:T(8,128)(2,1)S(1)} %collective-permute-done.9.refs_2_.refs_8_), channel_id=1, source_target_pairs={{0,1},{1,0},{2,3},{3,2},{4,5},{5,4},{6,7},{7,6},{8,9},{9,8},{10,11... | collective-permute-start | bytes 24584 | tf_op jit(solution)/shard_map/ppermute | solution.py:490

commit v7 on v6

--- a/solution.py
+++ b/solution.py
@@ -14,7 +14,7 @@
 LANES = 128
 BASE = 128
 EXT = 16
-EARLY = 2
+EARLY = 3
 MORE = 8
 NN = (((1,), (0,)), ((), ()))
 
@@ -131,7 +131,7 @@
             squares = jnp.where(row16 == j, jnp.sum(p * p, axis=0, keepdims=True), squares)
             target = owner_ref[tids_ref[s, k]] * LANES + offs_ref[s, k]
             for d in range(digits):
-                ids = jnp.where((row_x == d) & (lane_x == j), (target % BASE).astype(F32), ids)
+                ids = jnp.where((row_x == d) & (lane_x % listed == j), (target % BASE).astype(F32), ids)
                 target = target // BASE
     geo_ref[0:listed] = squares.astype(BF16)
     geo_ref[listed:] = ids.astype(BF16)
@@ -222,12 +222,10 @@
     slots = [(ref, i) for ref in refs for i in range(ref.shape[0])]
     for b in range(len(slots) // per):
         part = slots[b * per : (b + 1) * per]
-        row = iota((per, LANES), 0)
-        ids = jnp.zeros((per, LANES), F32)
+        lane = iota((1, LANES), 1)
+        ids = jnp.zeros((1, LANES), F32)
         for n, (ref, i) in enumerate(part):
-            ids = jnp.where(row == n, row_ids(ref[i, 2 * listed :], digits), ids)
-        ids = pltpu.roll(ids, 0, 1, stride=listed, stride_axis=0)
-        ids = jnp.sum(ids, axis=0, keepdims=True)
+            ids = jnp.where(lane // listed == n, row_ids(ref[i, 2 * listed :], digits), ids)
         sums = jnp.concatenate([ref[i, 0:listed] for ref, i in part], axis=0)
         squares = jnp.concatenate([ref[i, listed : 2 * listed] for ref, i in part], axis=0)
         yield ids, sums, squares
@@ -293,12 +291,15 @@
     send_ref[1] = project(mate_z, mate_pnt_ref[0:samples], seg, kblk).astype(BF16)
 
 
-def clean_rows(modes, at, ts_ref, keep_ref, g_ref, v3_ref, bq_ref, sig_ref, h2_ref):
+def stacked_modes(modes, bq_ref, sig_ref):
+    q_hi, q_lo = split(bq_ref[0:modes] - bq_ref[modes : 2 * modes] * sig_ref[0:1])
+    pad = jnp.zeros((LANES - 3 * modes, q_hi.shape[1]), BF16)
+    return jnp.concatenate([q_hi, q_lo, q_hi, pad], axis=0)
+
+
+def clean_rows(at, q3, ts_ref, keep_ref, g_ref, v3_ref, sig_ref, h2_ref):
     samples = ts_ref.shape[1]
     sig = sig_ref[0:1]
-    q_hi, q_lo = split(bq_ref[0:modes] - bq_ref[modes : 2 * modes] * sig)
-    pad = jnp.zeros((LANES - 3 * modes, samples), BF16)
-    q3 = jnp.concatenate([q_hi, q_lo, q_hi, pad], axis=0)
     count = at.stop - at.start
     eye = iota((count, count), 0) == iota((count, count), 1)
     g_col = jnp.sum(jnp.where(eye, g_ref[:, at], 0.0), axis=1, keepdims=True)
@@ -308,8 +309,11 @@
 
 
 def early_kernel(seg, kblk, digits, modes, *refs):
-    operands, vec_ref, all_refs, (early_ref, base_ref, scale_ref, same_ref) = refs[:7], refs[7], refs[8:-4], refs[-4:]
-    early_ref[...] = clean_rows(modes, slice(0, early_ref.shape[0]), *operands)
+    operands, bq_ref, vec_ref, all_refs = refs[:6], refs[6], refs[7], refs[8:-5]
+    early_ref, q3_ref, base_ref, scale_ref, same_ref = refs[-5:]
+    q3 = stacked_modes(modes, bq_ref, operands[4])
+    q3_ref[...] = q3
+    early_ref[...] = clean_rows(slice(0, early_ref.shape[0]), q3, *operands)
     psum = jnp.zeros((LANES, LANES), F32)
     wsum = jnp.zeros((LANES, LANES), F32)
     first = (lax.axis_index("det") * lax.axis_size("tm") + lax.axis_index("tm")) * LANES
@@ -325,15 +329,15 @@
     base_ref[...] = psum * scale
 
 
-def late_kernel(modes, *refs):
-    operands, early_ref, (out_hbm, late_ref, sem) = refs[:7], refs[7], refs[-3:]
+def late_kernel(*refs):
+    operands, q3_ref, early_ref, (out_hbm, late_ref, sem) = refs[:6], refs[6], refs[7], refs[-3:]
     cut, dets = early_ref.shape[0], operands[0].shape[0]
     copies = [
         pltpu.make_async_copy(early_ref, out_hbm.at[pl.ds(0, cut)], sem.at[0]),
         pltpu.make_async_copy(late_ref, out_hbm.at[pl.ds(cut, dets - cut)], sem.at[1]),
     ]
     copies[0].start()
-    late_ref[...] = clean_rows(modes, slice(cut, dets), *operands)
+    late_ref[...] = clean_rows(slice(cut, dets), q3_ref[...], *operands)
     copies[1].start()
     for copy in copies:
         copy.wait()
@@ -469,13 +473,14 @@
         arrived2 = (lax.all_to_all(send, "tm", 0, 0),)
 
     cut = EARLY * dets // 4
-    operands = (ts, keep, g, v3, bq, sig, h2)
-    early, base, scale, same = pl.pallas_call(
+    operands = (ts, keep, g, v3, sig, h2)
+    early, q3, base, scale, same = pl.pallas_call(
         functools.partial(early_kernel, seg, kblk, digits, modes),
         in_specs=[VM] * (8 + len(arrived1)),
-        out_specs=[VM] * 4,
+        out_specs=[VM] * 5,
         out_shape=[
             shape((cut, samples), BF16),
+            shape((LANES, samples), BF16),
             shape((LANES, LANES)),
             shape((LANES, LANES)),
             shape((lane_blocks, LANES, LANES), BF16),
@@ -483,14 +488,14 @@
         cost_estimate=pl.CostEstimate(flops=5 * 10**8, bytes_accessed=2 * 10**6, transcendentals=0),
         compiler_params=GRANT,
         name="early",
-    )(*operands, vec, *arrived1)
+    )(*operands, bq, vec, *arrived1)
     after = vec
     if paired:
         far, base = lax.optimization_barrier((far, base))
         arrived2 = (send, near, far, lax.ppermute(far, "tm", mates))
         after = far
     cleaned = pl.pallas_call(
-        functools.partial(late_kernel, modes),
+        late_kernel,
         in_specs=[VM] * 9,
         out_specs=HB,
         out_shape=shape((dets, samples), BF16),
@@ -498,7 +503,7 @@
         cost_estimate=pl.CostEstimate(flops=5 * 10**8, bytes_accessed=2 * 10**6, transcendentals=0),
         compiler_params=GRANT,
         name="late",
-    )(*operands, early, after)
+    )(*operands, q3, early, after)
 
     tile = pl.pallas_call(
         tile_kernel,

time: 30.5 us -> 30.4 us (level)
  transfers between devices with their start and end apart: 11 -> 11, of which waited for: 7 -> 6; matrix products, arithmetic and copies ran while one was open for 0% -> 0% of each run, Pallas kernels for 8% -> 7%
where the time goes in v7:
time: 30.4 us; the launch traced here: 30.2 us
  starting transfers between devices  12.9 us (42%)
  Pallas kernels  8.11 us (27%)
  waiting for transfers between devices  7.75 us (25%)
  between operations  0.71 us (2%)
  local copies, waits for them, and re-layouts  0.69 us (2%)
    ppermute x3, waiting for transfers between devices, others(): return [lax.ppermute(x, axis, p) for p in pairs]  4.22 us
    ppermute x3, starting transfers between devices, others(): return [lax.ppermute(x, axis, p) for p in pairs]  4.15 us
    ppermute x1, starting transfers between devices, shards(): far = lax.ppermute(pair, 'tm', fars)  2.66 us
    pallas_call x1, Pallas kernels, shards(): pl.pallas_call(functools.partial(prep_kernel, seg, kblk, digits), in_spec...  2.22 us
    ppermute x1, starting transfers between devices, shards(): far = lax.ppermute(send, 'tm', fars)  2.08 us
    pallas_call x1, Pallas kernels, shards(): pl.pallas_call(functools.partial(sums_kernel, modes), in_specs=[HB] * 4,...  1.99 us
    ppermute x1, starting transfers between devices, shards(): near = lax.ppermute(send, 'tm', nears)  1.83 us
    ppermute x1, starting transfers between devices, shards(): near = lax.ppermute(pair, 'tm', nears)  1.58 us
  transfers between devices with their start and end apart: 11, of which 6 were waited for; matrix products, arithmetic and copies ran while one was open for 0% of the time, Pallas kernels for 7%

profile of v7, /device:TPU:0, one launch (start us, length us, event | category | flops | bytes accessed | tf_op | source)
XLA Modules:
  0.0 30.2 jit_solution(2197665411446879001)
XLA Ops:
  0.6 0.7 %reshape.11.gain_ref = f32[1,257]{1,0:T(1,128)S(1)} reshape(f32[257]{0:T(512)} %param.18) | data formatting | bytes 2056 | tf_op jit(solution)/shard_map/reshape | solution.py:429
  1.3 2.0 %sums.1 = (bf16[72,512]{1,0:T(8,128)(2,1)S(1)}, f32[512,512]{1,0:T(8,128)S(1)}, bf16[512,512]{1,0:T(8,128)(2,1)S(1)}, f32[32,512]{1,0:T(8,128)S(1)}, f32[1,512]{1,0:T(1,128)S(1)}) custom-call(f32[512,512]{1,0:T(8,128)} %ts_hbm.1, s32[512,512]{1,0:T(8,128)} %flag_hbm.1, f32[32,512]{1,0:T(8,128)} %bitcast.2, f32[1,512]{1,0:T(1,128)} %bitcast.3), custom_call_target="tpu_custom_call" | custom-call | tf_op jit(solution)/shard_map/sums/pallas_call | solution.py:384
  3.3 2.2 %prep.1 = (bf16[1024,512]{1,0:T(8,128)(2,1)S(1)}, bf16[512,256]{1,0:T(8,128)(2,1)S(1)}, bf16[1024,512]{1,0:T(8,128)(2,1)S(1)}, bf16[512,128]{1,0:T(8,128)(2,1)S(1)}, bf16[24,128]{1,0:T(8,128)(2,1)S(1)}) custom-call(s32[4,4]{1,0:T(4,128)} %tids_hbm.1, s32[4,4]{1,0:T(4,128)} %offs_hbm.1, s32[32]{0:T(128)} %owner_hbm.1, f32[384,512]{1,0:T(8,128)} %constant.2.clone.cos_hbm, ...), custom_call_target="tpu_custom_call" | custom-call | flops 100000000 | bytes 3000000 | tf_op jit(solution)/shard_map/prep/pallas_call | solution.py:406
  5.5 0.6 %collective-permute-start.7 = (bf16[1024,512]{1,0:T(8,128)(2,1)S(1)}, bf16[1024,512]{1,0:T(8,128)(2,1)S(1)}, u32[]{:S(2)}, u32[]{:S(2)}) collective-permute-start(bf16[1024,512]{1,0:T(8,128)(2,1)S(1)} %get-tuple-element.27.pnt_ref), channel_id=1, source_target_pairs={{0,1},{1,0},{2,3},{3,2},{4,5},{5,4},{6,7},{7,6},{8,9},{9,8},{10,11... | collective-permute-start | bytes 3145736 | tf_op jit(solution)/shard_map/ppermute | solution.py:447
  6.1 3.5 %collective-permute-start.2 = (bf16[72,512]{1,0:T(8,128)(2,1)S(1)}, bf16[72,512]{1,0:T(8,128)(2,1)S(1)}, u32[]{:S(2)}, u32[]{:S(2)}) collective-permute-start(bf16[72,512]{1,0:T(8,128)(2,1)S(1)} %get-tuple-element.24.m0), channel_id=1, source_target_pairs={{0,24},{8,16},{16,8},{24,0},{1,25},{9,17},{17,9},{25,1},{2,26},{10... | collective-permute-start | bytes 221192 | tf_op jit(solution)/shard_map/ppermute | solution.py:371
  9.6 0.5 %collective-permute-start.1 = (bf16[72,512]{1,0:T(8,128)(2,1)S(1)}, bf16[72,512]{1,0:T(8,128)(2,1)S(1)}, u32[]{:S(2)}, u32[]{:S(2)}) collective-permute-start(bf16[72,512]{1,0:T(8,128)(2,1)S(1)} %get-tuple-element.24.m0), channel_id=1, source_target_pairs={{0,16},{8,24},{16,0},{24,8},{1,17},{9,25},{17,1},{25,9},{2,18},{10... | collective-permute-start | bytes 221192 | tf_op jit(solution)/shard_map/ppermute | solution.py:371
  10.1 0.1 collective-permute-start
  10.2 2.2 %collective-permute-done.2.m3 = bf16[72,512]{1,0:T(8,128)(2,1)S(1)} collective-permute-done((bf16[72,512]{1,0:T(8,128)(2,1)S(1)}, bf16[72,512]{1,0:T(8,128)(2,1)S(1)}, u32[]{:S(2)}, u32[]{:S(2)}) %collective-permute-start.2) | collective-permute-done | bytes 73760 | tf_op jit(solution)/shard_map/ppermute | solution.py:371
  12.5 1.6 %collective-permute-done.1.m2 = bf16[72,512]{1,0:T(8,128)(2,1)S(1)} collective-permute-done((bf16[72,512]{1,0:T(8,128)(2,1)S(1)}, bf16[72,512]{1,0:T(8,128)(2,1)S(1)}, u32[]{:S(2)}, u32[]{:S(2)}) %collective-permute-start.1) | collective-permute-done | bytes 73760 | tf_op jit(solution)/shard_map/ppermute | solution.py:371
  14.0 0.4 %collective-permute-done.m1 = bf16[72,512]{1,0:T(8,128)(2,1)S(1)} collective-permute-done((bf16[72,512]{1,0:T(8,128)(2,1)S(1)}, bf16[72,512]{1,0:T(8,128)(2,1)S(1)}, u32[]{:S(2)}, u32[]{:S(2)}) %collective-permute-start) | collective-permute-done | bytes 73760 | tf_op jit(solution)/shard_map/ppermute | solution.py:371
  14.5 0.4 %first.1 = (f32[64,512]{1,0:T(8,128)S(1)}, f32[8,512]{1,0:T(8,128)S(1)}, bf16[1,56,128]{2,1,0:T(8,128)(2,1)S(1)}) custom-call(bf16[72,512]{1,0:T(8,128)(2,1)S(1)} %get-tuple-element.24.m0, bf16[72,512]{1,0:T(8,128)(2,1)S(1)} %collective-permute-done.m1, bf16[72,512]{1,0:T(8,128)(2,1)S(1)} %collective-permute-done.1.m2, ...), custom_call_target="tpu_custom_call" | custom-call | tf_op jit(solution)/shard_map/first/pallas_call | solution.py:438
  14.9 0.0 collective-permute-start.3
  14.9 1.2 %collective-permute-done.3.mate_ref = bf16[1,56,128]{2,1,0:T(8,128)(2,1)S(1)} collective-permute-done((bf16[1,56,128]{2,1,0:T(8,128)(2,1)S(1)}, bf16[1,56,128]{2,1,0:T(8,128)(2,1)S(1)}, u32[]{:S(2)}, u32[]{:S(2)}) %collective-permute-start.3) | collective-permute-done | bytes 14368 | tf_op jit(solution)/shard_map/ppermute | solution.py:448
  16.1 2.7 %collective-permute-start.5 = (bf16[2,40,128]{2,1,0:T(8,128)(2,1)S(1)}, bf16[2,40,128]{2,1,0:T(8,128)(2,1)S(1)}, u32[]{:S(2)}, u32[]{:S(2)}) collective-permute-start(bf16[2,40,128]{2,1,0:T(8,128)(2,1)S(1)} %pad_maximum_fusion.pair_ref.refs_8_), channel_id=1, source_target_pairs={{0,4},{1,7},{2,6},{3,5},{4,0},{5,3},{6,2},{7,1},{8,12},{9,15},{10,... | collective-permute-start | bytes 61448 | tf_op jit(solution)/shard_map/ppermute | solution.py:451
  18.7 1.6 %collective-permute-start.4 = (bf16[2,40,128]{2,1,0:T(8,128)(2,1)S(1)}, bf16[2,40,128]{2,1,0:T(8,128)(2,1)S(1)}, u32[]{:S(2)}, u32[]{:S(2)}) collective-permute-start(bf16[2,40,128]{2,1,0:T(8,128)(2,1)S(1)} %pad_maximum_fusion.pair_ref.refs_8_), channel_id=1, source_target_pairs={{0,2},{1,3},{2,0},{3,1},{4,6},{5,7},{6,4},{7,5},{8,10},{9,11},{10,... | collective-permute-start | bytes 61448 | tf_op jit(solution)/shard_map/ppermute | solution.py:450
  20.3 0.7 %collective-permute-done.5.far_ref.refs_10_ = bf16[2,40,128]{2,1,0:T(8,128)(2,1)S(1)} collective-permute-done((bf16[2,40,128]{2,1,0:T(8,128)(2,1)S(1)}, bf16[2,40,128]{2,1,0:T(8,128)(2,1)S(1)}, u32[]{:S(2)}, u32[]{:S(2)}) %collective-permute-start.5) | collective-permute-done | bytes 20512 | tf_op jit(solution)/shard_map/ppermute | solution.py:451
  21.0 0.0 collective-permute-start.6
  21.0 1.6 %collective-permute-done.4.near_ref.refs_9_ = bf16[2,40,128]{2,1,0:T(8,128)(2,1)S(1)} collective-permute-done((bf16[2,40,128]{2,1,0:T(8,128)(2,1)S(1)}, bf16[2,40,128]{2,1,0:T(8,128)(2,1)S(1)}, u32[]{:S(2)}, u32[]{:S(2)}) %collective-permute-start.4) | collective-permute-done | bytes 20512 | tf_op jit(solution)/shard_map/ppermute | solution.py:450
  22.6 0.0 collective-permute-done.6.cross_ref.refs_11_
  22.6 0.0 collective-permute-done.7.mate_pnt_ref
  22.6 0.9 %second.1 = (f32[8,512]{1,0:T(8,128)S(1)}, bf16[2,16,128]{2,1,0:T(8,128)(2,1)S(1)}) custom-call(bf16[2,40,128]{2,1,0:T(8,128)(2,1)S(1)} %pad_maximum_fusion.pair_ref.refs_8_, bf16[2,40,128]{2,1,0:T(8,128)(2,1)S(1)} %collective-permute-done.4.near_ref.refs_9_, bf16[2,40,128]{2,1,0:T(8,128)(2,1)S(1)} %collective-permute-done.5.far_ref.refs_10_, ...), custom_call_target="tpu_custom_call" | custom-call | tf_op jit(solution)/shard_map/second/pallas_call | solution.py:453
  23.5 2.1 %collective-permute-start.9 = (bf16[2,16,128]{2,1,0:T(8,128)(2,1)S(1)}, bf16[2,16,128]{2,1,0:T(8,128)(2,1)S(1)}, u32[]{:S(2)}, u32[]{:S(2)}) collective-permute-start(bf16[2,16,128]{2,1,0:T(8,128)(2,1)S(1)} %get-tuple-element.31.refs_0_), channel_id=1, source_target_pairs={{0,4},{1,7},{2,6},{3,5},{4,0},{5,3},{6,2},{7,1},{8,12},{9,15},{10,... | collective-permute-start | bytes 24584 | tf_op jit(solution)/shard_map/ppermute | solution.py:462
  25.6 1.8 %collective-permute-start.8 = (bf16[2,16,128]{2,1,0:T(8,128)(2,1)S(1)}, bf16[2,16,128]{2,1,0:T(8,128)(2,1)S(1)}, u32[]{:S(2)}, u32[]{:S(2)}) collective-permute-start(bf16[2,16,128]{2,1,0:T(8,128)(2,1)S(1)} %get-tuple-element.31.refs_0_), channel_id=1, source_target_pairs={{0,2},{1,3},{2,0},{3,1},{4,6},{5,7},{6,4},{7,5},{8,10},{9,11},{10,... | collective-permute-start | bytes 24584 | tf_op jit(solution)/shard_map/ppermute | solution.py:461
  27.4 0.8 %early.1 = (bf16[384,512]{1,0:T(8,128)(2,1)S(1)}, bf16[128,512]{1,0:T(8,128)(2,1)S(1)}, f32[128,128]{1,0:T(8,128)S(1)}, f32[128,128]{1,0:T(8,128)S(1)}, bf16[1,128,128]{2,1,0:T(8,128)(2,1)S(1)}) custom-call(f32[512,512]{1,0:T(8,128)S(1)} %get-tuple-element.32.refs_0_, bf16[512,512]{1,0:T(8,128)(2,1)S(1)} %get-tuple-element.33.refs_1_, ...), custom_call_target="tpu_custom_call" | custom-call | flops 500000000 | bytes 2000000 | tf_op jit(solution)/shard_map/early/pallas_call | solution.py:477
  28.2 0.0 collective-permute-done.9.refs_2_.refs_8_
  28.2 0.1 collective-permute-start.10
  28.3 1.1 %late.1 = bf16[512,512]{1,0:T(8,128)(2,1)} custom-call(f32[512,512]{1,0:T(8,128)S(1)} %get-tuple-element.32.refs_0_, bf16[512,512]{1,0:T(8,128)(2,1)S(1)} %get-tuple-element.33.refs_1_, f32[1,512]{1,0:T(1,128)S(1)} %get-tuple-element.34.refs_2_, bf16[512,128]{1,0:T(8,128)(2,1)S(1)} %get-tuple-element.35.refs_3_, f32[8,512]{1,0:T(8,128)S(1)} %get-tuple-element.36.refs_4_, ...), custom_call_target="tpu_custom_call" | custom-call | flops 500000000 | bytes 2000000 | tf_op jit(solution)/shard_map/late/pallas_call | solution.py:497
  29.4 0.0 collective-permute-done.8.refs_1_
  29.4 0.0 collective-permute-done.10.refs_3_
  29.4 0.8 %tile.1 = f32[1,128,128]{2,1,0:T(8,128)} custom-call(bf16[2,16,128]{2,1,0:T(8,128)(2,1)S(1)} %get-tuple-element.31.refs_0_, bf16[2,16,128]{2,1,0:T(8,128)(2,1)S(1)} %collective-permute-done.8.refs_1_, bf16[2,16,128]{2,1,0:T(8,128)(2,1)S(1)} %collective-permute-done.9.refs_2_.refs_8_, bf16[2,16,128]{2,1,0:T(8,128)(2,1)S(1)} %collective-permute-done.10.refs_3_, ...), custom_call_target="tpu_custom_call" | custom-call | tf_op jit(solution)/shard_map/tile/pallas_call | solution.py:508
  (3 shorter events, 0.0 us)
Async XLA Ops:
  5.5 17.1 %collective-permute-start.7 = (bf16[1024,512]{1,0:T(8,128)(2,1)S(1)}, bf16[1024,512]{1,0:T(8,128)(2,1)S(1)}, u32[]{:S(2)}, u32[]{:S(2)}) collective-permute-start(bf16[1024,512]{1,0:T(8,128)(2,1)S(1)} %get-tuple-element.27.pnt_ref), channel_id=1, source_target_pairs={{0,1},{1,0},{2,3},{3,2},{4,5},{5,4},{6,7},{7,6},{8,9},{9,8},{10,11... | collective-permute-start | bytes 3145736 | tf_op jit(solution)/shard_map/ppermute | solution.py:447
  6.1 6.4 %collective-permute-start.2 = (bf16[72,512]{1,0:T(8,128)(2,1)S(1)}, bf16[72,512]{1,0:T(8,128)(2,1)S(1)}, u32[]{:S(2)}, u32[]{:S(2)}) collective-permute-start(bf16[72,512]{1,0:T(8,128)(2,1)S(1)} %get-tuple-element.24.m0), channel_id=1, source_target_pairs={{0,24},{8,16},{16,8},{24,0},{1,25},{9,17},{17,9},{25,1},{2,26},{10... | collective-permute-start | bytes 221192 | tf_op jit(solution)/shard_map/ppermute | solution.py:371
  9.6 4.4 %collective-permute-start.1 = (bf16[72,512]{1,0:T(8,128)(2,1)S(1)}, bf16[72,512]{1,0:T(8,128)(2,1)S(1)}, u32[]{:S(2)}, u32[]{:S(2)}) collective-permute-start(bf16[72,512]{1,0:T(8,128)(2,1)S(1)} %get-tuple-element.24.m0), channel_id=1, source_target_pairs={{0,16},{8,24},{16,0},{24,8},{1,17},{9,25},{17,1},{25,9},{2,18},{10... | collective-permute-start | bytes 221192 | tf_op jit(solution)/shard_map/ppermute | solution.py:371
  10.1 4.4 %collective-permute-start = (bf16[72,512]{1,0:T(8,128)(2,1)S(1)}, bf16[72,512]{1,0:T(8,128)(2,1)S(1)}, u32[]{:S(2)}, u32[]{:S(2)}) collective-permute-start(bf16[72,512]{1,0:T(8,128)(2,1)S(1)} %get-tuple-element.24.m0), channel_id=1, source_target_pairs={{0,8},{8,0},{16,24},{24,16},{1,9},{9,1},{17,25},{25,17},{2,10},{10... | collective-permute-start | bytes 221192 | tf_op jit(solution)/shard_map/ppermute | solution.py:371
  14.9 1.2 %collective-permute-start.3 = (bf16[1,56,128]{2,1,0:T(8,128)(2,1)S(1)}, bf16[1,56,128]{2,1,0:T(8,128)(2,1)S(1)}, u32[]{:S(2)}, u32[]{:S(2)}) collective-permute-start(bf16[1,56,128]{2,1,0:T(8,128)(2,1)S(1)} %get-tuple-element.29), channel_id=1, source_target_pairs={{0,1},{1,0},{2,3},{3,2},{4,5},{5,4},{6,7},{7,6},{8,9},{9,8},{10,11... | collective-permute-start | bytes 43016 | tf_op jit(solution)/shard_map/ppermute | solution.py:448
  16.1 5.0 %collective-permute-start.5 = (bf16[2,40,128]{2,1,0:T(8,128)(2,1)S(1)}, bf16[2,40,128]{2,1,0:T(8,128)(2,1)S(1)}, u32[]{:S(2)}, u32[]{:S(2)}) collective-permute-start(bf16[2,40,128]{2,1,0:T(8,128)(2,1)S(1)} %pad_maximum_fusion.pair_ref.refs_8_), channel_id=1, source_target_pairs={{0,4},{1,7},{2,6},{3,5},{4,0},{5,3},{6,2},{7,1},{8,12},{9,15},{10,... | collective-permute-start | bytes 61448 | tf_op jit(solution)/shard_map/ppermute | solution.py:451
  18.7 3.9 %collective-permute-start.4 = (bf16[2,40,128]{2,1,0:T(8,128)(2,1)S(1)}, bf16[2,40,128]{2,1,0:T(8,128)(2,1)S(1)}, u32[]{:S(2)}, u32[]{:S(2)}) collective-permute-start(bf16[2,40,128]{2,1,0:T(8,128)(2,1)S(1)} %pad_maximum_fusion.pair_ref.refs_8_), channel_id=1, source_target_pairs={{0,2},{1,3},{2,0},{3,1},{4,6},{5,7},{6,4},{7,5},{8,10},{9,11},{10,... | collective-permute-start | bytes 61448 | tf_op jit(solution)/shard_map/ppermute | solution.py:450
  21.0 1.6 %collective-permute-start.6 = (bf16[2,40,128]{2,1,0:T(8,128)(2,1)S(1)}, bf16[2,40,128]{2,1,0:T(8,128)(2,1)S(1)}, u32[]{:S(2)}, u32[]{:S(2)}) collective-permute-start(bf16[2,40,128]{2,1,0:T(8,128)(2,1)S(1)} %collective-permute-done.5.far_ref.refs_10_), channel_id=1, source_target_pairs={{0,1},{1,0},{2,3},{3,2},{4,5},{5,4},{6,7},{7,6},{8,9},{9,8},{10,11... | collective-permute-start | bytes 61448 | tf_op jit(solution)/shard_map/ppermute | solution.py:452
  23.5 4.7 %collective-permute-start.9 = (bf16[2,16,128]{2,1,0:T(8,128)(2,1)S(1)}, bf16[2,16,128]{2,1,0:T(8,128)(2,1)S(1)}, u32[]{:S(2)}, u32[]{:S(2)}) collective-permute-start(bf16[2,16,128]{2,1,0:T(8,128)(2,1)S(1)} %get-tuple-element.31.refs_0_), channel_id=1, source_target_pairs={{0,4},{1,7},{2,6},{3,5},{4,0},{5,3},{6,2},{7,1},{8,12},{9,15},{10,... | collective-permute-start | bytes 24584 | tf_op jit(solution)/shard_map/ppermute | solution.py:462
  25.6 3.8 %collective-permute-start.8 = (bf16[2,16,128]{2,1,0:T(8,128)(2,1)S(1)}, bf16[2,16,128]{2,1,0:T(8,128)(2,1)S(1)}, u32[]{:S(2)}, u32[]{:S(2)}) collective-permute-start(bf16[2,16,128]{2,1,0:T(8,128)(2,1)S(1)} %get-tuple-element.31.refs_0_), channel_id=1, source_target_pairs={{0,2},{1,3},{2,0},{3,1},{4,6},{5,7},{6,4},{7,5},{8,10},{9,11},{10,... | collective-permute-start | bytes 24584 | tf_op jit(solution)/shard_map/ppermute | solution.py:461
  28.2 1.2 %collective-permute-start.10 = (bf16[2,16,128]{2,1,0:T(8,128)(2,1)S(1)}, bf16[2,16,128]{2,1,0:T(8,128)(2,1)S(1)}, u32[]{:S(2)}, u32[]{:S(2)}) collective-permute-start(bf16[2,16,128]{2,1,0:T(8,128)(2,1)S(1)} %collective-permute-done.9.refs_2_.refs_8_), channel_id=1, source_target_pairs={{0,1},{1,0},{2,3},{3,2},{4,5},{5,4},{6,7},{7,6},{8,9},{9,8},{10,11... | collective-permute-start | bytes 24584 | tf_op jit(solution)/shard_map/ppermute | solution.py:495

commit v8 on v7

--- a/solution.py
+++ b/solution.py
@@ -181,9 +181,8 @@
 
 
 def first_kernel(modes, seg, kblk, m0, m1, m2, m3, toep_ref, pnt_ref, geo_ref,
-                 bq_ref, vec_ref, send_ref):
+                 vec_ref, send_ref):
     tot = m0[...].astype(F32) + m1[...].astype(F32) + m2[...].astype(F32) + m3[...].astype(F32)
-    bq_ref[...] = tot[0 : 2 * modes]
     ext = tot[2 * modes :]
     u_row = ext[4:5, 0:LANES] + ext[5:6, 0:LANES]
     u_col = jnp.sum(jnp.where(iota((modes, LANES), 0) == iota((modes, LANES), 1), u_row, 0.0), axis=1, keepdims=True)
@@ -291,8 +290,9 @@
     send_ref[1] = project(mate_z, mate_pnt_ref[0:samples], seg, kblk).astype(BF16)
 
 
-def stacked_modes(modes, bq_ref, sig_ref):
-    q_hi, q_lo = split(bq_ref[0:modes] - bq_ref[modes : 2 * modes] * sig_ref[0:1])
+def stacked_modes(modes, messages, sig_ref):
+    tot = sum(message[0 : 2 * modes].astype(F32) for message in messages)
+    q_hi, q_lo = split(tot[0:modes] - tot[modes:] * sig_ref[0:1])
     pad = jnp.zeros((LANES - 3 * modes, q_hi.shape[1]), BF16)
     return jnp.concatenate([q_hi, q_lo, q_hi, pad], axis=0)
 
@@ -308,10 +308,10 @@
     return (mm(rest, h2_ref[0:samples]) + mm(rest, h2_ref[samples:])).astype(BF16)
 
 
-def early_kernel(seg, kblk, digits, modes, *refs):
-    operands, bq_ref, vec_ref, all_refs = refs[:6], refs[6], refs[7], refs[8:-5]
+def early_kernel(seg, kblk, digits, modes, count, *refs):
+    operands, messages, vec_ref, all_refs = refs[:6], refs[6 : 6 + count], refs[6 + count], refs[7 + count : -5]
     early_ref, q3_ref, base_ref, scale_ref, same_ref = refs[-5:]
-    q3 = stacked_modes(modes, bq_ref, operands[4])
+    q3 = stacked_modes(modes, messages, operands[4])
     q3_ref[...] = q3
     early_ref[...] = clean_rows(slice(0, early_ref.shape[0]), q3, *operands)
     psum = jnp.zeros((LANES, LANES), F32)
@@ -435,11 +435,11 @@
     fars = [(i, i ^ (4 + 2 * (i % 2))) for i in range(n_tm)]
     block = 2 * listed + id_rows
     first_shape = (1, block + 4 * samples // LANES, LANES) if paired else (n_tm, block, LANES)
-    bq, vec, send = pl.pallas_call(
+    vec, send = pl.pallas_call(
         functools.partial(first_kernel, modes, seg, kblk),
         in_specs=[VM] * 7,
-        out_specs=[VM] * 3,
-        out_shape=[shape((2 * modes, samples)), shape((8, samples)), shape(first_shape, BF16)],
+        out_specs=[VM] * 2,
+        out_shape=[shape((8, samples)), shape(first_shape, BF16)],
         compiler_params=GRANT,
         name="first",
     )(*parts_of_all, toep, pnt, geo)
@@ -475,8 +475,8 @@
     cut = EARLY * dets // 4
     operands = (ts, keep, g, v3, sig, h2)
     early, q3, base, scale, same = pl.pallas_call(
-        functools.partial(early_kernel, seg, kblk, digits, modes),
-        in_specs=[VM] * (8 + len(arrived1)),
+        functools.partial(early_kernel, seg, kblk, digits, modes, len(parts_of_all)),
+        in_specs=[VM] * (7 + len(parts_of_all) + len(arrived1)),
         out_specs=[VM] * 5,
         out_shape=[
             shape((cut, samples), BF16),
@@ -488,7 +488,7 @@
         cost_estimate=pl.CostEstimate(flops=5 * 10**8, bytes_accessed=2 * 10**6, transcendentals=0),
         compiler_params=GRANT,
         name="early",
-    )(*operands, bq, vec, *arrived1)
+    )(*operands, *parts_of_all, vec, *arrived1)
     after = vec
     if paired:
         far, base = lax.optimization_barrier((far, base))

time: 30.4 us -> 30.4 us (level)
  transfers between devices with their start and end apart: 11 -> 11, of which waited for: 6 -> 6; matrix products, arithmetic and copies ran while one was open for 0% -> 0% of each run, Pallas kernels for 7% -> 8%
where the time goes in v8:
time: 30.4 us; the launch traced here: 30.2 us
  starting transfers between devices  12.9 us (42%)
  Pallas kernels  8.14 us (27%)
  waiting for transfers between devices  7.75 us (25%)
  between operations  0.71 us (2%)
  local copies, waits for them, and re-layouts  0.69 us (2%)
    ppermute x3, waiting for transfers between devices, others(): return [lax.ppermute(x, axis, p) for p in pairs]  4.22 us
    ppermute x3, starting transfers between devices, others(): return [lax.ppermute(x, axis, p) for p in pairs]  4.15 us
    ppermute x1, starting transfers between devices, shards(): far = lax.ppermute(pair, 'tm', fars)  2.65 us
    pallas_call x1, Pallas kernels, shards(): pl.pallas_call(functools.partial(prep_kernel, seg, kblk, digits), in_spec...  2.22 us
    ppermute x1, starting transfers between devices, shards(): far = lax.ppermute(send, 'tm', fars)  2.08 us
    pallas_call x1, Pallas kernels, shards(): pl.pallas_call(functools.partial(sums_kernel, modes), in_specs=[HB] * 4,...  1.99 us
    ppermute x1, starting transfers between devices, shards(): near = lax.ppermute(send, 'tm', nears)  1.83 us
    ppermute x1, starting transfers between devices, shards(): near = lax.ppermute(pair, 'tm', nears)  1.58 us
  transfers between devices with their start and end apart: 11, of which 6 were waited for; matrix products, arithmetic and copies ran while one was open for 0% of the time, Pallas kernels for 8%

profile of v8, /device:TPU:0, one launch (start us, length us, event | category | flops | bytes accessed | tf_op | source)
XLA Modules:
  0.0 30.2 jit_solution(12409217827101188109)
XLA Ops:
  0.6 0.7 %reshape.11.gain_ref = f32[1,257]{1,0:T(1,128)S(1)} reshape(f32[257]{0:T(512)} %param.18) | data formatting | bytes 2056 | tf_op jit(solution)/shard_map/reshape | solution.py:429
  1.3 2.0 %sums.1 = (bf16[72,512]{1,0:T(8,128)(2,1)S(1)}, f32[512,512]{1,0:T(8,128)S(1)}, bf16[512,512]{1,0:T(8,128)(2,1)S(1)}, f32[32,512]{1,0:T(8,128)S(1)}, f32[1,512]{1,0:T(1,128)S(1)}) custom-call(f32[512,512]{1,0:T(8,128)} %ts_hbm.1, s32[512,512]{1,0:T(8,128)} %flag_hbm.1, f32[32,512]{1,0:T(8,128)} %bitcast.2, f32[1,512]{1,0:T(1,128)} %bitcast.3), custom_call_target="tpu_custom_call" | custom-call | tf_op jit(solution)/shard_map/sums/pallas_call | solution.py:384
  3.3 2.2 %prep.1 = (bf16[1024,512]{1,0:T(8,128)(2,1)S(1)}, bf16[512,256]{1,0:T(8,128)(2,1)S(1)}, bf16[1024,512]{1,0:T(8,128)(2,1)S(1)}, bf16[512,128]{1,0:T(8,128)(2,1)S(1)}, bf16[24,128]{1,0:T(8,128)(2,1)S(1)}) custom-call(s32[4,4]{1,0:T(4,128)} %tids_hbm.1, s32[4,4]{1,0:T(4,128)} %offs_hbm.1, s32[32]{0:T(128)} %owner_hbm.1, f32[384,512]{1,0:T(8,128)} %constant.2.clone.cos_hbm, ...), custom_call_target="tpu_custom_call" | custom-call | flops 100000000 | bytes 3000000 | tf_op jit(solution)/shard_map/prep/pallas_call | solution.py:406
  5.5 0.6 %collective-permute-start.7 = (bf16[1024,512]{1,0:T(8,128)(2,1)S(1)}, bf16[1024,512]{1,0:T(8,128)(2,1)S(1)}, u32[]{:S(2)}, u32[]{:S(2)}) collective-permute-start(bf16[1024,512]{1,0:T(8,128)(2,1)S(1)} %get-tuple-element.26.pnt_ref), channel_id=1, source_target_pairs={{0,1},{1,0},{2,3},{3,2},{4,5},{5,4},{6,7},{7,6},{8,9},{9,8},{10,11... | collective-permute-start | bytes 3145736 | tf_op jit(solution)/shard_map/ppermute | solution.py:447
  6.1 3.5 %collective-permute-start.2 = (bf16[72,512]{1,0:T(8,128)(2,1)S(1)}, bf16[72,512]{1,0:T(8,128)(2,1)S(1)}, u32[]{:S(2)}, u32[]{:S(2)}) collective-permute-start(bf16[72,512]{1,0:T(8,128)(2,1)S(1)} %get-tuple-element.23.m0.refs_6_), channel_id=1, source_target_pairs={{0,24},{8,16},{16,8},{24,0},{1,25},{9,17},{17,9},{25,1},{2,26},{10... | collective-permute-start | bytes 221192 | tf_op jit(solution)/shard_map/ppermute | solution.py:371
  9.6 0.5 %collective-permute-start.1 = (bf16[72,512]{1,0:T(8,128)(2,1)S(1)}, bf16[72,512]{1,0:T(8,128)(2,1)S(1)}, u32[]{:S(2)}, u32[]{:S(2)}) collective-permute-start(bf16[72,512]{1,0:T(8,128)(2,1)S(1)} %get-tuple-element.23.m0.refs_6_), channel_id=1, source_target_pairs={{0,16},{8,24},{16,0},{24,8},{1,17},{9,25},{17,1},{25,9},{2,18},{10... | collective-permute-start | bytes 221192 | tf_op jit(solution)/shard_map/ppermute | solution.py:371
  10.1 0.1 collective-permute-start
  10.2 2.2 %collective-permute-done.2.m3.refs_9_ = bf16[72,512]{1,0:T(8,128)(2,1)S(1)} collective-permute-done((bf16[72,512]{1,0:T(8,128)(2,1)S(1)}, bf16[72,512]{1,0:T(8,128)(2,1)S(1)}, u32[]{:S(2)}, u32[]{:S(2)}) %collective-permute-start.2) | collective-permute-done | bytes 73760 | tf_op jit(solution)/shard_map/ppermute | solution.py:371
  12.5 1.6 %collective-permute-done.1.m2.refs_8_ = bf16[72,512]{1,0:T(8,128)(2,1)S(1)} collective-permute-done((bf16[72,512]{1,0:T(8,128)(2,1)S(1)}, bf16[72,512]{1,0:T(8,128)(2,1)S(1)}, u32[]{:S(2)}, u32[]{:S(2)}) %collective-permute-start.1) | collective-permute-done | bytes 73760 | tf_op jit(solution)/shard_map/ppermute | solution.py:371
  14.0 0.4 %collective-permute-done.m1.refs_7_ = bf16[72,512]{1,0:T(8,128)(2,1)S(1)} collective-permute-done((bf16[72,512]{1,0:T(8,128)(2,1)S(1)}, bf16[72,512]{1,0:T(8,128)(2,1)S(1)}, u32[]{:S(2)}, u32[]{:S(2)}) %collective-permute-start) | collective-permute-done | bytes 73760 | tf_op jit(solution)/shard_map/ppermute | solution.py:371
  14.5 0.4 %first.1 = (f32[8,512]{1,0:T(8,128)S(1)}, bf16[1,56,128]{2,1,0:T(8,128)(2,1)S(1)}) custom-call(bf16[72,512]{1,0:T(8,128)(2,1)S(1)} %get-tuple-element.23.m0.refs_6_, bf16[72,512]{1,0:T(8,128)(2,1)S(1)} %collective-permute-done.m1.refs_7_, bf16[72,512]{1,0:T(8,128)(2,1)S(1)} %collective-permute-done.1.m2.refs_8_, ...), custom_call_target="tpu_custom_call" | custom-call | tf_op jit(solution)/shard_map/first/pallas_call | solution.py:438
  14.9 0.0 collective-permute-start.3
  14.9 1.2 %collective-permute-done.3.mate_ref = bf16[1,56,128]{2,1,0:T(8,128)(2,1)S(1)} collective-permute-done((bf16[1,56,128]{2,1,0:T(8,128)(2,1)S(1)}, bf16[1,56,128]{2,1,0:T(8,128)(2,1)S(1)}, u32[]{:S(2)}, u32[]{:S(2)}) %collective-permute-start.3) | collective-permute-done | bytes 14368 | tf_op jit(solution)/shard_map/ppermute | solution.py:448
  16.1 2.7 %collective-permute-start.5 = (bf16[2,40,128]{2,1,0:T(8,128)(2,1)S(1)}, bf16[2,40,128]{2,1,0:T(8,128)(2,1)S(1)}, u32[]{:S(2)}, u32[]{:S(2)}) collective-permute-start(bf16[2,40,128]{2,1,0:T(8,128)(2,1)S(1)} %pad_maximum_fusion.pair_ref.refs_11_), channel_id=1, source_target_pairs={{0,4},{1,7},{2,6},{3,5},{4,0},{5,3},{6,2},{7,1},{8,12},{9,15},{10,... | collective-permute-start | bytes 61448 | tf_op jit(solution)/shard_map/ppermute | solution.py:451
  18.7 1.6 %collective-permute-start.4 = (bf16[2,40,128]{2,1,0:T(8,128)(2,1)S(1)}, bf16[2,40,128]{2,1,0:T(8,128)(2,1)S(1)}, u32[]{:S(2)}, u32[]{:S(2)}) collective-permute-start(bf16[2,40,128]{2,1,0:T(8,128)(2,1)S(1)} %pad_maximum_fusion.pair_ref.refs_11_), channel_id=1, source_target_pairs={{0,2},{1,3},{2,0},{3,1},{4,6},{5,7},{6,4},{7,5},{8,10},{9,11},{10,... | collective-permute-start | bytes 61448 | tf_op jit(solution)/shard_map/ppermute | solution.py:450
  20.3 0.7 %collective-permute-done.5.far_ref.refs_13_ = bf16[2,40,128]{2,1,0:T(8,128)(2,1)S(1)} collective-permute-done((bf16[2,40,128]{2,1,0:T(8,128)(2,1)S(1)}, bf16[2,40,128]{2,1,0:T(8,128)(2,1)S(1)}, u32[]{:S(2)}, u32[]{:S(2)}) %collective-permute-start.5) | collective-permute-done | bytes 20512 | tf_op jit(solution)/shard_map/ppermute | solution.py:451
  21.0 0.0 collective-permute-start.6
  21.0 1.6 %collective-permute-done.4.near_ref.refs_12_ = bf16[2,40,128]{2,1,0:T(8,128)(2,1)S(1)} collective-permute-done((bf16[2,40,128]{2,1,0:T(8,128)(2,1)S(1)}, bf16[2,40,128]{2,1,0:T(8,128)(2,1)S(1)}, u32[]{:S(2)}, u32[]{:S(2)}) %collective-permute-start.4) | collective-permute-done | bytes 20512 | tf_op jit(solution)/shard_map/ppermute | solution.py:450
  22.6 0.0 collective-permute-done.6.cross_ref.refs_14_
  22.6 0.0 collective-permute-done.7.mate_pnt_ref
  22.6 0.9 %second.1 = (f32[8,512]{1,0:T(8,128)S(1)}, bf16[2,16,128]{2,1,0:T(8,128)(2,1)S(1)}) custom-call(bf16[2,40,128]{2,1,0:T(8,128)(2,1)S(1)} %pad_maximum_fusion.pair_ref.refs_11_, bf16[2,40,128]{2,1,0:T(8,128)(2,1)S(1)} %collective-permute-done.4.near_ref.refs_12_, bf16[2,40,128]{2,1,0:T(8,128)(2,1)S(1)} %collective-permute-done.5.far_ref.refs_13_, ...), custom_call_target="tpu_custom_call" | custom-call | tf_op jit(solution)/shard_map/second/pallas_call | solution.py:453
  23.5 2.1 %collective-permute-start.9 = (bf16[2,16,128]{2,1,0:T(8,128)(2,1)S(1)}, bf16[2,16,128]{2,1,0:T(8,128)(2,1)S(1)}, u32[]{:S(2)}, u32[]{:S(2)}) collective-permute-start(bf16[2,16,128]{2,1,0:T(8,128)(2,1)S(1)} %get-tuple-element.30.refs_0_), channel_id=1, source_target_pairs={{0,4},{1,7},{2,6},{3,5},{4,0},{5,3},{6,2},{7,1},{8,12},{9,15},{10,... | collective-permute-start | bytes 24584 | tf_op jit(solution)/shard_map/ppermute | solution.py:462
  25.6 1.8 %collective-permute-start.8 = (bf16[2,16,128]{2,1,0:T(8,128)(2,1)S(1)}, bf16[2,16,128]{2,1,0:T(8,128)(2,1)S(1)}, u32[]{:S(2)}, u32[]{:S(2)}) collective-permute-start(bf16[2,16,128]{2,1,0:T(8,128)(2,1)S(1)} %get-tuple-element.30.refs_0_), channel_id=1, source_target_pairs={{0,2},{1,3},{2,0},{3,1},{4,6},{5,7},{6,4},{7,5},{8,10},{9,11},{10,... | collective-permute-start | bytes 24584 | tf_op jit(solution)/shard_map/ppermute | solution.py:461
  27.4 0.8 %early.1 = (bf16[384,512]{1,0:T(8,128)(2,1)S(1)}, bf16[128,512]{1,0:T(8,128)(2,1)S(1)}, f32[128,128]{1,0:T(8,128)S(1)}, f32[128,128]{1,0:T(8,128)S(1)}, bf16[1,128,128]{2,1,0:T(8,128)(2,1)S(1)}) custom-call(f32[512,512]{1,0:T(8,128)S(1)} %get-tuple-element.31.refs_0_, bf16[512,512]{1,0:T(8,128)(2,1)S(1)} %get-tuple-element.32.refs_1_, ...), custom_call_target="tpu_custom_call" | custom-call | flops 500000000 | bytes 2000000 | tf_op jit(solution)/shard_map/early/pallas_call | solution.py:477
  28.2 0.0 collective-permute-done.9.refs_2_.refs_8_
  28.2 0.1 collective-permute-start.10
  28.3 1.1 %late.1 = bf16[512,512]{1,0:T(8,128)(2,1)} custom-call(f32[512,512]{1,0:T(8,128)S(1)} %get-tuple-element.31.refs_0_, bf16[512,512]{1,0:T(8,128)(2,1)S(1)} %get-tuple-element.32.refs_1_, f32[1,512]{1,0:T(1,128)S(1)} %get-tuple-element.33.refs_2_, bf16[512,128]{1,0:T(8,128)(2,1)S(1)} %get-tuple-element.34.refs_3_, f32[8,512]{1,0:T(8,128)S(1)} %get-tuple-element.35.refs_4_, ...), custom_call_target="tpu_custom_call" | custom-call | flops 500000000 | bytes 2000000 | tf_op jit(solution)/shard_map/late/pallas_call | solution.py:497
  29.4 0.0 collective-permute-done.8.refs_1_
  29.4 0.0 collective-permute-done.10.refs_3_
  29.5 0.8 %tile.1 = f32[1,128,128]{2,1,0:T(8,128)} custom-call(bf16[2,16,128]{2,1,0:T(8,128)(2,1)S(1)} %get-tuple-element.30.refs_0_, bf16[2,16,128]{2,1,0:T(8,128)(2,1)S(1)} %collective-permute-done.8.refs_1_, bf16[2,16,128]{2,1,0:T(8,128)(2,1)S(1)} %collective-permute-done.9.refs_2_.refs_8_, bf16[2,16,128]{2,1,0:T(8,128)(2,1)S(1)} %collective-permute-done.10.refs_3_, ...), custom_call_target="tpu_custom_call" | custom-call | tf_op jit(solution)/shard_map/tile/pallas_call | solution.py:508
  (3 shorter events, 0.0 us)
Async XLA Ops:
  5.5 17.1 %collective-permute-start.7 = (bf16[1024,512]{1,0:T(8,128)(2,1)S(1)}, bf16[1024,512]{1,0:T(8,128)(2,1)S(1)}, u32[]{:S(2)}, u32[]{:S(2)}) collective-permute-start(bf16[1024,512]{1,0:T(8,128)(2,1)S(1)} %get-tuple-element.26.pnt_ref), channel_id=1, source_target_pairs={{0,1},{1,0},{2,3},{3,2},{4,5},{5,4},{6,7},{7,6},{8,9},{9,8},{10,11... | collective-permute-start | bytes 3145736 | tf_op jit(solution)/shard_map/ppermute | solution.py:447
  6.1 6.4 %collective-permute-start.2 = (bf16[72,512]{1,0:T(8,128)(2,1)S(1)}, bf16[72,512]{1,0:T(8,128)(2,1)S(1)}, u32[]{:S(2)}, u32[]{:S(2)}) collective-permute-start(bf16[72,512]{1,0:T(8,128)(2,1)S(1)} %get-tuple-element.23.m0.refs_6_), channel_id=1, source_target_pairs={{0,24},{8,16},{16,8},{24,0},{1,25},{9,17},{17,9},{25,1},{2,26},{10... | collective-permute-start | bytes 221192 | tf_op jit(solution)/shard_map/ppermute | solution.py:371
  9.6 4.4 %collective-permute-start.1 = (bf16[72,512]{1,0:T(8,128)(2,1)S(1)}, bf16[72,512]{1,0:T(8,128)(2,1)S(1)}, u32[]{:S(2)}, u32[]{:S(2)}) collective-permute-start(bf16[72,512]{1,0:T(8,128)(2,1)S(1)} %get-tuple-element.23.m0.refs_6_), channel_id=1, source_target_pairs={{0,16},{8,24},{16,0},{24,8},{1,17},{9,25},{17,1},{25,9},{2,18},{10... | collective-permute-start | bytes 221192 | tf_op jit(solution)/shard_map/ppermute | solution.py:371
  10.1 4.4 %collective-permute-start = (bf16[72,512]{1,0:T(8,128)(2,1)S(1)}, bf16[72,512]{1,0:T(8,128)(2,1)S(1)}, u32[]{:S(2)}, u32[]{:S(2)}) collective-permute-start(bf16[72,512]{1,0:T(8,128)(2,1)S(1)} %get-tuple-element.23.m0.refs_6_), channel_id=1, source_target_pairs={{0,8},{8,0},{16,24},{24,16},{1,9},{9,1},{17,25},{25,17},{2,10},{10... | collective-permute-start | bytes 221192 | tf_op jit(solution)/shard_map/ppermute | solution.py:371
  14.9 1.2 %collective-permute-start.3 = (bf16[1,56,128]{2,1,0:T(8,128)(2,1)S(1)}, bf16[1,56,128]{2,1,0:T(8,128)(2,1)S(1)}, u32[]{:S(2)}, u32[]{:S(2)}) collective-permute-start(bf16[1,56,128]{2,1,0:T(8,128)(2,1)S(1)} %get-tuple-element.28), channel_id=1, source_target_pairs={{0,1},{1,0},{2,3},{3,2},{4,5},{5,4},{6,7},{7,6},{8,9},{9,8},{10,11... | collective-permute-start | bytes 43016 | tf_op jit(solution)/shard_map/ppermute | solution.py:448
  16.1 5.0 %collective-permute-start.5 = (bf16[2,40,128]{2,1,0:T(8,128)(2,1)S(1)}, bf16[2,40,128]{2,1,0:T(8,128)(2,1)S(1)}, u32[]{:S(2)}, u32[]{:S(2)}) collective-permute-start(bf16[2,40,128]{2,1,0:T(8,128)(2,1)S(1)} %pad_maximum_fusion.pair_ref.refs_11_), channel_id=1, source_target_pairs={{0,4},{1,7},{2,6},{3,5},{4,0},{5,3},{6,2},{7,1},{8,12},{9,15},{10,... | collective-permute-start | bytes 61448 | tf_op jit(solution)/shard_map/ppermute | solution.py:451
  18.7 3.9 %collective-permute-start.4 = (bf16[2,40,128]{2,1,0:T(8,128)(2,1)S(1)}, bf16[2,40,128]{2,1,0:T(8,128)(2,1)S(1)}, u32[]{:S(2)}, u32[]{:S(2)}) collective-permute-start(bf16[2,40,128]{2,1,0:T(8,128)(2,1)S(1)} %pad_maximum_fusion.pair_ref.refs_11_), channel_id=1, source_target_pairs={{0,2},{1,3},{2,0},{3,1},{4,6},{5,7},{6,4},{7,5},{8,10},{9,11},{10,... | collective-permute-start | bytes 61448 | tf_op jit(solution)/shard_map/ppermute | solution.py:450
  21.0 1.6 %collective-permute-start.6 = (bf16[2,40,128]{2,1,0:T(8,128)(2,1)S(1)}, bf16[2,40,128]{2,1,0:T(8,128)(2,1)S(1)}, u32[]{:S(2)}, u32[]{:S(2)}) collective-permute-start(bf16[2,40,128]{2,1,0:T(8,128)(2,1)S(1)} %collective-permute-done.5.far_ref.refs_13_), channel_id=1, source_target_pairs={{0,1},{1,0},{2,3},{3,2},{4,5},{5,4},{6,7},{7,6},{8,9},{9,8},{10,11... | collective-permute-start | bytes 61448 | tf_op jit(solution)/shard_map/ppermute | solution.py:452
  23.5 4.7 %collective-permute-start.9 = (bf16[2,16,128]{2,1,0:T(8,128)(2,1)S(1)}, bf16[2,16,128]{2,1,0:T(8,128)(2,1)S(1)}, u32[]{:S(2)}, u32[]{:S(2)}) collective-permute-start(bf16[2,16,128]{2,1,0:T(8,128)(2,1)S(1)} %get-tuple-element.30.refs_0_), channel_id=1, source_target_pairs={{0,4},{1,7},{2,6},{3,5},{4,0},{5,3},{6,2},{7,1},{8,12},{9,15},{10,... | collective-permute-start | bytes 24584 | tf_op jit(solution)/shard_map/ppermute | solution.py:462
  25.6 3.8 %collective-permute-start.8 = (bf16[2,16,128]{2,1,0:T(8,128)(2,1)S(1)}, bf16[2,16,128]{2,1,0:T(8,128)(2,1)S(1)}, u32[]{:S(2)}, u32[]{:S(2)}) collective-permute-start(bf16[2,16,128]{2,1,0:T(8,128)(2,1)S(1)} %get-tuple-element.30.refs_0_), channel_id=1, source_target_pairs={{0,2},{1,3},{2,0},{3,1},{4,6},{5,7},{6,4},{7,5},{8,10},{9,11},{10,... | collective-permute-start | bytes 24584 | tf_op jit(solution)/shard_map/ppermute | solution.py:461
  28.2 1.2 %collective-permute-start.10 = (bf16[2,16,128]{2,1,0:T(8,128)(2,1)S(1)}, bf16[2,16,128]{2,1,0:T(8,128)(2,1)S(1)}, u32[]{:S(2)}, u32[]{:S(2)}) collective-permute-start(bf16[2,16,128]{2,1,0:T(8,128)(2,1)S(1)} %collective-permute-done.9.refs_2_.refs_8_), channel_id=1, source_target_pairs={{0,1},{1,0},{2,3},{3,2},{4,5},{5,4},{6,7},{7,6},{8,9},{9,8},{10,11... | collective-permute-start | bytes 24584 | tf_op jit(solution)/shard_map/ppermute | solution.py:495

commit v9 on v8

--- a/solution.py
+++ b/solution.py
@@ -399,7 +399,13 @@
         compiler_params=GRANT,
         name="sums",
     )(*(pltpu.with_memory_space_constraint(x, pltpu.HBM) for x in inputs))
-    parts_of_all = [msg] + others(msg, "det", n_det)
+    if n_det == 4:
+        parts_of_all = [msg]
+        for ks in ((1, 2), (2, 1), (3, 3)):
+            hops = [(d * n_tm + t, (d ^ ks[t % 2]) * n_tm + t) for d in range(n_det) for t in range(n_tm)]
+            parts_of_all.append(lax.ppermute(msg, ("det", "tm"), hops))
+    else:
+        parts_of_all = [msg] + others(msg, "det", n_det)
 
     rows = -(-filter_gain.shape[0] // LANES) * LANES
     inputs = (tile_ids, block_offsets, tile_owner, jnp.asarray(cosine_table(samples, rows)), pointing)

time: 30.4 us -> 30.4 us (level)
  no operation moved by 1% of the time
where the time goes in v9:
time: 30.4 us; the launch traced here: 30.2 us
  starting transfers between devices  12.9 us (42%)
  Pallas kernels  8.14 us (27%)
  waiting for transfers between devices  7.75 us (25%)
  between operations  0.71 us (2%)
  local copies, waits for them, and re-layouts  0.69 us (2%)
    ppermute x3, waiting for transfers between devices, shards(): parts_of_all.append(lax.ppermute(msg, ('det', 'tm'), hops))  4.22 us
    ppermute x3, starting transfers between devices, shards(): parts_of_all.append(lax.ppermute(msg, ('det', 'tm'), hops))  4.15 us
    ppermute x1, starting transfers between devices, shards(): far = lax.ppermute(pair, 'tm', fars)  2.65 us
    pallas_call x1, Pallas kernels, shards(): pl.pallas_call(functools.partial(prep_kernel, seg, kblk, digits), in_spec...  2.22 us
    ppermute x1, starting transfers between devices, shards(): far = lax.ppermute(send, 'tm', fars)  2.08 us
    pallas_call x1, Pallas kernels, shards(): pl.pallas_call(functools.partial(sums_kernel, modes), in_specs=[HB] * 4,...  1.99 us
    ppermute x1, starting transfers between devices, shards(): near = lax.ppermute(send, 'tm', nears)  1.83 us
    ppermute x1, starting transfers between devices, shards(): near = lax.ppermute(pair, 'tm', nears)  1.58 us
  transfers between devices with their start and end apart: 11, of which 6 were waited for; matrix products, arithmetic and copies ran while one was open for 0% of the time, Pallas kernels for 8%

profile of v9, /device:TPU:0, one launch (start us, length us, event | category | flops | bytes accessed | tf_op | source)
XLA Modules:
  0.0 30.2 jit_solution(4254531326901907376)
XLA Ops:
  0.6 0.7 %reshape.11.gain_ref = f32[1,257]{1,0:T(1,128)S(1)} reshape(f32[257]{0:T(512)} %param.18) | data formatting | bytes 2056 | tf_op jit(solution)/shard_map/reshape | solution.py:435
  1.3 2.0 %sums.1 = (bf16[72,512]{1,0:T(8,128)(2,1)S(1)}, f32[512,512]{1,0:T(8,128)S(1)}, bf16[512,512]{1,0:T(8,128)(2,1)S(1)}, f32[32,512]{1,0:T(8,128)S(1)}, f32[1,512]{1,0:T(1,128)S(1)}) custom-call(f32[512,512]{1,0:T(8,128)} %ts_hbm.1, s32[512,512]{1,0:T(8,128)} %flag_hbm.1, f32[32,512]{1,0:T(8,128)} %bitcast.2, f32[1,512]{1,0:T(1,128)} %bitcast.3), custom_call_target="tpu_custom_call" | custom-call | tf_op jit(solution)/shard_map/sums/pallas_call | solution.py:384
  3.3 2.2 %prep.1 = (bf16[1024,512]{1,0:T(8,128)(2,1)S(1)}, bf16[512,256]{1,0:T(8,128)(2,1)S(1)}, bf16[1024,512]{1,0:T(8,128)(2,1)S(1)}, bf16[512,128]{1,0:T(8,128)(2,1)S(1)}, bf16[24,128]{1,0:T(8,128)(2,1)S(1)}) custom-call(s32[4,4]{1,0:T(4,128)} %tids_hbm.1, s32[4,4]{1,0:T(4,128)} %offs_hbm.1, s32[32]{0:T(128)} %owner_hbm.1, f32[384,512]{1,0:T(8,128)} %constant.2.clone.cos_hbm, ...), custom_call_target="tpu_custom_call" | custom-call | flops 100000000 | bytes 3000000 | tf_op jit(solution)/shard_map/prep/pallas_call | solution.py:412
  5.5 0.6 %collective-permute-start.7 = (bf16[1024,512]{1,0:T(8,128)(2,1)S(1)}, bf16[1024,512]{1,0:T(8,128)(2,1)S(1)}, u32[]{:S(2)}, u32[]{:S(2)}) collective-permute-start(bf16[1024,512]{1,0:T(8,128)(2,1)S(1)} %get-tuple-element.26.pnt_ref), channel_id=1, source_target_pairs={{0,1},{1,0},{2,3},{3,2},{4,5},{5,4},{6,7},{7,6},{8,9},{9,8},{10,11... | collective-permute-start | bytes 3145736 | tf_op jit(solution)/shard_map/ppermute | solution.py:453
  6.1 3.5 %collective-permute-start.2 = (bf16[72,512]{1,0:T(8,128)(2,1)S(1)}, bf16[72,512]{1,0:T(8,128)(2,1)S(1)}, u32[]{:S(2)}, u32[]{:S(2)}) collective-permute-start(bf16[72,512]{1,0:T(8,128)(2,1)S(1)} %get-tuple-element.23.m0.refs_6_), channel_id=1, source_target_pairs={{0,24},{1,25},{2,26},{3,27},{4,28},{5,29},{6,30},{7,31},{8,16},{9,... | collective-permute-start | bytes 221192 | tf_op jit(solution)/shard_map/ppermute | solution.py:406
  9.6 0.5 %collective-permute-start.1 = (bf16[72,512]{1,0:T(8,128)(2,1)S(1)}, bf16[72,512]{1,0:T(8,128)(2,1)S(1)}, u32[]{:S(2)}, u32[]{:S(2)}) collective-permute-start(bf16[72,512]{1,0:T(8,128)(2,1)S(1)} %get-tuple-element.23.m0.refs_6_), channel_id=1, source_target_pairs={{0,16},{1,9},{2,18},{3,11},{4,20},{5,13},{6,22},{7,15},{8,24},{9,1... | collective-permute-start | bytes 221192 | tf_op jit(solution)/shard_map/ppermute | solution.py:406
  10.1 0.1 collective-permute-start
  10.2 2.4 %collective-permute-done.2.m3.refs_9_ = bf16[72,512]{1,0:T(8,128)(2,1)S(1)} collective-permute-done((bf16[72,512]{1,0:T(8,128)(2,1)S(1)}, bf16[72,512]{1,0:T(8,128)(2,1)S(1)}, u32[]{:S(2)}, u32[]{:S(2)}) %collective-permute-start.2) | collective-permute-done | bytes 73760 | tf_op jit(solution)/shard_map/ppermute | solution.py:406
  12.6 1.6 %collective-permute-done.1.m2.refs_8_ = bf16[72,512]{1,0:T(8,128)(2,1)S(1)} collective-permute-done((bf16[72,512]{1,0:T(8,128)(2,1)S(1)}, bf16[72,512]{1,0:T(8,128)(2,1)S(1)}, u32[]{:S(2)}, u32[]{:S(2)}) %collective-permute-start.1) | collective-permute-done | bytes 73760 | tf_op jit(solution)/shard_map/ppermute | solution.py:406
  14.2 0.3 collective-permute-done.m1.refs_7_
  14.5 0.4 %first.1 = (f32[8,512]{1,0:T(8,128)S(1)}, bf16[1,56,128]{2,1,0:T(8,128)(2,1)S(1)}) custom-call(bf16[72,512]{1,0:T(8,128)(2,1)S(1)} %get-tuple-element.23.m0.refs_6_, bf16[72,512]{1,0:T(8,128)(2,1)S(1)} %collective-permute-done.m1.refs_7_, bf16[72,512]{1,0:T(8,128)(2,1)S(1)} %collective-permute-done.1.m2.refs_8_, ...), custom_call_target="tpu_custom_call" | custom-call | tf_op jit(solution)/shard_map/first/pallas_call | solution.py:444
  14.9 0.0 collective-permute-start.3
  14.9 1.2 %collective-permute-done.3.mate_ref = bf16[1,56,128]{2,1,0:T(8,128)(2,1)S(1)} collective-permute-done((bf16[1,56,128]{2,1,0:T(8,128)(2,1)S(1)}, bf16[1,56,128]{2,1,0:T(8,128)(2,1)S(1)}, u32[]{:S(2)}, u32[]{:S(2)}) %collective-permute-start.3) | collective-permute-done | bytes 14368 | tf_op jit(solution)/shard_map/ppermute | solution.py:454
  16.1 2.7 %collective-permute-start.5 = (bf16[2,40,128]{2,1,0:T(8,128)(2,1)S(1)}, bf16[2,40,128]{2,1,0:T(8,128)(2,1)S(1)}, u32[]{:S(2)}, u32[]{:S(2)}) collective-permute-start(bf16[2,40,128]{2,1,0:T(8,128)(2,1)S(1)} %pad_maximum_fusion.pair_ref.refs_11_), channel_id=1, source_target_pairs={{0,4},{1,7},{2,6},{3,5},{4,0},{5,3},{6,2},{7,1},{8,12},{9,15},{10,... | collective-permute-start | bytes 61448 | tf_op jit(solution)/shard_map/ppermute | solution.py:457
  18.7 1.6 %collective-permute-start.4 = (bf16[2,40,128]{2,1,0:T(8,128)(2,1)S(1)}, bf16[2,40,128]{2,1,0:T(8,128)(2,1)S(1)}, u32[]{:S(2)}, u32[]{:S(2)}) collective-permute-start(bf16[2,40,128]{2,1,0:T(8,128)(2,1)S(1)} %pad_maximum_fusion.pair_ref.refs_11_), channel_id=1, source_target_pairs={{0,2},{1,3},{2,0},{3,1},{4,6},{5,7},{6,4},{7,5},{8,10},{9,11},{10,... | collective-permute-start | bytes 61448 | tf_op jit(solution)/shard_map/ppermute | solution.py:456
  20.3 0.7 %collective-permute-done.5.far_ref.refs_13_ = bf16[2,40,128]{2,1,0:T(8,128)(2,1)S(1)} collective-permute-done((bf16[2,40,128]{2,1,0:T(8,128)(2,1)S(1)}, bf16[2,40,128]{2,1,0:T(8,128)(2,1)S(1)}, u32[]{:S(2)}, u32[]{:S(2)}) %collective-permute-start.5) | collective-permute-done | bytes 20512 | tf_op jit(solution)/shard_map/ppermute | solution.py:457
  21.0 0.0 collective-permute-start.6
  21.0 1.6 %collective-permute-done.4.near_ref.refs_12_ = bf16[2,40,128]{2,1,0:T(8,128)(2,1)S(1)} collective-permute-done((bf16[2,40,128]{2,1,0:T(8,128)(2,1)S(1)}, bf16[2,40,128]{2,1,0:T(8,128)(2,1)S(1)}, u32[]{:S(2)}, u32[]{:S(2)}) %collective-permute-start.4) | collective-permute-done | bytes 20512 | tf_op jit(solution)/shard_map/ppermute | solution.py:456
  22.6 0.0 collective-permute-done.6.cross_ref.refs_14_
  22.6 0.0 collective-permute-done.7.mate_pnt_ref
  22.6 0.9 %second.1 = (f32[8,512]{1,0:T(8,128)S(1)}, bf16[2,16,128]{2,1,0:T(8,128)(2,1)S(1)}) custom-call(bf16[2,40,128]{2,1,0:T(8,128)(2,1)S(1)} %pad_maximum_fusion.pair_ref.refs_11_, bf16[2,40,128]{2,1,0:T(8,128)(2,1)S(1)} %collective-permute-done.4.near_ref.refs_12_, bf16[2,40,128]{2,1,0:T(8,128)(2,1)S(1)} %collective-permute-done.5.far_ref.refs_13_, ...), custom_call_target="tpu_custom_call" | custom-call | tf_op jit(solution)/shard_map/second/pallas_call | solution.py:459
  23.5 2.1 %collective-permute-start.9 = (bf16[2,16,128]{2,1,0:T(8,128)(2,1)S(1)}, bf16[2,16,128]{2,1,0:T(8,128)(2,1)S(1)}, u32[]{:S(2)}, u32[]{:S(2)}) collective-permute-start(bf16[2,16,128]{2,1,0:T(8,128)(2,1)S(1)} %get-tuple-element.30.refs_0_), channel_id=1, source_target_pairs={{0,4},{1,7},{2,6},{3,5},{4,0},{5,3},{6,2},{7,1},{8,12},{9,15},{10,... | collective-permute-start | bytes 24584 | tf_op jit(solution)/shard_map/ppermute | solution.py:468
  25.6 1.8 %collective-permute-start.8 = (bf16[2,16,128]{2,1,0:T(8,128)(2,1)S(1)}, bf16[2,16,128]{2,1,0:T(8,128)(2,1)S(1)}, u32[]{:S(2)}, u32[]{:S(2)}) collective-permute-start(bf16[2,16,128]{2,1,0:T(8,128)(2,1)S(1)} %get-tuple-element.30.refs_0_), channel_id=1, source_target_pairs={{0,2},{1,3},{2,0},{3,1},{4,6},{5,7},{6,4},{7,5},{8,10},{9,11},{10,... | collective-permute-start | bytes 24584 | tf_op jit(solution)/shard_map/ppermute | solution.py:467
  27.4 0.8 %early.1 = (bf16[384,512]{1,0:T(8,128)(2,1)S(1)}, bf16[128,512]{1,0:T(8,128)(2,1)S(1)}, f32[128,128]{1,0:T(8,128)S(1)}, f32[128,128]{1,0:T(8,128)S(1)}, bf16[1,128,128]{2,1,0:T(8,128)(2,1)S(1)}) custom-call(f32[512,512]{1,0:T(8,128)S(1)} %get-tuple-element.31.refs_0_, bf16[512,512]{1,0:T(8,128)(2,1)S(1)} %get-tuple-element.32.refs_1_, ...), custom_call_target="tpu_custom_call" | custom-call | flops 500000000 | bytes 2000000 | tf_op jit(solution)/shard_map/early/pallas_call | solution.py:483
  28.2 0.0 collective-permute-done.9.refs_2_.refs_8_
  28.2 0.1 collective-permute-start.10
  28.3 1.1 %late.1 = bf16[512,512]{1,0:T(8,128)(2,1)} custom-call(f32[512,512]{1,0:T(8,128)S(1)} %get-tuple-element.31.refs_0_, bf16[512,512]{1,0:T(8,128)(2,1)S(1)} %get-tuple-element.32.refs_1_, f32[1,512]{1,0:T(1,128)S(1)} %get-tuple-element.33.refs_2_, bf16[512,128]{1,0:T(8,128)(2,1)S(1)} %get-tuple-element.34.refs_3_, f32[8,512]{1,0:T(8,128)S(1)} %get-tuple-element.35.refs_4_, ...), custom_call_target="tpu_custom_call" | custom-call | flops 500000000 | bytes 2000000 | tf_op jit(solution)/shard_map/late/pallas_call | solution.py:503
  29.4 0.0 collective-permute-done.8.refs_1_
  29.4 0.0 collective-permute-done.10.refs_3_
  29.5 0.8 %tile.1 = f32[1,128,128]{2,1,0:T(8,128)} custom-call(bf16[2,16,128]{2,1,0:T(8,128)(2,1)S(1)} %get-tuple-element.30.refs_0_, bf16[2,16,128]{2,1,0:T(8,128)(2,1)S(1)} %collective-permute-done.8.refs_1_, bf16[2,16,128]{2,1,0:T(8,128)(2,1)S(1)} %collective-permute-done.9.refs_2_.refs_8_, bf16[2,16,128]{2,1,0:T(8,128)(2,1)S(1)} %collective-permute-done.10.refs_3_, ...), custom_call_target="tpu_custom_call" | custom-call | tf_op jit(solution)/shard_map/tile/pallas_call | solution.py:514
  (3 shorter events, 0.0 us)
Async XLA Ops:
  5.5 17.1 %collective-permute-start.7 = (bf16[1024,512]{1,0:T(8,128)(2,1)S(1)}, bf16[1024,512]{1,0:T(8,128)(2,1)S(1)}, u32[]{:S(2)}, u32[]{:S(2)}) collective-permute-start(bf16[1024,512]{1,0:T(8,128)(2,1)S(1)} %get-tuple-element.26.pnt_ref), channel_id=1, source_target_pairs={{0,1},{1,0},{2,3},{3,2},{4,5},{5,4},{6,7},{7,6},{8,9},{9,8},{10,11... | collective-permute-start | bytes 3145736 | tf_op jit(solution)/shard_map/ppermute | solution.py:453
  6.1 6.5 %collective-permute-start.2 = (bf16[72,512]{1,0:T(8,128)(2,1)S(1)}, bf16[72,512]{1,0:T(8,128)(2,1)S(1)}, u32[]{:S(2)}, u32[]{:S(2)}) collective-permute-start(bf16[72,512]{1,0:T(8,128)(2,1)S(1)} %get-tuple-element.23.m0.refs_6_), channel_id=1, source_target_pairs={{0,24},{1,25},{2,26},{3,27},{4,28},{5,29},{6,30},{7,31},{8,16},{9,... | collective-permute-start | bytes 221192 | tf_op jit(solution)/shard_map/ppermute | solution.py:406
  9.6 4.6 %collective-permute-start.1 = (bf16[72,512]{1,0:T(8,128)(2,1)S(1)}, bf16[72,512]{1,0:T(8,128)(2,1)S(1)}, u32[]{:S(2)}, u32[]{:S(2)}) collective-permute-start(bf16[72,512]{1,0:T(8,128)(2,1)S(1)} %get-tuple-element.23.m0.refs_6_), channel_id=1, source_target_pairs={{0,16},{1,9},{2,18},{3,11},{4,20},{5,13},{6,22},{7,15},{8,24},{9,1... | collective-permute-start | bytes 221192 | tf_op jit(solution)/shard_map/ppermute | solution.py:406
  10.1 4.4 %collective-permute-start = (bf16[72,512]{1,0:T(8,128)(2,1)S(1)}, bf16[72,512]{1,0:T(8,128)(2,1)S(1)}, u32[]{:S(2)}, u32[]{:S(2)}) collective-permute-start(bf16[72,512]{1,0:T(8,128)(2,1)S(1)} %get-tuple-element.23.m0.refs_6_), channel_id=1, source_target_pairs={{0,8},{1,17},{2,10},{3,19},{4,12},{5,21},{6,14},{7,23},{8,0},{9,25... | collective-permute-start | bytes 221192 | tf_op jit(solution)/shard_map/ppermute | solution.py:406
  14.9 1.2 %collective-permute-start.3 = (bf16[1,56,128]{2,1,0:T(8,128)(2,1)S(1)}, bf16[1,56,128]{2,1,0:T(8,128)(2,1)S(1)}, u32[]{:S(2)}, u32[]{:S(2)}) collective-permute-start(bf16[1,56,128]{2,1,0:T(8,128)(2,1)S(1)} %get-tuple-element.28), channel_id=1, source_target_pairs={{0,1},{1,0},{2,3},{3,2},{4,5},{5,4},{6,7},{7,6},{8,9},{9,8},{10,11... | collective-permute-start | bytes 43016 | tf_op jit(solution)/shard_map/ppermute | solution.py:454
  16.1 5.0 %collective-permute-start.5 = (bf16[2,40,128]{2,1,0:T(8,128)(2,1)S(1)}, bf16[2,40,128]{2,1,0:T(8,128)(2,1)S(1)}, u32[]{:S(2)}, u32[]{:S(2)}) collective-permute-start(bf16[2,40,128]{2,1,0:T(8,128)(2,1)S(1)} %pad_maximum_fusion.pair_ref.refs_11_), channel_id=1, source_target_pairs={{0,4},{1,7},{2,6},{3,5},{4,0},{5,3},{6,2},{7,1},{8,12},{9,15},{10,... | collective-permute-start | bytes 61448 | tf_op jit(solution)/shard_map/ppermute | solution.py:457
  18.7 3.9 %collective-permute-start.4 = (bf16[2,40,128]{2,1,0:T(8,128)(2,1)S(1)}, bf16[2,40,128]{2,1,0:T(8,128)(2,1)S(1)}, u32[]{:S(2)}, u32[]{:S(2)}) collective-permute-start(bf16[2,40,128]{2,1,0:T(8,128)(2,1)S(1)} %pad_maximum_fusion.pair_ref.refs_11_), channel_id=1, source_target_pairs={{0,2},{1,3},{2,0},{3,1},{4,6},{5,7},{6,4},{7,5},{8,10},{9,11},{10,... | collective-permute-start | bytes 61448 | tf_op jit(solution)/shard_map/ppermute | solution.py:456
  21.0 1.6 %collective-permute-start.6 = (bf16[2,40,128]{2,1,0:T(8,128)(2,1)S(1)}, bf16[2,40,128]{2,1,0:T(8,128)(2,1)S(1)}, u32[]{:S(2)}, u32[]{:S(2)}) collective-permute-start(bf16[2,40,128]{2,1,0:T(8,128)(2,1)S(1)} %collective-permute-done.5.far_ref.refs_13_), channel_id=1, source_target_pairs={{0,1},{1,0},{2,3},{3,2},{4,5},{5,4},{6,7},{7,6},{8,9},{9,8},{10,11... | collective-permute-start | bytes 61448 | tf_op jit(solution)/shard_map/ppermute | solution.py:458
  23.5 4.7 %collective-permute-start.9 = (bf16[2,16,128]{2,1,0:T(8,128)(2,1)S(1)}, bf16[2,16,128]{2,1,0:T(8,128)(2,1)S(1)}, u32[]{:S(2)}, u32[]{:S(2)}) collective-permute-start(bf16[2,16,128]{2,1,0:T(8,128)(2,1)S(1)} %get-tuple-element.30.refs_0_), channel_id=1, source_target_pairs={{0,4},{1,7},{2,6},{3,5},{4,0},{5,3},{6,2},{7,1},{8,12},{9,15},{10,... | collective-permute-start | bytes 24584 | tf_op jit(solution)/shard_map/ppermute | solution.py:468
  25.6 3.8 %collective-permute-start.8 = (bf16[2,16,128]{2,1,0:T(8,128)(2,1)S(1)}, bf16[2,16,128]{2,1,0:T(8,128)(2,1)S(1)}, u32[]{:S(2)}, u32[]{:S(2)}) collective-permute-start(bf16[2,16,128]{2,1,0:T(8,128)(2,1)S(1)} %get-tuple-element.30.refs_0_), channel_id=1, source_target_pairs={{0,2},{1,3},{2,0},{3,1},{4,6},{5,7},{6,4},{7,5},{8,10},{9,11},{10,... | collective-permute-start | bytes 24584 | tf_op jit(solution)/shard_map/ppermute | solution.py:467
  28.2 1.2 %collective-permute-start.10 = (bf16[2,16,128]{2,1,0:T(8,128)(2,1)S(1)}, bf16[2,16,128]{2,1,0:T(8,128)(2,1)S(1)}, u32[]{:S(2)}, u32[]{:S(2)}) collective-permute-start(bf16[2,16,128]{2,1,0:T(8,128)(2,1)S(1)} %collective-permute-done.9.refs_2_.refs_8_), channel_id=1, source_target_pairs={{0,1},{1,0},{2,3},{3,2},{4,5},{5,4},{6,7},{7,6},{8,9},{9,8},{10,11... | collective-permute-start | bytes 24584 | tf_op jit(solution)/shard_map/ppermute | solution.py:501
